TPU v7x, 32 devices: a whole 2x2x4 slice. The times are simulated.
32 devices in a mesh: resp: 2 (over y), item: 16 (over z, x, core).
Axes of the slice: x: 2, y: 2, z: 4, core: 2. Of those that a mesh axis runs over, the one named last changes fastest.
Arguments:
- coupling: bfloat16 [2, 4096, 2048], P('resp', 'item'), may hold values from -6 to 6
- noise: bfloat16 [2, 4096, 2048], P('resp', 'item'), may hold values from -6 to 6
- bias: float32 [16, 256], P('item', 'resp'), may hold values from -4 to 4
- responses: int32 [1024, 4096], P(None, 'item'), may hold values 0 or 1
- indices: int32 [512], replicated, may hold values from 0 to 1023
Outputs:
- new_coupling: bfloat16 [2, 4096, 2048], P('resp', 'item')
All inputs are finite; a program needn't handle non-finite values. No bound on the sum of `responses` on one device may be relied on, other than what follows from the above.
Results may differ from a plain program's by a relative error of at most 0.0035.
Values may be sent and summed in bfloat16 or wider, within the bound.
No kernel may reach another device: no remote copies, remote signals or barrier semaphores. Data moves between devices by JAX's collectives and lax.ppermute only.
A program may use at most 64 MiB of HBM per device.

v0:
```python
import math

import jax
import jax.numpy as jnp
from jax import lax
from jax.sharding import PartitionSpec as P

DRIFT = 0.01
DATA_RATIO = 900.0
NOISE_SCALE = math.sqrt(0.02)


def shards(coupling, noise, bias, responses, indices):
    couple = coupling[0]
    item_dev = couple.shape[0]
    n_resp = lax.axis_size("resp")
    n_item = lax.axis_size("item")
    sub_len = item_dev // n_resp
    inv_root = 1.0 / math.sqrt(item_dev * n_item)
    resp_idx = lax.axis_index("resp")
    item_idx = lax.axis_index("item")
    chosen = jnp.take(responses, indices, axis=0)
    spin_vals = (2 * chosen - 1).astype(jnp.bfloat16)
    summed = lax.psum_scatter(
        lax.dot_general(
            couple, spin_vals, (((0,), (1,)), ((), ())), preferred_element_type=jnp.float32
        ),
        "item",
        scatter_dimension=0,
        tiled=True,
    )
    own_start = resp_idx * sub_len
    diag_block = lax.dynamic_slice(couple, (own_start, item_idx * sub_len), (sub_len, sub_len))
    self_weight = jnp.diagonal(diag_block).astype(jnp.float32)
    spin_slice = lax.dynamic_slice_in_dim(spin_vals, own_start, sub_len, 1).T
    own_spin = spin_slice.astype(jnp.float32)
    own_answer = lax.dynamic_slice_in_dim(chosen, own_start, sub_len, 1).astype(jnp.float32).T
    fields = (summed - self_weight[:, None] * own_spin) * inv_root + bias[0][:, None]
    residual = (own_answer - jax.nn.sigmoid(fields)).astype(jnp.bfloat16)
    gathered = lax.all_gather(residual, "item", axis=0, tiled=True)
    tiles = jnp.einsum(
        "brt,kub->rktu",
        spin_vals.reshape(-1, n_resp, sub_len),
        gathered.reshape(n_item, sub_len, -1),
        preferred_element_type=jnp.float32,
    )
    flat_tiles = tiles.reshape(n_resp, n_item, sub_len * sub_len)
    moved = lax.all_to_all(
        lax.all_to_all(flat_tiles, "resp", split_axis=0, concat_axis=0, tiled=True),
        "item",
        split_axis=1,
        concat_axis=1,
        tiled=True,
    )
    own_part = tiles.transpose(0, 2, 1, 3).reshape(item_dev, n_item * sub_len)
    mirror = (
        moved.reshape(n_resp, n_item, sub_len, sub_len)
        .transpose(0, 3, 1, 2)
        .reshape(item_dev, n_item * sub_len)
    )
    row_ids = lax.broadcasted_iota(jnp.int32, (item_dev, n_item * sub_len), 0)
    col_ids = lax.broadcasted_iota(jnp.int32, (item_dev, n_item * sub_len), 1)
    on_diag = (
        (col_ids == item_idx * sub_len + row_ids - own_start)
        & (row_ids >= own_start)
        & (row_ids < own_start + sub_len)
    )
    gradient = jnp.where(on_diag, jnp.float32(0.0), own_part + mirror) * inv_root
    current = couple.astype(jnp.float32)
    updated = (
        current
        + DRIFT * (DATA_RATIO * gradient - current)
        + NOISE_SCALE * noise[0].astype(jnp.float32)
    )
    return updated.astype(jnp.bfloat16)[None]


def solution(mesh):
    return jax.shard_map(
        shards,
        mesh=mesh,
        in_specs=(
            P("resp", "item", None),
            P("resp", "item", None),
            P("item", "resp"),
            P(None, "item"),
            P(),
        ),
        out_specs=P("resp", "item", None),
        check_vma=False,
    )
```

profile of v0, /device:TPU:11, one launch (start us, length us, event | category | flops | bytes accessed | tf_op | source)
XLA Modules:
  0.0 247.9 jit_solution(4028890291314251297)
XLA Ops:
  6.5 0.0 copy-start
  6.5 0.0 reduce-scatter.2.cloned.1.call-start
  6.5 0.8 compare_select_fusion
  7.3 0.7 compare_and_fusion
  8.0 0.0 copy-done
  8.0 0.0 copy-start.1
  8.0 1.6 gather_fusion
  9.6 0.9 add_convert_fusion
  10.6 0.0 copy-done.1
  10.6 2.7 %convolution_bitcast_fusion = f32[2048,512]{0,1:T(8,128)} fusion(bf16[512,256]{1,0:T(8,128)(2,1)S(1)} %get-tuple-element.5, bf16[1,256,2048]{2,1,0:T(8,128)(2,1)S(1)} %copy-done.1), kind=kOutput, calls=%fused_computation.2 | convolution fusion | flops 536870912 | bytes 5505024 | tf_op jit(solution)/shard_map/dot_general | solution.py:25
  13.2 0.0 copy-start.2
  13.2 0.0 copy-start.3
  13.2 0.0 reduce-scatter.2.cloned.1.call-update
  13.3 0.0 all-gather.2.cloned.1.call-start
  13.4 1.5 gather_fusion.1
  14.9 69.9 %reduce-scatter.2.cloned.1.call-done = f32[128,512]{0,1:T(8,128)} async-done(((f32[2048,512]{0,1:T(8,128)}), f32[128,512]{0,1:T(8,128)}) %reduce-scatter.2.cloned.1.call-update) | async-done | bytes 262160 | tf_op jit(solution)/shard_map/reduce_scatter | solution.py:24
  84.7 0.0 copy-done.2
  84.8 0.0 copy-done.3
  84.8 1.7 fusion.15
  86.5 0.0 all-gather.2.cloned.1.call-update
  86.5 43.1 %all-gather.2.cloned.1.call-done = bf16[2048,512]{0,1:T(8,128)(2,1)} async-done(((bf16[128,512]{0,1:T(8,128)(2,1)}), bf16[2048,512]{0,1:T(8,128)(2,1)}) %all-gather.2.cloned.1.call-update) | async-done | bytes 2097168 | tf_op jit(solution)/shard_map/all_gather | solution.py:40
  129.6 3.9 %copy.19 = bf16[2048,512]{1,0:T(8,128)(2,1)} copy(bf16[2048,512]{0,1:T(8,128)(2,1)} %all-gather.2.cloned.1.call-done) | data formatting | bytes 4194304 | tf_op jit(solution)/shard_map/reshape | solution.py:44
  133.5 2.3 fusion.6
  135.8 1.8 copy.15
  137.7 2.7 %reshape.138 = f32[2,16,16384]{2,1,0:T(8,128)} reshape(f32[2,16,128,128]{3,2,1,0:T(8,128)} %copy.15) | data formatting | bytes 4194304 | tf_op jit(solution)/shard_map/reshape | solution.py:47
  140.4 28.5 %all_to_all.10 = f32[2,16,16384]{2,1,0:T(8,128)S(1)} all-to-all(f32[2,16,16384]{2,1,0:T(8,128)} %reshape.138), channel_id=1, replica_groups=mesh['resp'=2,'item'=16] {'resp'}, dimensions={0} | all-to-all | bytes 4194304 | tf_op jit(solution)/shard_map/all_to_all | solution.py:49
  168.9 2.9 %copy.16 = f32[2,16,16384]{2,0,1:T(2,128)} copy(f32[2,16,16384]{2,1,0:T(8,128)S(1)} %all_to_all.10) | data formatting | bytes 4194304 | tf_op jit(solution)/shard_map/all_to_all | solution.py:49
  171.8 5.8 %all-to-all-start.1 = ((f32[2,16,16384]{2,0,1:T(2,128)}), f32[2,16,16384]{2,0,1:T(2,128)}, u32[]{:S(2)}, u32[]{:S(2)}) async-start(f32[2,16,16384]{2,0,1:T(2,128)} %copy.16), calls=%async_computation.2 | async-start | bytes 4194304 | tf_op jit(solution)/shard_map/all_to_all | solution.py:48
  177.7 47.5 %all-to-all-done.1 = f32[2,16,16384]{2,0,1:T(2,128)} async-done(((f32[2,16,16384]{2,0,1:T(2,128)}), f32[2,16,16384]{2,0,1:T(2,128)}, u32[]{:S(2)}, u32[]{:S(2)}) %all-to-all-start.1) | async-done | bytes 2097184 | tf_op jit(solution)/shard_map/all_to_all | solution.py:48
  225.2 4.0 %reshape.139 = f32[2,16,128,128]{3,2,0,1:T(8,128)} reshape(f32[2,16,16384]{2,0,1:T(2,128)} %all-to-all-done.1) | data formatting | bytes 4194304 | tf_op jit(solution)/shard_map/reshape | solution.py:57
  229.2 3.2 %bitcast_add_fusion = f32[2,128,16,128]{1,3,0,2:T(8,128)} fusion(f32[2,16,128,128]{3,2,0,1:T(8,128)} %reshape.139, f32[16,128,2,128]{3,1,2,0:T(8,128)S(1)} %fusion.6), kind=kLoop, calls=%fused_computation.8 | loop fusion | flops 524288 | bytes 6291456 | tf_op jit(solution)/shard_map/add | solution.py:68
  232.4 3.1 %copy.17 = f32[2,128,16,128]{3,2,1,0:T(8,128)} copy(f32[2,128,16,128]{1,3,0,2:T(8,128)} %bitcast_add_fusion) | data formatting | bytes 4194304 | tf_op jit(solution)/shard_map/add | solution.py:68
  235.5 1.7 add.87
  237.2 3.9 %fusion.2 = bf16[1,256,2048]{2,1,0:T(8,128)(2,1)} fusion(bf16[1,256,2048]{2,1,0:T(8,128)(2,1)} %param.5, bf16[1,256,2048]{2,1,0:T(8,128)(2,1)} %param.6, f32[1,256,2048]{2,1,0:T(8,128)S(1)} %add.87, s32[256]{0:T(256)S(1)} %add_subtract_fusion, pred[256]{0:T(512)(128)(4,1)S(1)} %get-tuple-element.7, pred[256]{0:T(512)(128)(4,1)S(1)} %get-tuple-element.8), kind=kLoop, calls=%fused_computation.7 | loop fusion | flops 6815744 | bytes 5244416 | tf_op jit(solution)/shard_map/convert_element_type | solution.py:75
  (6 shorter events, 0.1 us)
Async XLA Ops:
  6.5 1.5 copy-start
  6.5 78.2 %reduce-scatter.2.cloned.1.call-start = ((), (), s32[]{:S(2)}) async-start(), calls=%async_computation.3 | async-start | bytes 4456448 | tf_op jit(solution)/shard_map/reduce_scatter | solution.py:24
  8.0 2.5 %copy-start.1 = (bf16[1,256,2048]{2,1,0:T(8,128)(2,1)S(1)}, bf16[1,256,2048]{2,1,0:T(8,128)(2,1)}, u32[]{:S(2)}) copy-start(bf16[1,256,2048]{2,1,0:T(8,128)(2,1)} %param.5) | copy-start | bytes 3145732
  13.2 71.5 %copy-start.2 = (s32[512,256]{1,0:T(8,128)S(1)}, s32[512,256]{1,0:T(8,128)}, u32[]{:S(2)}) copy-start(s32[512,256]{1,0:T(8,128)} %get-tuple-element.6) | copy-start | bytes 1572868
  13.2 71.5 %copy-start.3 = (f32[1,128]{1,0:T(1,128)S(1)}, f32[1,128]{1,0:T(1,128)}, u32[]{:S(2)}) copy-start(f32[1,128]{1,0:T(1,128)} %param.7) | copy-start | bytes 1540
  13.3 116.3 %all-gather.2.cloned.1.call-start = ((), (), s32[]{:S(2)}) async-start(), calls=%async_computation.4 | async-start | bytes 2228224 | tf_op jit(solution)/shard_map/all_gather | solution.py:40
  171.8 53.4 %all-to-all-start.1 = ((f32[2,16,16384]{2,0,1:T(2,128)}), f32[2,16,16384]{2,0,1:T(2,128)}, u32[]{:S(2)}, u32[]{:S(2)}) async-start(f32[2,16,16384]{2,0,1:T(2,128)} %copy.16), calls=%async_computation.2 | async-start | bytes 4194304 | tf_op jit(solution)/shard_map/all_to_all | solution.py:48
Sparse Core Ops, SparseCore 0:
  13.4 71.3 reduce-scatter.1
  87.1 42.4 all-gather.1
where the time goes:
time: 248 us
  waiting for transfers between devices  161 us (65%)
  blocking collectives  28.5 us (11%)
  local copies, waits for them, and re-layouts  23.4 us (9%)
  between operations  13.5 us (5%)
  other arithmetic  11.2 us (5%)
  starting transfers between devices  5.89 us (2%)
  matrix products  4.96 us (2%)
    reduce_scatter x1, waiting for transfers between devices, shards(): lax.psum_scatter(lax.dot_general(couple, spin_vals, (((0,), (1,)), ((), (...  69.9 us
    all_to_all x1, waiting for transfers between devices, shards(): lax.all_to_all(lax.all_to_all(flat_tiles, 'resp', split_axis=0, concat_ax...  47.5 us
    all_gather x1, waiting for transfers between devices, shards(): gathered = lax.all_gather(residual, 'item', axis=0, tiled=True)  43.1 us
    all_to_all x1, blocking collectives, shards(): lax.all_to_all(flat_tiles, 'resp', split_axis=0, concat_axis=0, tiled=True)  28.5 us
    all_to_all x1, starting transfers between devices, shards(): lax.all_to_all(lax.all_to_all(flat_tiles, 'resp', split_axis=0, concat_ax...  5.85 us
  transfers between devices with their start and end apart: 3, of which 3 were waited for; matrix products, arithmetic and copies ran while one was open for 1% of the time, Pallas kernels for 0%

commit v1 on v0

v1 whole, which is shorter than its diff:
```python
import functools
import math

import jax
import jax.numpy as jnp
from jax import lax
from jax.experimental import pallas as pl
from jax.experimental.pallas import tpu as pltpu
from jax.sharding import PartitionSpec as P

DRIFT = 0.01
DATA_RATIO = 900.0
NOISE_SCALE = math.sqrt(0.02)
NT = (((1,), (1,)), ((), ()))
TN = (((0,), (0,)), ((), ()))


def spins_kernel(index_ref, responses_ref, spins_ref):
    pool = responses_ref.shape[0]
    batch = index_ref.shape[1]
    row_ids = lax.broadcasted_iota(jnp.int32, (pool, batch), 0)
    picks = jnp.where(row_ids == index_ref[...], 1.0, 0.0).astype(jnp.bfloat16)
    pool_spins = (2 * responses_ref[...] - 1).astype(jnp.float32).astype(jnp.bfloat16)
    spins_ref[...] = lax.dot_general(
        pool_spins, picks, TN, preferred_element_type=jnp.float32
    ).astype(jnp.bfloat16)


def gather_spins(responses, indices):
    return pl.pallas_call(
        spins_kernel,
        out_shape=jax.ShapeDtypeStruct((responses.shape[1], indices.shape[0]), jnp.bfloat16),
        name="gather_spins",
    )(indices[None], responses)


def update_kernel(
    inv_root, place_ref, spin_ref, res_ref, all_res_ref, all_spin_ref, couple_ref, noise_ref, out_ref
):
    grad = lax.dot_general(
        spin_ref[...], all_res_ref[...], NT, preferred_element_type=jnp.float32
    ) + lax.dot_general(res_ref[...], all_spin_ref[...], NT, preferred_element_type=jnp.float32)
    rows, cols = grad.shape
    row_ids = lax.broadcasted_iota(jnp.int32, (rows, cols), 0)
    col_ids = lax.broadcasted_iota(jnp.int32, (rows, cols), 1) + pl.program_id(0) * cols
    own_start, sub_len, first_col = place_ref[0], place_ref[1], place_ref[2]
    on_diag = (
        (col_ids - first_col == row_ids - own_start)
        & (row_ids >= own_start)
        & (row_ids < own_start + sub_len)
    )
    grad = jnp.where(on_diag, 0.0, grad) * inv_root
    current = couple_ref[...].astype(jnp.float32)
    out_ref[...] = (
        current
        + DRIFT * (DATA_RATIO * grad - current)
        + NOISE_SCALE * noise_ref[...].astype(jnp.float32)
    ).astype(jnp.bfloat16)


def update(place, spins, res, all_res, all_spin, couple, noise, inv_root):
    rows, width = couple.shape
    batch = spins.shape[1]
    block = min(512, width)
    fixed = lambda shape: pl.BlockSpec(shape, lambda j: (0, 0))
    return pl.pallas_call(
        functools.partial(update_kernel, inv_root),
        grid=(width // block,),
        in_specs=[
            pl.BlockSpec(memory_space=pltpu.SMEM),
            fixed((rows, batch)),
            fixed((rows, batch)),
            pl.BlockSpec((block, batch), lambda j: (j, 0)),
            pl.BlockSpec((block, batch), lambda j: (j, 0)),
            pl.BlockSpec((rows, block), lambda j: (0, j)),
            pl.BlockSpec((rows, block), lambda j: (0, j)),
        ],
        out_specs=pl.BlockSpec((rows, block), lambda j: (0, j)),
        out_shape=jax.ShapeDtypeStruct((rows, width), jnp.bfloat16),
        name="update",
    )(place, spins, res, all_res, all_spin, couple, noise)


def shards(coupling, noise, bias, responses, indices):
    couple = coupling[0]
    item_dev = couple.shape[0]
    batch = indices.shape[0]
    n_resp = lax.axis_size("resp")
    n_item = lax.axis_size("item")
    sub_len = item_dev // n_resp
    n_far = n_item // 4
    inv_root = 1.0 / math.sqrt(item_dev * n_item)
    resp_idx = lax.axis_index("resp")
    item_idx = lax.axis_index("item")
    far_idx, near_idx, core_idx = item_idx // 4, item_idx // 2 % 2, item_idx % 2
    own_start = resp_idx * sub_len
    swap_core = [(i, i ^ 1) for i in range(n_item)]
    swap_near = [(i, i ^ 2) for i in range(n_item)]

    def half(blocks, axis, index):
        return lax.dynamic_index_in_dim(blocks, index, axis, keepdims=False)

    by_core = couple.reshape(item_dev, 2 * n_far, 2, sub_len)
    kept = half(by_core, 2, core_idx).reshape(item_dev, -1)
    given = half(by_core, 2, 1 - core_idx).reshape(item_dev, -1)
    got = lax.ppermute(given, "item", swap_core)

    spins = gather_spins(responses, indices)
    peer_spins = lax.ppermute(spins, "item", swap_core)
    own_spins = lax.dynamic_slice_in_dim(spins, own_start, sub_len, 0)
    all_spins = lax.all_gather(own_spins, "item", axis=0, tiled=True)

    partial = lax.dot_general(
        kept, spins, TN, preferred_element_type=jnp.float32
    ) + lax.dot_general(got, peer_spins, TN, preferred_element_type=jnp.float32)

    by_near = partial.reshape(n_far, 2, sub_len, batch)
    sent = half(by_near, 1, 1 - near_idx).astype(jnp.bfloat16)
    held = half(by_near, 1, near_idx) + lax.ppermute(sent, "item", swap_near).astype(jnp.float32)
    total = half(held, 0, far_idx)
    for step in range(1, n_far):
        ring = [(i, (i + 4 * step) % n_item) for i in range(n_item)]
        piece = half(held, 0, (far_idx + step) % n_far).astype(jnp.bfloat16)
        total = total + lax.ppermute(piece, "item", ring).astype(jnp.float32)

    diag_block = lax.dynamic_slice(couple, (own_start, item_idx * sub_len), (sub_len, sub_len))
    row_ids = lax.broadcasted_iota(jnp.int32, (sub_len, sub_len), 0)
    col_ids = lax.broadcasted_iota(jnp.int32, (sub_len, sub_len), 1)
    self_weight = jnp.sum(
        jnp.where(row_ids == col_ids, diag_block.astype(jnp.float32), 0.0), axis=1, keepdims=True
    )
    own_spin = own_spins.astype(jnp.float32)
    fields = (total - self_weight * own_spin) * inv_root + bias[0][:, None]
    residual = (0.5 * (own_spin + 1.0) - jax.nn.sigmoid(fields)).astype(jnp.bfloat16)

    all_res = lax.all_gather(residual, "item", axis=0, tiled=True)
    row_res = lax.dynamic_update_slice_in_dim(
        jnp.zeros((item_dev, batch), jnp.bfloat16), residual, own_start, 0
    )
    for step in range(1, n_resp):
        ring = [(i, (i + step) % n_resp) for i in range(n_resp)]
        came = lax.ppermute(residual, "resp", ring)
        source = (resp_idx - step) % n_resp
        row_res = lax.dynamic_update_slice_in_dim(row_res, came, source * sub_len, 0)

    place = jnp.stack([own_start, jnp.int32(sub_len), item_idx * sub_len]).astype(jnp.int32)
    return update(place, spins, row_res, all_res, all_spins, couple, noise[0], inv_root)[None]


def solution(mesh):
    return jax.shard_map(
        shards,
        mesh=mesh,
        in_specs=(
            P("resp", "item", None),
            P("resp", "item", None),
            P("item", "resp"),
            P(None, "item"),
            P(),
        ),
        out_specs=P("resp", "item", None),
        check_vma=False,
    )
```

time: 248 us -> 143 us (0.58)
  the two profiles are of different devices: /device:TPU:11 before, /device:TPU:0 now
where the time goes in v1:
time: 143 us; the launch traced here: 142 us
  waiting for transfers between devices  104 us (73%)
  between operations  13.5 us (9%)
  starting transfers between devices  9.83 us (7%)
  Pallas kernels  8.45 us (6%)
  other arithmetic  3.58 us (3%)
  matrix products  1.81 us (1%)
  local copies, waits for them, and re-layouts  1.75 us (1%)
    all_gather x1, waiting for transfers between devices, shards(): all_res = lax.all_gather(residual, 'item', axis=0, tiled=True)  42.4 us
    all_gather x1, waiting for transfers between devices, shards(): all_spins = lax.all_gather(own_spins, 'item', axis=0, tiled=True)  34.5 us
    ppermute x1, waiting for transfers between devices, shards(): lax.ppermute(sent, 'item', swap_near).astype(jnp.float32)  12.5 us
    ppermute x3, waiting for transfers between devices, shards(): total = total + lax.ppermute(piece, 'item', ring).astype(jnp.float32)  9.75 us
    pallas_call x1, Pallas kernels, update(): pl.pallas_call(functools.partial(update_kernel, inv_root), grid=(width //...  5.95 us
    ppermute x3, starting transfers between devices, shards(): total = total + lax.ppermute(piece, 'item', ring).astype(jnp.float32)  4.91 us
    ppermute x1, waiting for transfers between devices, shards(): came = lax.ppermute(residual, 'resp', ring)  3.29 us
  transfers between devices with their start and end apart: 9, of which 8 were waited for; matrix products, arithmetic and copies ran while one was open for 2% of the time, Pallas kernels for 2%

profile of v1, /device:TPU:0, one launch (start us, length us, event | category | flops | bytes accessed | tf_op | source)
XLA Modules:
  0.0 142.5 jit_solution(8598207151115612515)
XLA Ops:
  6.5 0.0 all-gather.5.cloned.1.call-start
  6.5 1.5 %copy.7 = bf16[1,256,2048]{1,2,0:T(8,128)(2,1)S(1)} copy(bf16[1,256,2048]{2,1,0:T(8,128)(2,1)} %param.5) | data formatting | bytes 2097152 | tf_op args[0]
  8.0 0.1 constant_dynamic-slice_fusion
  8.1 0.5 collective-permute-start
  8.7 2.5 %gather_spins.1.spin_ref = bf16[256,512]{1,0:T(8,128)(2,1)} custom-call(s32[1,512]{1,0:T(1,128)} %bitcast.48, s32[1024,256]{1,0:T(8,128)} %responses_ref.1), custom_call_target="tpu_custom_call" | custom-call | tf_op jit(solution)/shard_map/gather_spins/pallas_call | solution.py:30
  11.2 0.1 collective-permute-start.1
  11.2 1.4 fusion.18
  12.6 0.3 collective-permute-done.1
  12.9 0.0 collective-permute-done
  12.9 0.4 convolution_add_fusion
  13.3 0.1 fusion
  13.4 0.0 copy-start
  13.4 0.0 copy-start.2
  13.4 2.7 %collective-permute-start.2 = (bf16[4,128,512]{2,1,0:T(8,128)(2,1)S(1)}, bf16[4,128,512]{2,1,0:T(8,128)(2,1)}, u32[]{:S(2)}, u32[]{:S(2)}) collective-permute-start(bf16[4,128,512]{2,1,0:T(8,128)(2,1)S(1)} %fusion), channel_id=1, source_target_pairs={{0,2},{1,3},{2,0},{3,1},{4,6},{5,7},{6,4},{7,5},{8,10},{9,11},{10,... | collective-permute-start | bytes 1572872 | tf_op jit(solution)/shard_map/ppermute | solution.py:119
  16.2 12.5 %collective-permute-done.2 = bf16[4,128,512]{2,1,0:T(8,128)(2,1)} collective-permute-done((bf16[4,128,512]{2,1,0:T(8,128)(2,1)S(1)}, bf16[4,128,512]{2,1,0:T(8,128)(2,1)}, u32[]{:S(2)}, u32[]{:S(2)}) %collective-permute-start.2) | collective-permute-done | bytes 524320 | tf_op jit(solution)/shard_map/ppermute | solution.py:119
  28.7 1.2 bitcast_add_fusion
  29.9 0.1 fusion.13
  30.0 1.9 %collective-permute-start.3 = (bf16[128,512]{1,0:T(8,128)(2,1)S(1)}, bf16[128,512]{1,0:T(8,128)(2,1)S(1)}, u32[]{:S(2)}, u32[]{:S(2)}) collective-permute-start(bf16[128,512]{1,0:T(8,128)(2,1)S(1)} %get-tuple-element.8), channel_id=1, source_target_pairs={{0,4},{1,5},{2,6},{3,7},{4,8},{5,9},{6,10},{7,11},{8,12},{9,13},{1... | collective-permute-start | bytes 393224 | tf_op jit(solution)/shard_map/ppermute | solution.py:124
  31.9 2.1 %collective-permute-start.5 = (bf16[128,512]{1,0:T(8,128)(2,1)S(1)}, bf16[128,512]{1,0:T(8,128)(2,1)S(1)}, u32[]{:S(2)}, u32[]{:S(2)}) collective-permute-start(bf16[128,512]{1,0:T(8,128)(2,1)S(1)} %get-tuple-element.9), channel_id=1, source_target_pairs={{0,12},{1,13},{2,14},{3,15},{4,0},{5,1},{6,2},{7,3},{8,4},{9,5},{1... | collective-permute-start | bytes 393224 | tf_op jit(solution)/shard_map/ppermute | solution.py:124
  34.0 1.0 collective-permute-start.4
  34.9 0.9 fusion.16
  35.8 2.5 %collective-permute-done.3 = bf16[128,512]{1,0:T(8,128)(2,1)S(1)} collective-permute-done((bf16[128,512]{1,0:T(8,128)(2,1)S(1)}, bf16[128,512]{1,0:T(8,128)(2,1)S(1)}, u32[]{:S(2)}, u32[]{:S(2)}) %collective-permute-start.3) | collective-permute-done | bytes 131104 | tf_op jit(solution)/shard_map/ppermute | solution.py:124
  38.3 1.1 collective-permute-done.5
  39.3 6.2 %collective-permute-done.4 = bf16[128,512]{1,0:T(8,128)(2,1)S(1)} collective-permute-done((bf16[128,512]{1,0:T(8,128)(2,1)S(1)}, bf16[128,512]{1,0:T(8,128)(2,1)S(1)}, u32[]{:S(2)}, u32[]{:S(2)}) %collective-permute-start.4) | collective-permute-done | bytes 131104 | tf_op jit(solution)/shard_map/ppermute | solution.py:124
  45.5 0.0 copy-done
  45.6 0.0 copy-done.2
  45.6 0.9 constant_dynamic-update-slice_fusion.1
  46.4 0.0 all-gather.5.cloned.1.call-update
  46.4 0.0 all-gather.3.cloned.1.call-start
  46.5 0.7 all-gather.3.cloned.1.call-update
  47.2 1.6 %collective-permute-start.6 = (bf16[128,512]{1,0:T(8,128)(2,1)}, bf16[128,512]{1,0:T(8,128)(2,1)S(1)}, u32[]{:S(2)}, u32[]{:S(2)}) collective-permute-start(bf16[128,512]{1,0:T(8,128)(2,1)} %get-tuple-element.6), channel_id=1, source_target_pairs={{0,16},{16,0},{1,17},{17,1},{2,18},{18,2},{3,19},{19,3},{4,20},{20... | collective-permute-start | bytes 393224 | tf_op jit(solution)/shard_map/ppermute | solution.py:142
  48.8 0.7 pad_add_fusion.place_ref
  49.4 3.3 %collective-permute-done.6 = bf16[128,512]{1,0:T(8,128)(2,1)S(1)} collective-permute-done((bf16[128,512]{1,0:T(8,128)(2,1)}, bf16[128,512]{1,0:T(8,128)(2,1)S(1)}, u32[]{:S(2)}, u32[]{:S(2)}) %collective-permute-start.6) | collective-permute-done | bytes 131104 | tf_op jit(solution)/shard_map/ppermute | solution.py:142
  52.7 0.0 copy-start.1
  52.8 34.5 %all-gather.5.cloned.1.call-done.all_spin_ref = bf16[2048,512]{1,0:T(8,128)(2,1)} async-done(((bf16[128,512]{1,0:T(8,128)(2,1)}), bf16[2048,512]{1,0:T(8,128)(2,1)}) %all-gather.5.cloned.1.call-update) | async-done | bytes 2097168 | tf_op jit(solution)/shard_map/all_gather | solution.py:111
  87.3 42.4 %all-gather.3.cloned.1.call-done.all_res_ref = bf16[2048,512]{1,0:T(8,128)(2,1)} async-done(((bf16[128,512]{1,0:T(8,128)(2,1)}), bf16[2048,512]{1,0:T(8,128)(2,1)}) %all-gather.3.cloned.1.call-update) | async-done | bytes 2097168 | tf_op jit(solution)/shard_map/all_gather | solution.py:136
  129.7 0.0 copy-done.1
  129.7 5.9 %update.1 = bf16[256,2048]{1,0:T(8,128)(2,1)} custom-call(s32[3]{0:T(128)} %pad_add_fusion.place_ref, bf16[256,512]{1,0:T(8,128)(2,1)} %gather_spins.1.spin_ref, bf16[256,512]{1,0:T(8,128)(2,1)} %copy-done.1, bf16[2048,512]{1,0:T(8,128)(2,1)} %all-gather.3.cloned.1.call-done.all_res_ref, bf16[2048,512]{1,0:T(8,128)(2,1)} %all-gather.5.cloned.1.call-done.all_spin_ref, ...), custom_call_target="tpu_custom_call" | custom-call | tf_op jit(solution)/shard_map/update/pallas_call | solution.py:66
  (2 shorter events, 0.0 us)
Async XLA Ops:
  6.5 80.8 %all-gather.5.cloned.1.call-start = ((), (), s32[]{:S(2)}) async-start(), calls=%async_computation.1 | async-start | bytes 2228224 | tf_op jit(solution)/shard_map/all_gather | solution.py:111
  8.1 4.8 %collective-permute-start = (bf16[256,1024]{0,1:T(8,128)(2,1)S(1)}, bf16[256,1024]{0,1:T(8,128)(2,1)S(1)}, u32[]{:S(2)}, u32[]{:S(2)}) collective-permute-start(bf16[256,1024]{0,1:T(8,128)(2,1)S(1)} %bitcast.47), channel_id=1, source_target_pairs={{0,1},{1,0},{2,3},{3,2},{4,5},{5,4},{6,7},{7,6},{8,9},{9,8},{10,11... | collective-permute-start | bytes 1572872 | tf_op jit(solution)/shard_map/ppermute | solution.py:106
  11.2 1.7 %collective-permute-start.1 = (bf16[256,512]{1,0:T(8,128)(2,1)}, bf16[256,512]{1,0:T(8,128)(2,1)S(1)}, u32[]{:S(2)}, u32[]{:S(2)}) collective-permute-start(bf16[256,512]{1,0:T(8,128)(2,1)} %gather_spins.1.spin_ref), channel_id=1, source_target_pairs={{0,1},{1,0},{2,3},{3,2},{4,5},{5,4},{6,7},{7,6},{8,9},{9,8},{10,11... | collective-permute-start | bytes 786440 | tf_op jit(solution)/shard_map/ppermute | solution.py:109
  13.4 32.1 %copy-start = (bf16[256,512]{1,0:T(8,128)(2,1)S(1)}, bf16[256,512]{1,0:T(8,128)(2,1)}, u32[]{:S(2)}) copy-start(bf16[256,512]{1,0:T(8,128)(2,1)} %gather_spins.1.spin_ref) | copy-start | bytes 786436
  13.4 32.1 %copy-start.2 = (f32[1,128]{1,0:T(1,128)S(1)}, f32[1,128]{1,0:T(1,128)}, u32[]{:S(2)}) copy-start(f32[1,128]{1,0:T(1,128)} %param.7) | copy-start | bytes 1540
  13.4 15.3 %collective-permute-start.2 = (bf16[4,128,512]{2,1,0:T(8,128)(2,1)S(1)}, bf16[4,128,512]{2,1,0:T(8,128)(2,1)}, u32[]{:S(2)}, u32[]{:S(2)}) collective-permute-start(bf16[4,128,512]{2,1,0:T(8,128)(2,1)S(1)} %fusion), channel_id=1, source_target_pairs={{0,2},{1,3},{2,0},{3,1},{4,6},{5,7},{6,4},{7,5},{8,10},{9,11},{10,... | collective-permute-start | bytes 1572872 | tf_op jit(solution)/shard_map/ppermute | solution.py:119
  30.0 8.3 %collective-permute-start.3 = (bf16[128,512]{1,0:T(8,128)(2,1)S(1)}, bf16[128,512]{1,0:T(8,128)(2,1)S(1)}, u32[]{:S(2)}, u32[]{:S(2)}) collective-permute-start(bf16[128,512]{1,0:T(8,128)(2,1)S(1)} %get-tuple-element.8), channel_id=1, source_target_pairs={{0,4},{1,5},{2,6},{3,7},{4,8},{5,9},{6,10},{7,11},{8,12},{9,13},{1... | collective-permute-start | bytes 393224 | tf_op jit(solution)/shard_map/ppermute | solution.py:124
  31.9 7.5 %collective-permute-start.5 = (bf16[128,512]{1,0:T(8,128)(2,1)S(1)}, bf16[128,512]{1,0:T(8,128)(2,1)S(1)}, u32[]{:S(2)}, u32[]{:S(2)}) collective-permute-start(bf16[128,512]{1,0:T(8,128)(2,1)S(1)} %get-tuple-element.9), channel_id=1, source_target_pairs={{0,12},{1,13},{2,14},{3,15},{4,0},{5,1},{6,2},{7,3},{8,4},{9,5},{1... | collective-permute-start | bytes 393224 | tf_op jit(solution)/shard_map/ppermute | solution.py:124
  34.0 11.6 %collective-permute-start.4 = (bf16[128,512]{1,0:T(8,128)(2,1)S(1)}, bf16[128,512]{1,0:T(8,128)(2,1)S(1)}, u32[]{:S(2)}, u32[]{:S(2)}) collective-permute-start(bf16[128,512]{1,0:T(8,128)(2,1)S(1)} %get-tuple-element.10), channel_id=1, source_target_pairs={{0,8},{1,9},{2,10},{3,11},{4,12},{5,13},{6,14},{7,15},{8,0},{9,1},... | collective-permute-start | bytes 393224 | tf_op jit(solution)/shard_map/ppermute | solution.py:124
  46.4 83.2 %all-gather.3.cloned.1.call-start = ((), (), s32[]{:S(2)}) async-start(), calls=%async_computation | async-start | bytes 2228224 | tf_op jit(solution)/shard_map/all_gather | solution.py:136
  47.2 5.5 %collective-permute-start.6 = (bf16[128,512]{1,0:T(8,128)(2,1)}, bf16[128,512]{1,0:T(8,128)(2,1)S(1)}, u32[]{:S(2)}, u32[]{:S(2)}) collective-permute-start(bf16[128,512]{1,0:T(8,128)(2,1)} %get-tuple-element.6), channel_id=1, source_target_pairs={{0,16},{16,0},{1,17},{17,1},{2,18},{18,2},{3,19},{19,3},{4,20},{20... | collective-permute-start | bytes 393224 | tf_op jit(solution)/shard_map/ppermute | solution.py:142
  52.7 76.9 %copy-start.1 = (bf16[256,512]{1,0:T(8,128)(2,1)}, bf16[256,512]{1,0:T(8,128)(2,1)S(1)}, u32[]{:S(2)}) copy-start(bf16[256,512]{1,0:T(8,128)(2,1)S(1)} %constant_dynamic-update-slice_fusion.res_ref) | copy-start | bytes 786436
Sparse Core Ops, SparseCore 0:
  46.6 40.6 all-gather.4
  89.5 40.1 all-gather.2

commit v2 on v1

v2 whole, which is shorter than its diff:
```python
import functools
import math

import jax
import jax.numpy as jnp
from jax import lax
from jax.experimental import pallas as pl
from jax.experimental.pallas import tpu as pltpu
from jax.sharding import PartitionSpec as P

DRIFT = 0.01
DATA_RATIO = 900.0
NOISE_SCALE = math.sqrt(0.02)
NT = (((1,), (1,)), ((), ()))
TN = (((0,), (0,)), ((), ()))


def spins_kernel(index_ref, responses_ref, spins_ref):
    pool = responses_ref.shape[0]
    batch = index_ref.shape[1]
    row_ids = lax.broadcasted_iota(jnp.int32, (pool, batch), 0)
    picks = jnp.where(row_ids == index_ref[...], 1.0, 0.0).astype(jnp.bfloat16)
    pool_spins = (2 * responses_ref[...] - 1).astype(jnp.float32).astype(jnp.bfloat16)
    spins_ref[...] = lax.dot_general(
        pool_spins, picks, TN, preferred_element_type=jnp.float32
    ).astype(jnp.bfloat16)


def gather_spins(responses, indices):
    return pl.pallas_call(
        spins_kernel,
        out_shape=jax.ShapeDtypeStruct((responses.shape[1], indices.shape[0]), jnp.bfloat16),
        name="gather_spins",
    )(indices[None], responses)


def block_rows(block, sub_len):
    return pl.ds(pl.multiple_of(block * sub_len, sub_len), sub_len)


def off_diag(grad, place_ref, sub_len):
    row_ids = lax.broadcasted_iota(jnp.int32, grad.shape, 0) - place_ref[0]
    col_ids = lax.broadcasted_iota(jnp.int32, grad.shape, 1) - place_ref[1] * sub_len
    on_diag = (col_ids == row_ids) & (row_ids >= 0) & (row_ids < sub_len)
    return jnp.where(on_diag, 0.0, grad)


def base_kernel(inv_root, place_ref, res_ref, *refs):
    *spin_refs, couple_ref, noise_ref, base_ref, spin_scr = refs
    sub_len = spin_refs[0].shape[1]
    step = pl.program_id(0)
    for low in range(8):
        block = spin_refs[low % 4][2 * step + low // 4]
        spin_scr[block_rows(place_ref[1] ^ low, sub_len), :] = block
    grad = lax.dot_general(res_ref[...], spin_scr[...], NT, preferred_element_type=jnp.float32)
    grad = jnp.where(step == 0, off_diag(grad, place_ref, sub_len), grad) * inv_root
    current = couple_ref[...].astype(jnp.float32)
    base_ref[...] = (
        current
        + DRIFT * (DATA_RATIO * grad - current)
        + NOISE_SCALE * noise_ref[...].astype(jnp.float32)
    )


def base_update(place, res, spin_blocks, couple, noise, inv_root):
    rows, width = couple.shape
    batch = res.shape[1]
    n_far, sub_len = spin_blocks[0].shape[0] // 2, spin_blocks[0].shape[1]
    columns = pl.BlockSpec((rows, 8 * sub_len), lambda j, place: (0, place[2] ^ j))
    whole = lambda array: pl.BlockSpec(array.shape, lambda j, place: (0,) * array.ndim)
    return pl.pallas_call(
        functools.partial(base_kernel, inv_root),
        grid_spec=pltpu.PrefetchScalarGridSpec(
            num_scalar_prefetch=1,
            grid=(n_far,),
            in_specs=[whole(res)] + [whole(x) for x in spin_blocks] + [columns, columns],
            out_specs=columns,
            scratch_shapes=[pltpu.VMEM((8 * sub_len, batch), jnp.bfloat16)],
        ),
        out_shape=jax.ShapeDtypeStruct((rows, width), jnp.float32),
        name="base_update",
    )(place, res, *spin_blocks, couple, noise)


def add_kernel(inv_root, step, place_ref, spin_ref, *refs):
    res_refs, peer_ref, base_ref, out_ref, res_scr = refs[:4], refs[4], refs[5], refs[-2], refs[-1]
    sub_len = res_refs[0].shape[0]
    for pair in range(4):
        low = 2 * pair
        res_scr[block_rows(place_ref[1] ^ low, sub_len), :] = res_refs[pair][...]
        res_scr[block_rows(place_ref[1] ^ (low + 1), sub_len), :] = peer_ref[pair]
    grad = lax.dot_general(spin_ref[...], res_scr[...], NT, preferred_element_type=jnp.float32)
    if step == 0:
        grad = off_diag(grad, place_ref, sub_len)
    out_ref[...] = (base_ref[...] + (DRIFT * DATA_RATIO * inv_root) * grad).astype(jnp.bfloat16)


def add_update(place, spins, blocks, peers, base, out, step, inv_root):
    rows, width = base.shape
    sub_len, batch = blocks[0].shape
    columns = pl.BlockSpec((rows, 8 * sub_len), lambda j, place: (0, place[2] ^ step))
    whole = lambda array: pl.BlockSpec(array.shape, lambda j, place: (0,) * array.ndim)
    operands = [spins, *blocks, peers]
    specs = [whole(x) for x in operands] + [columns]
    operands.append(base)
    aliases = {}
    if out is not None:
        aliases = {1 + len(operands): 0}
        operands.append(out)
        specs.append(pl.BlockSpec(memory_space=pl.ANY))
    return pl.pallas_call(
        functools.partial(add_kernel, inv_root, step),
        grid_spec=pltpu.PrefetchScalarGridSpec(
            num_scalar_prefetch=1,
            grid=(1,),
            in_specs=specs,
            out_specs=columns,
            scratch_shapes=[pltpu.VMEM((8 * sub_len, batch), jnp.bfloat16)],
        ),
        out_shape=jax.ShapeDtypeStruct((rows, width), jnp.bfloat16),
        input_output_aliases=aliases,
        name="add_update",
    )(place, *operands)


def shards(coupling, noise, bias, responses, indices):
    couple = coupling[0]
    item_dev = couple.shape[0]
    batch = indices.shape[0]
    n_resp = lax.axis_size("resp")
    n_item = lax.axis_size("item")
    sub_len = item_dev // n_resp
    n_far = n_item // 4
    inv_root = 1.0 / math.sqrt(item_dev * n_item)
    resp_idx = lax.axis_index("resp")
    item_idx = lax.axis_index("item")
    far_idx, near_idx, core_idx = item_idx // 4, item_idx // 2 % 2, item_idx % 2
    own_start = resp_idx * sub_len

    def swap(array, bits):
        return lax.ppermute(array, "item", [(i, i ^ bits) for i in range(n_item)])

    def half(blocks, axis, index):
        return lax.dynamic_index_in_dim(blocks, index, axis, keepdims=False)

    by_core = couple.reshape(item_dev, 2 * n_far, 2, sub_len)
    kept = half(by_core, 2, core_idx).reshape(item_dev, -1)
    given = half(by_core, 2, 1 - core_idx).reshape(item_dev, -1)
    got = swap(given, 1)

    spins = gather_spins(responses, indices)
    peer_spins = swap(spins, 1)
    own_spins = lax.dynamic_slice_in_dim(spins, own_start, sub_len, 0)

    partial = lax.dot_general(
        kept, spins, TN, preferred_element_type=jnp.float32
    ) + lax.dot_general(got, peer_spins, TN, preferred_element_type=jnp.float32)

    by_near = partial.reshape(n_far, 2, sub_len, batch)
    sent = half(by_near, 1, 1 - near_idx).astype(jnp.bfloat16)
    held = half(by_near, 1, near_idx) + swap(sent, 2).astype(jnp.float32)
    total = half(held, 0, far_idx)
    for step in range(1, n_far):
        piece = half(held, 0, far_idx ^ step).astype(jnp.bfloat16)
        total = total + swap(piece, 4 * step).astype(jnp.float32)

    line_spins = jnp.stack([own_spins] + [swap(own_spins, 4 * step) for step in range(1, n_far)])
    near_spins = swap(line_spins, 2)
    spin_blocks = [line_spins, swap(line_spins, 1), near_spins, swap(near_spins, 1)]

    diag_block = lax.dynamic_slice(couple, (own_start, item_idx * sub_len), (sub_len, sub_len))
    row_ids = lax.broadcasted_iota(jnp.int32, (sub_len, sub_len), 0)
    col_ids = lax.broadcasted_iota(jnp.int32, (sub_len, sub_len), 1)
    self_weight = jnp.sum(
        jnp.where(row_ids == col_ids, diag_block.astype(jnp.float32), 0.0), axis=1, keepdims=True
    )
    own_spin = own_spins.astype(jnp.float32)
    fields = (total - self_weight * own_spin) * inv_root + bias[0][:, None]
    residual = (0.5 * (own_spin + 1.0) - jax.nn.sigmoid(fields)).astype(jnp.bfloat16)

    row_res = lax.dynamic_update_slice_in_dim(
        jnp.zeros((item_dev, batch), jnp.bfloat16), residual, own_start, 0
    )
    for step in range(1, n_resp):
        ring = [(i, (i + step) % n_resp) for i in range(n_resp)]
        came = lax.ppermute(residual, "resp", ring)
        source = (resp_idx - step) % n_resp
        row_res = lax.dynamic_update_slice_in_dim(row_res, came, source * sub_len, 0)

    place = jnp.stack([own_start, item_idx % 8, item_idx // 8]).astype(jnp.int32)
    base = base_update(place, row_res, spin_blocks, couple, noise[0], inv_root)
    out = None
    for step in range(n_item // 8):
        start = swap(residual, 8 * step) if step else residual
        blocks = [start] + [swap(start, bits) for bits in (2, 4, 6)]
        out = add_update(place, spins, blocks, swap(jnp.stack(blocks), 1), base, out, step, inv_root)
    return out[None]


def solution(mesh):
    return jax.shard_map(
        shards,
        mesh=mesh,
        in_specs=(
            P("resp", "item", None),
            P("resp", "item", None),
            P("item", "resp"),
            P(None, "item"),
            P(),
        ),
        out_specs=P("resp", "item", None),
        check_vma=False,
    )
```

time: 143 us -> 99.9 us (0.70)
  waiting for transfers between devices: 104 us -> 47.4 us
  starting transfers between devices: 9.83 us -> 28.4 us
  between operations: 13.5 us -> 0.29 us
  Pallas kernels: 8.45 us -> 15.3 us
  local copies, waits for them, and re-layouts: 1.75 us -> 3.24 us
    all_gather x2 -> x0, waiting for transfers between devices: 76.9 us -> none  [the longest x1 42.4 us: shards(): all_res = lax.all_gather(residual, 'item', axis=0, tiled=True)]
    ppermute x6 -> x21, waiting for transfers between devices: 22.6 us -> 43.7 us  [swap(): return lax.ppermute(array, 'item', [(i, i ^ bits) for i in range(n_item)])]
    ppermute x6 -> x21, starting transfers between devices: 8.19 us -> 26.8 us  [swap(): return lax.ppermute(array, 'item', [(i, i ^ bits) for i in range(n_item)])]
    pallas_call x1 -> x3, Pallas kernels: 5.95 us -> 12.8 us  [the longest x2 7.43 us: add_update(): pl.pallas_call(functools.partial(add_kernel, inv_root, step), grid_spec=p...]
    unnamed x7 -> x27, local copies, waits for them, and re-layouts: 1.49 us -> 2.97 us
  transfers between devices with their start and end apart: 9 -> 22, of which waited for: 8 -> 11; matrix products, arithmetic and copies ran while one was open for 2% -> 3% of each run, Pallas kernels for 2% -> 12%
where the time goes in v2:
time: 99.9 us; the launch traced here: 99.5 us
  waiting for transfers between devices  47.4 us (47%)
  starting transfers between devices  28.4 us (28%)
  Pallas kernels  15.3 us (15%)
  local copies, waits for them, and re-layouts  3.24 us (3%)
  other arithmetic  3.05 us (3%)
  matrix products  1.8 us (2%)
    ppermute x21, waiting for transfers between devices, swap(): return lax.ppermute(array, 'item', [(i, i ^ bits) for i in range(n_item)])  43.7 us
    ppermute x21, starting transfers between devices, swap(): return lax.ppermute(array, 'item', [(i, i ^ bits) for i in range(n_item)])  26.8 us
    pallas_call x2, Pallas kernels, add_update(): pl.pallas_call(functools.partial(add_kernel, inv_root, step), grid_spec=p...  7.43 us
    pallas_call x1, Pallas kernels, base_update(): pl.pallas_call(functools.partial(base_kernel, inv_root), grid_spec=pltpu....  5.36 us
    ppermute x1, waiting for transfers between devices, shards(): came = lax.ppermute(residual, 'resp', ring)  3.76 us
    unnamed x27, local copies, waits for them, and re-layouts  2.97 us
    pallas_call x1, Pallas kernels, gather_spins(): pl.pallas_call(spins_kernel, out_shape=jax.ShapeDtypeStruct((responses.sh...  2.51 us
  transfers between devices with their start and end apart: 22, of which 11 were waited for; matrix products, arithmetic and copies ran while one was open for 3% of the time, Pallas kernels for 12%

profile of v2, /device:TPU:0, one launch (start us, length us, event | category | flops | bytes accessed | tf_op | source)
XLA Modules:
  0.0 99.5 jit_solution(264916829601271299)
XLA Ops:
  0.0 1.5 %copy.8 = bf16[1,256,2048]{1,2,0:T(8,128)(2,1)S(1)} copy(bf16[1,256,2048]{2,1,0:T(8,128)(2,1)} %param.5) | data formatting | bytes 2097152 | tf_op args[0]
  1.5 0.1 constant_dynamic-slice_fusion
  1.6 0.5 collective-permute-start
  2.1 2.5 %gather_spins.1.spin_ref = bf16[256,512]{1,0:T(8,128)(2,1)} custom-call(s32[1,512]{1,0:T(1,128)} %bitcast.73, s32[1024,256]{1,0:T(8,128)} %responses_ref.1), custom_call_target="tpu_custom_call" | custom-call | tf_op jit(solution)/shard_map/gather_spins/pallas_call | solution.py:30
  4.6 0.1 collective-permute-start.1
  4.7 1.4 %fusion.18 = f32[1024,512]{1,0:T(8,128)S(1)} fusion(bf16[256,1024]{0,1:T(8,128)(2,1)S(1)} %bitcast.58, bf16[256,512]{1,0:T(8,128)(2,1)} %gather_spins.1.spin_ref), kind=kOutput, calls=%fused_computation.37 | convolution fusion | flops 268435456 | bytes 2883584 | tf_op jit(solution)/shard_map/dot_general | solution.py:155
  6.1 0.3 collective-permute-done.1
  6.4 0.0 collective-permute-done
  6.4 0.4 convolution_add_fusion
  6.8 0.1 fusion
  6.9 0.0 copy-start.12
  6.9 2.7 %collective-permute-start.2 = (bf16[4,128,512]{2,1,0:T(8,128)(2,1)S(1)}, bf16[4,128,512]{2,1,0:T(8,128)(2,1)}, u32[]{:S(2)}, u32[]{:S(2)}) collective-permute-start(bf16[4,128,512]{2,1,0:T(8,128)(2,1)S(1)} %fusion), channel_id=1, source_target_pairs={{0,2},{1,3},{2,0},{3,1},{4,6},{5,7},{6,4},{7,5},{8,10},{9,11},{10,... | collective-permute-start | bytes 1572872 | tf_op jit(solution)/shard_map/ppermute | solution.py:141
  9.6 12.5 %collective-permute-done.2 = bf16[4,128,512]{2,1,0:T(8,128)(2,1)} collective-permute-done((bf16[4,128,512]{2,1,0:T(8,128)(2,1)S(1)}, bf16[4,128,512]{2,1,0:T(8,128)(2,1)}, u32[]{:S(2)}, u32[]{:S(2)}) %collective-permute-start.2) | collective-permute-done | bytes 524320 | tf_op jit(solution)/shard_map/ppermute | solution.py:141
  22.2 1.2 %bitcast_add_fusion = f32[4,128,512]{2,1,0:T(8,128)S(1)} fusion(bf16[4,128,512]{2,1,0:T(8,128)(2,1)} %collective-permute-done.2, f32[4,2,128,512]{3,2,1,0:T(8,128)S(1)} %bitcast.55, s32[]{:T(128)S(6)} %select_n.79), kind=kLoop, calls=%fused_computation.2 | loop fusion | flops 524288 | bytes 2621444 | tf_op jit(solution)/shard_map/add | solution.py:161
  23.4 0.1 fusion.13
  23.5 1.9 %collective-permute-start.3 = (bf16[128,512]{1,0:T(8,128)(2,1)S(1)}, bf16[128,512]{1,0:T(8,128)(2,1)S(1)}, u32[]{:S(2)}, u32[]{:S(2)}) collective-permute-start(bf16[128,512]{1,0:T(8,128)(2,1)S(1)} %get-tuple-element.8), channel_id=1, source_target_pairs={{0,4},{1,5},{2,6},{3,7},{4,0},{5,1},{6,2},{7,3},{8,12},{9,13},{10,... | collective-permute-start | bytes 393224 | tf_op jit(solution)/shard_map/ppermute | solution.py:141
  25.3 2.6 %collective-permute-start.4 = (bf16[128,512]{1,0:T(8,128)(2,1)S(1)}, bf16[128,512]{1,0:T(8,128)(2,1)S(1)}, u32[]{:S(2)}, u32[]{:S(2)}) collective-permute-start(bf16[128,512]{1,0:T(8,128)(2,1)S(1)} %get-tuple-element.10), channel_id=1, source_target_pairs={{0,8},{1,9},{2,10},{3,11},{4,12},{5,13},{6,14},{7,15},{8,0},{9,1},... | collective-permute-start | bytes 393224 | tf_op jit(solution)/shard_map/ppermute | solution.py:141
  27.9 0.0 collective-permute-start.5
  27.9 0.9 fusion.16
  28.8 1.4 %collective-permute-done.3 = bf16[128,512]{1,0:T(8,128)(2,1)S(1)} collective-permute-done((bf16[128,512]{1,0:T(8,128)(2,1)S(1)}, bf16[128,512]{1,0:T(8,128)(2,1)S(1)}, u32[]{:S(2)}, u32[]{:S(2)}) %collective-permute-start.3) | collective-permute-done | bytes 131104 | tf_op jit(solution)/shard_map/ppermute | solution.py:141
  30.2 7.8 %collective-permute-done.4 = bf16[128,512]{1,0:T(8,128)(2,1)S(1)} collective-permute-done((bf16[128,512]{1,0:T(8,128)(2,1)S(1)}, bf16[128,512]{1,0:T(8,128)(2,1)S(1)}, u32[]{:S(2)}, u32[]{:S(2)}) %collective-permute-start.4) | collective-permute-done | bytes 131104 | tf_op jit(solution)/shard_map/ppermute | solution.py:141
  38.0 0.0 collective-permute-done.5
  38.0 0.2 constant_dynamic-update-slice_fusion.1
  38.2 2.0 %collective-permute-start.12 = (bf16[128,512]{1,0:T(8,128)(2,1)S(1)}, bf16[128,512]{1,0:T(8,128)(2,1)S(1)}, u32[]{:S(2)}, u32[]{:S(2)}) collective-permute-start(bf16[128,512]{1,0:T(8,128)(2,1)S(1)} %get-tuple-element.7), channel_id=1, source_target_pairs={{0,4},{1,5},{2,6},{3,7},{4,0},{5,1},{6,2},{7,3},{8,12},{9,13},{10,... | collective-permute-start | bytes 393224 | tf_op jit(solution)/shard_map/ppermute | solution.py:141
  40.3 1.1 %collective-permute-start.13 = (bf16[128,512]{1,0:T(8,128)(2,1)S(1)}, bf16[128,512]{1,0:T(8,128)(2,1)S(1)}, u32[]{:S(2)}, u32[]{:S(2)}) collective-permute-start(bf16[128,512]{1,0:T(8,128)(2,1)S(1)} %get-tuple-element.7), channel_id=1, source_target_pairs={{0,8},{1,9},{2,10},{3,11},{4,12},{5,13},{6,14},{7,15},{8,0},{9,1},... | collective-permute-start | bytes 393224 | tf_op jit(solution)/shard_map/ppermute | solution.py:141
  41.4 1.4 %collective-permute-start.14 = (bf16[128,512]{1,0:T(8,128)(2,1)S(1)}, bf16[128,512]{1,0:T(8,128)(2,1)S(1)}, u32[]{:S(2)}, u32[]{:S(2)}) collective-permute-start(bf16[128,512]{1,0:T(8,128)(2,1)S(1)} %get-tuple-element.7), channel_id=1, source_target_pairs={{0,12},{1,13},{2,14},{3,15},{4,8},{5,9},{6,10},{7,11},{8,4},{9,5},... | collective-permute-start | bytes 393224 | tf_op jit(solution)/shard_map/ppermute | solution.py:141
  42.8 1.9 %collective-permute-done.12 = bf16[128,512]{1,0:T(8,128)(2,1)S(1)} collective-permute-done((bf16[128,512]{1,0:T(8,128)(2,1)S(1)}, bf16[128,512]{1,0:T(8,128)(2,1)S(1)}, u32[]{:S(2)}, u32[]{:S(2)}) %collective-permute-start.12) | collective-permute-done | bytes 131104 | tf_op jit(solution)/shard_map/ppermute | solution.py:141
  44.6 7.2 %collective-permute-done.13 = bf16[128,512]{1,0:T(8,128)(2,1)S(1)} collective-permute-done((bf16[128,512]{1,0:T(8,128)(2,1)S(1)}, bf16[128,512]{1,0:T(8,128)(2,1)S(1)}, u32[]{:S(2)}, u32[]{:S(2)}) %collective-permute-start.13) | collective-permute-done | bytes 131104 | tf_op jit(solution)/shard_map/ppermute | solution.py:141
  51.9 0.0 collective-permute-done.14
  51.9 0.1 pad_maximum_fusion.1.refs_0_
  52.0 0.0 copy-start.1
  52.0 1.6 %collective-permute-start.16 = (bf16[4,128,512]{2,1,0:T(8,128)(2,1)S(1)}, bf16[4,128,512]{2,1,0:T(8,128)(2,1)}, u32[]{:S(2)}, u32[]{:S(2)}) collective-permute-start(bf16[4,128,512]{2,1,0:T(8,128)(2,1)S(1)} %pad_maximum_fusion.1.refs_0_), channel_id=1, source_target_pairs={{0,2},{1,3},{2,0},{3,1},{4,6},{5,7},{6,4},{7,5},{8,10},{9,11},{10,... | collective-permute-start | bytes 1572872 | tf_op jit(solution)/shard_map/ppermute | solution.py:141
  53.5 2.9 %collective-permute-start.6 = (bf16[128,512]{1,0:T(8,128)(2,1)S(1)}, bf16[128,512]{1,0:T(8,128)(2,1)S(1)}, u32[]{:S(2)}, u32[]{:S(2)}) collective-permute-start(bf16[128,512]{1,0:T(8,128)(2,1)S(1)} %get-tuple-element.6.refs_0_), channel_id=1, source_target_pairs={{0,8},{1,9},{2,10},{3,11},{4,12},{5,13},{6,14},{7,15},{8,0},{9,1},... | collective-permute-start | bytes 393224 | tf_op jit(solution)/shard_map/ppermute | solution.py:141
  56.5 0.5 collective-permute-start.18
  57.0 0.0 collective-permute-start.19
  57.0 3.0 %collective-permute-start.20 = (bf16[128,512]{1,0:T(8,128)(2,1)S(1)}, bf16[128,512]{1,0:T(8,128)(2,1)S(1)}, u32[]{:S(2)}, u32[]{:S(2)}) collective-permute-start(bf16[128,512]{1,0:T(8,128)(2,1)S(1)} %get-tuple-element.6.refs_0_), channel_id=1, source_target_pairs={{0,6},{1,7},{2,4},{3,5},{4,2},{5,3},{6,0},{7,1},{8,14},{9,15},{10,... | collective-permute-start | bytes 393224 | tf_op jit(solution)/shard_map/ppermute | solution.py:141
  60.0 1.6 %collective-permute-done.6.refs_0_ = bf16[128,512]{1,0:T(8,128)(2,1)S(1)} collective-permute-done((bf16[128,512]{1,0:T(8,128)(2,1)S(1)}, bf16[128,512]{1,0:T(8,128)(2,1)S(1)}, u32[]{:S(2)}, u32[]{:S(2)}) %collective-permute-start.6) | collective-permute-done | bytes 131104 | tf_op jit(solution)/shard_map/ppermute | solution.py:141
  61.6 0.6 collective-permute-start.7
  62.2 6.8 %collective-permute-done.18.refs_1_ = bf16[128,512]{1,0:T(8,128)(2,1)S(1)} collective-permute-done((bf16[128,512]{1,0:T(8,128)(2,1)S(1)}, bf16[128,512]{1,0:T(8,128)(2,1)S(1)}, u32[]{:S(2)}, u32[]{:S(2)}) %collective-permute-start.18) | collective-permute-done | bytes 131104 | tf_op jit(solution)/shard_map/ppermute | solution.py:141
  69.0 4.2 %collective-permute-start.8 = (bf16[128,512]{1,0:T(8,128)(2,1)S(1)}, bf16[128,512]{1,0:T(8,128)(2,1)S(1)}, u32[]{:S(2)}, u32[]{:S(2)}) collective-permute-start(bf16[128,512]{1,0:T(8,128)(2,1)S(1)} %collective-permute-done.6.refs_0_), channel_id=1, source_target_pairs={{0,4},{1,5},{2,6},{3,7},{4,0},{5,1},{6,2},{7,3},{8,12},{9,13},{10,... | collective-permute-start | bytes 393224 | tf_op jit(solution)/shard_map/ppermute | solution.py:141
  73.2 0.0 collective-permute-done.19.refs_2_
  73.2 1.0 %collective-permute-start.9 = (bf16[128,512]{1,0:T(8,128)(2,1)S(1)}, bf16[128,512]{1,0:T(8,128)(2,1)S(1)}, u32[]{:S(2)}, u32[]{:S(2)}) collective-permute-start(bf16[128,512]{1,0:T(8,128)(2,1)S(1)} %collective-permute-done.6.refs_0_), channel_id=1, source_target_pairs={{0,6},{1,7},{2,4},{3,5},{4,2},{5,3},{6,0},{7,1},{8,14},{9,15},{10,... | collective-permute-start | bytes 393224 | tf_op jit(solution)/shard_map/ppermute | solution.py:141
  74.2 0.0 collective-permute-done.20.refs_3_
  74.2 0.0 collective-permute-start.15
  74.2 0.1 pad_maximum_fusion.2
  74.3 0.0 collective-permute-done.7.refs_1_
  74.3 0.6 collective-permute-start.21
  74.9 0.0 collective-permute-done.16.refs_2_
  74.9 0.1 collective-permute-start.17
  75.0 1.2 %collective-permute-done.8.refs_2_ = bf16[128,512]{1,0:T(8,128)(2,1)S(1)} collective-permute-done((bf16[128,512]{1,0:T(8,128)(2,1)S(1)}, bf16[128,512]{1,0:T(8,128)(2,1)S(1)}, u32[]{:S(2)}, u32[]{:S(2)}) %collective-permute-start.8) | collective-permute-done | bytes 131104 | tf_op jit(solution)/shard_map/ppermute | solution.py:141
  76.1 2.9 %collective-permute-done.9.refs_3_ = bf16[128,512]{1,0:T(8,128)(2,1)S(1)} collective-permute-done((bf16[128,512]{1,0:T(8,128)(2,1)S(1)}, bf16[128,512]{1,0:T(8,128)(2,1)S(1)}, u32[]{:S(2)}, u32[]{:S(2)}) %collective-permute-start.9) | collective-permute-done | bytes 131104 | tf_op jit(solution)/shard_map/ppermute | solution.py:141
  79.1 0.1 pad_maximum_fusion
  79.1 0.1 collective-permute-start.10
  79.2 1.6 %collective-permute-start.11 = (bf16[128,512]{1,0:T(8,128)(2,1)S(1)}, bf16[128,512]{1,0:T(8,128)(2,1)S(1)}, u32[]{:S(2)}, u32[]{:S(2)}) collective-permute-start(bf16[128,512]{1,0:T(8,128)(2,1)S(1)} %get-tuple-element.6.refs_0_), channel_id=1, source_target_pairs={{0,16},{16,0},{1,17},{17,1},{2,18},{18,2},{3,19},{19,3},{4,20},{20... | collective-permute-start | bytes 393224 | tf_op jit(solution)/shard_map/ppermute | solution.py:186
  80.8 0.6 pad_add_fusion.place_ref
  81.4 3.8 %collective-permute-done.11 = bf16[128,512]{1,0:T(8,128)(2,1)S(1)} collective-permute-done((bf16[128,512]{1,0:T(8,128)(2,1)S(1)}, bf16[128,512]{1,0:T(8,128)(2,1)S(1)}, u32[]{:S(2)}, u32[]{:S(2)}) %collective-permute-start.11) | collective-permute-done | bytes 131104 | tf_op jit(solution)/shard_map/ppermute | solution.py:186
  85.2 0.0 collective-permute-done.15.refs_1_
  85.2 0.0 collective-permute-done.17.refs_3_
  85.2 0.7 copy-done.3
  85.9 5.4 %base_update.1.refs_5_ = f32[256,2048]{1,0:T(8,128)} custom-call(s32[3]{0:T(128)} %pad_add_fusion.place_ref, bf16[256,512]{1,0:T(8,128)(2,1)} %copy-done.3, bf16[4,128,512]{2,1,0:T(8,128)(2,1)} %copy-done.1, bf16[4,128,512]{2,1,0:T(8,128)(2,1)} %collective-permute-done.15.refs_1_, bf16[4,128,512]{2,1,0:T(8,128)(2,1)} %collective-permute-done.16.refs_2_, ...), custom_call_target="tpu_custom_call" | custom-call | tf_op jit(solution)/shard_map/base_update/pallas_call | solution.py:71
  91.3 0.0 collective-permute-done.21.refs_4_
  91.3 0.8 copy-done.4
  92.1 3.7 %add_update.2.refs_6_ = bf16[256,2048]{1,0:T(8,128)(2,1)} custom-call(s32[3]{0:T(128)} %pad_add_fusion.place_ref, bf16[256,512]{1,0:T(8,128)(2,1)} %gather_spins.1.spin_ref, bf16[128,512]{1,0:T(8,128)(2,1)} %copy-done.2, bf16[128,512]{1,0:T(8,128)(2,1)} %copy-done.6, bf16[128,512]{1,0:T(8,128)(2,1)} %copy-done.7, bf16[128,512]{1,0:T(8,128)(2,1)} %copy-done.9, ...), custom_call_target="tpu_custom_call" | custom-call | tf_op jit(solution)/shard_map/add_update/pallas_call | solution.py:111
  95.8 3.7 %add_update.3 = bf16[256,2048]{1,0:T(8,128)(2,1)} custom-call(s32[3]{0:T(128)} %pad_add_fusion.place_ref, bf16[256,512]{1,0:T(8,128)(2,1)} %gather_spins.1.spin_ref, bf16[128,512]{1,0:T(8,128)(2,1)} %copy-done.5, bf16[128,512]{1,0:T(8,128)(2,1)} %copy-done.8, bf16[128,512]{1,0:T(8,128)(2,1)} %copy-done.10, ...), custom_call_target="tpu_custom_call", output_to_operand_aliasing={{}: (8, {})} | custom-call | tf_op jit(solution)/shard_map/add_update/pallas_call | solution.py:111
  (25 shorter events, 0.1 us)
Async XLA Ops:
  1.6 4.8 %collective-permute-start = (bf16[256,1024]{0,1:T(8,128)(2,1)S(1)}, bf16[256,1024]{0,1:T(8,128)(2,1)S(1)}, u32[]{:S(2)}, u32[]{:S(2)}) collective-permute-start(bf16[256,1024]{0,1:T(8,128)(2,1)S(1)} %bitcast.61), channel_id=1, source_target_pairs={{0,1},{1,0},{2,3},{3,2},{4,5},{5,4},{6,7},{7,6},{8,9},{9,8},{10,11... | collective-permute-start | bytes 1572872 | tf_op jit(solution)/shard_map/ppermute | solution.py:141
  4.6 1.7 %collective-permute-start.1 = (bf16[256,512]{1,0:T(8,128)(2,1)}, bf16[256,512]{1,0:T(8,128)(2,1)S(1)}, u32[]{:S(2)}, u32[]{:S(2)}) collective-permute-start(bf16[256,512]{1,0:T(8,128)(2,1)} %gather_spins.1.spin_ref), channel_id=1, source_target_pairs={{0,1},{1,0},{2,3},{3,2},{4,5},{5,4},{6,7},{7,6},{8,9},{9,8},{10,11... | collective-permute-start | bytes 786440 | tf_op jit(solution)/shard_map/ppermute | solution.py:141
  6.9 31.1 %copy-start = (bf16[256,512]{1,0:T(8,128)(2,1)S(1)}, bf16[256,512]{1,0:T(8,128)(2,1)}, u32[]{:S(2)}) copy-start(bf16[256,512]{1,0:T(8,128)(2,1)} %gather_spins.1.spin_ref) | copy-start | bytes 786436
  6.9 31.1 %copy-start.12 = (f32[1,128]{1,0:T(1,128)S(1)}, f32[1,128]{1,0:T(1,128)}, u32[]{:S(2)}) copy-start(f32[1,128]{1,0:T(1,128)} %param.7) | copy-start | bytes 1540
  6.9 15.3 %collective-permute-start.2 = (bf16[4,128,512]{2,1,0:T(8,128)(2,1)S(1)}, bf16[4,128,512]{2,1,0:T(8,128)(2,1)}, u32[]{:S(2)}, u32[]{:S(2)}) collective-permute-start(bf16[4,128,512]{2,1,0:T(8,128)(2,1)S(1)} %fusion), channel_id=1, source_target_pairs={{0,2},{1,3},{2,0},{3,1},{4,6},{5,7},{6,4},{7,5},{8,10},{9,11},{10,... | collective-permute-start | bytes 1572872 | tf_op jit(solution)/shard_map/ppermute | solution.py:141
  23.5 6.7 %collective-permute-start.3 = (bf16[128,512]{1,0:T(8,128)(2,1)S(1)}, bf16[128,512]{1,0:T(8,128)(2,1)S(1)}, u32[]{:S(2)}, u32[]{:S(2)}) collective-permute-start(bf16[128,512]{1,0:T(8,128)(2,1)S(1)} %get-tuple-element.8), channel_id=1, source_target_pairs={{0,4},{1,5},{2,6},{3,7},{4,0},{5,1},{6,2},{7,3},{8,12},{9,13},{10,... | collective-permute-start | bytes 393224 | tf_op jit(solution)/shard_map/ppermute | solution.py:141
  25.3 12.6 %collective-permute-start.4 = (bf16[128,512]{1,0:T(8,128)(2,1)S(1)}, bf16[128,512]{1,0:T(8,128)(2,1)S(1)}, u32[]{:S(2)}, u32[]{:S(2)}) collective-permute-start(bf16[128,512]{1,0:T(8,128)(2,1)S(1)} %get-tuple-element.10), channel_id=1, source_target_pairs={{0,8},{1,9},{2,10},{3,11},{4,12},{5,13},{6,14},{7,15},{8,0},{9,1},... | collective-permute-start | bytes 393224 | tf_op jit(solution)/shard_map/ppermute | solution.py:141
  27.9 10.0 %collective-permute-start.5 = (bf16[128,512]{1,0:T(8,128)(2,1)S(1)}, bf16[128,512]{1,0:T(8,128)(2,1)S(1)}, u32[]{:S(2)}, u32[]{:S(2)}) collective-permute-start(bf16[128,512]{1,0:T(8,128)(2,1)S(1)} %get-tuple-element.9), channel_id=1, source_target_pairs={{0,12},{1,13},{2,14},{3,15},{4,8},{5,9},{6,10},{7,11},{8,4},{9,5},... | collective-permute-start | bytes 393224 | tf_op jit(solution)/shard_map/ppermute | solution.py:141
  38.2 53.0 %copy-start.2 = (bf16[128,512]{1,0:T(8,128)(2,1)}, bf16[128,512]{1,0:T(8,128)(2,1)S(1)}, u32[]{:S(2)}) copy-start(bf16[128,512]{1,0:T(8,128)(2,1)S(1)} %get-tuple-element.6.refs_0_) | copy-start | bytes 393220
  38.2 6.4 %collective-permute-start.12 = (bf16[128,512]{1,0:T(8,128)(2,1)S(1)}, bf16[128,512]{1,0:T(8,128)(2,1)S(1)}, u32[]{:S(2)}, u32[]{:S(2)}) collective-permute-start(bf16[128,512]{1,0:T(8,128)(2,1)S(1)} %get-tuple-element.7), channel_id=1, source_target_pairs={{0,4},{1,5},{2,6},{3,7},{4,0},{5,1},{6,2},{7,3},{8,12},{9,13},{10,... | collective-permute-start | bytes 393224 | tf_op jit(solution)/shard_map/ppermute | solution.py:141
  40.3 11.6 %collective-permute-start.13 = (bf16[128,512]{1,0:T(8,128)(2,1)S(1)}, bf16[128,512]{1,0:T(8,128)(2,1)S(1)}, u32[]{:S(2)}, u32[]{:S(2)}) collective-permute-start(bf16[128,512]{1,0:T(8,128)(2,1)S(1)} %get-tuple-element.7), channel_id=1, source_target_pairs={{0,8},{1,9},{2,10},{3,11},{4,12},{5,13},{6,14},{7,15},{8,0},{9,1},... | collective-permute-start | bytes 393224 | tf_op jit(solution)/shard_map/ppermute | solution.py:141
  41.4 10.5 %collective-permute-start.14 = (bf16[128,512]{1,0:T(8,128)(2,1)S(1)}, bf16[128,512]{1,0:T(8,128)(2,1)S(1)}, u32[]{:S(2)}, u32[]{:S(2)}) collective-permute-start(bf16[128,512]{1,0:T(8,128)(2,1)S(1)} %get-tuple-element.7), channel_id=1, source_target_pairs={{0,12},{1,13},{2,14},{3,15},{4,8},{5,9},{6,10},{7,11},{8,4},{9,5},... | collective-permute-start | bytes 393224 | tf_op jit(solution)/shard_map/ppermute | solution.py:141
  52.0 33.2 %copy-start.1 = (bf16[4,128,512]{2,1,0:T(8,128)(2,1)}, bf16[4,128,512]{2,1,0:T(8,128)(2,1)S(1)}, u32[]{:S(2)}) copy-start(bf16[4,128,512]{2,1,0:T(8,128)(2,1)S(1)} %pad_maximum_fusion.1.refs_0_) | copy-start | bytes 1572868
  52.0 22.9 %collective-permute-start.16 = (bf16[4,128,512]{2,1,0:T(8,128)(2,1)S(1)}, bf16[4,128,512]{2,1,0:T(8,128)(2,1)}, u32[]{:S(2)}, u32[]{:S(2)}) collective-permute-start(bf16[4,128,512]{2,1,0:T(8,128)(2,1)S(1)} %pad_maximum_fusion.1.refs_0_), channel_id=1, source_target_pairs={{0,2},{1,3},{2,0},{3,1},{4,6},{5,7},{6,4},{7,5},{8,10},{9,11},{10,... | collective-permute-start | bytes 1572872 | tf_op jit(solution)/shard_map/ppermute | solution.py:141
  53.5 8.1 %collective-permute-start.6 = (bf16[128,512]{1,0:T(8,128)(2,1)S(1)}, bf16[128,512]{1,0:T(8,128)(2,1)S(1)}, u32[]{:S(2)}, u32[]{:S(2)}) collective-permute-start(bf16[128,512]{1,0:T(8,128)(2,1)S(1)} %get-tuple-element.6.refs_0_), channel_id=1, source_target_pairs={{0,8},{1,9},{2,10},{3,11},{4,12},{5,13},{6,14},{7,15},{8,0},{9,1},... | collective-permute-start | bytes 393224 | tf_op jit(solution)/shard_map/ppermute | solution.py:141
  56.5 12.5 %collective-permute-start.18 = (bf16[128,512]{1,0:T(8,128)(2,1)S(1)}, bf16[128,512]{1,0:T(8,128)(2,1)S(1)}, u32[]{:S(2)}, u32[]{:S(2)}) collective-permute-start(bf16[128,512]{1,0:T(8,128)(2,1)S(1)} %get-tuple-element.6.refs_0_), channel_id=1, source_target_pairs={{0,2},{1,3},{2,0},{3,1},{4,6},{5,7},{6,4},{7,5},{8,10},{9,11},{10,... | collective-permute-start | bytes 393224 | tf_op jit(solution)/shard_map/ppermute | solution.py:141
  57.0 16.2 %collective-permute-start.19 = (bf16[128,512]{1,0:T(8,128)(2,1)S(1)}, bf16[128,512]{1,0:T(8,128)(2,1)S(1)}, u32[]{:S(2)}, u32[]{:S(2)}) collective-permute-start(bf16[128,512]{1,0:T(8,128)(2,1)S(1)} %get-tuple-element.6.refs_0_), channel_id=1, source_target_pairs={{0,4},{1,5},{2,6},{3,7},{4,0},{5,1},{6,2},{7,3},{8,12},{9,13},{10,... | collective-permute-start | bytes 393224 | tf_op jit(solution)/shard_map/ppermute | solution.py:141
  57.0 17.2 %collective-permute-start.20 = (bf16[128,512]{1,0:T(8,128)(2,1)S(1)}, bf16[128,512]{1,0:T(8,128)(2,1)S(1)}, u32[]{:S(2)}, u32[]{:S(2)}) collective-permute-start(bf16[128,512]{1,0:T(8,128)(2,1)S(1)} %get-tuple-element.6.refs_0_), channel_id=1, source_target_pairs={{0,6},{1,7},{2,4},{3,5},{4,2},{5,3},{6,0},{7,1},{8,14},{9,15},{10,... | collective-permute-start | bytes 393224 | tf_op jit(solution)/shard_map/ppermute | solution.py:141
  61.6 29.6 %copy-start.5 = (bf16[128,512]{1,0:T(8,128)(2,1)}, bf16[128,512]{1,0:T(8,128)(2,1)S(1)}, u32[]{:S(2)}) copy-start(bf16[128,512]{1,0:T(8,128)(2,1)S(1)} %collective-permute-done.6.refs_0_) | copy-start | bytes 393220
  61.6 12.7 %collective-permute-start.7 = (bf16[128,512]{1,0:T(8,128)(2,1)S(1)}, bf16[128,512]{1,0:T(8,128)(2,1)S(1)}, u32[]{:S(2)}, u32[]{:S(2)}) collective-permute-start(bf16[128,512]{1,0:T(8,128)(2,1)S(1)} %collective-permute-done.6.refs_0_), channel_id=1, source_target_pairs={{0,2},{1,3},{2,0},{3,1},{4,6},{5,7},{6,4},{7,5},{8,10},{9,11},{10,... | collective-permute-start | bytes 393224 | tf_op jit(solution)/shard_map/ppermute | solution.py:141
  69.0 22.2 %copy-start.6 = (bf16[128,512]{1,0:T(8,128)(2,1)}, bf16[128,512]{1,0:T(8,128)(2,1)S(1)}, u32[]{:S(2)}) copy-start(bf16[128,512]{1,0:T(8,128)(2,1)S(1)} %collective-permute-done.18.refs_1_) | copy-start | bytes 393220
  69.0 7.1 %collective-permute-start.8 = (bf16[128,512]{1,0:T(8,128)(2,1)S(1)}, bf16[128,512]{1,0:T(8,128)(2,1)S(1)}, u32[]{:S(2)}, u32[]{:S(2)}) collective-permute-start(bf16[128,512]{1,0:T(8,128)(2,1)S(1)} %collective-permute-done.6.refs_0_), channel_id=1, source_target_pairs={{0,4},{1,5},{2,6},{3,7},{4,0},{5,1},{6,2},{7,3},{8,12},{9,13},{10,... | collective-permute-start | bytes 393224 | tf_op jit(solution)/shard_map/ppermute | solution.py:141
  73.2 18.0 %copy-start.7 = (bf16[128,512]{1,0:T(8,128)(2,1)}, bf16[128,512]{1,0:T(8,128)(2,1)S(1)}, u32[]{:S(2)}) copy-start(bf16[128,512]{1,0:T(8,128)(2,1)S(1)} %collective-permute-done.19.refs_2_) | copy-start | bytes 393220
  73.2 5.9 %collective-permute-start.9 = (bf16[128,512]{1,0:T(8,128)(2,1)S(1)}, bf16[128,512]{1,0:T(8,128)(2,1)S(1)}, u32[]{:S(2)}, u32[]{:S(2)}) collective-permute-start(bf16[128,512]{1,0:T(8,128)(2,1)S(1)} %collective-permute-done.6.refs_0_), channel_id=1, source_target_pairs={{0,6},{1,7},{2,4},{3,5},{4,2},{5,3},{6,0},{7,1},{8,14},{9,15},{10,... | collective-permute-start | bytes 393224 | tf_op jit(solution)/shard_map/ppermute | solution.py:141
  74.2 17.0 %copy-start.9 = (bf16[128,512]{1,0:T(8,128)(2,1)}, bf16[128,512]{1,0:T(8,128)(2,1)S(1)}, u32[]{:S(2)}) copy-start(bf16[128,512]{1,0:T(8,128)(2,1)S(1)} %collective-permute-done.20.refs_3_) | copy-start | bytes 393220
  74.2 10.9 %collective-permute-start.15 = (bf16[4,128,512]{2,1,0:T(8,128)(2,1)S(1)}, bf16[4,128,512]{2,1,0:T(8,128)(2,1)}, u32[]{:S(2)}, u32[]{:S(2)}) collective-permute-start(bf16[4,128,512]{2,1,0:T(8,128)(2,1)S(1)} %pad_maximum_fusion.1.refs_0_), channel_id=1, source_target_pairs={{0,1},{1,0},{2,3},{3,2},{4,5},{5,4},{6,7},{7,6},{8,9},{9,8},{10,11... | collective-permute-start | bytes 1572872 | tf_op jit(solution)/shard_map/ppermute | solution.py:141
  74.3 16.9 %copy-start.8 = (bf16[128,512]{1,0:T(8,128)(2,1)}, bf16[128,512]{1,0:T(8,128)(2,1)S(1)}, u32[]{:S(2)}) copy-start(bf16[128,512]{1,0:T(8,128)(2,1)S(1)} %collective-permute-done.7.refs_1_) | copy-start | bytes 393220
  74.3 17.0 %collective-permute-start.21 = (bf16[4,128,512]{2,1,0:T(8,128)(2,1)S(1)}, bf16[4,128,512]{2,1,0:T(8,128)(2,1)S(1)}, u32[]{:S(2)}, u32[]{:S(2)}) collective-permute-start(bf16[4,128,512]{2,1,0:T(8,128)(2,1)S(1)} %pad_maximum_fusion.2), channel_id=1, source_target_pairs={{0,1},{1,0},{2,3},{3,2},{4,5},{5,4},{6,7},{7,6},{8,9},{9,8},{10,11... | collective-permute-start | bytes 1572872 | tf_op jit(solution)/shard_map/ppermute | solution.py:141
  74.9 10.3 %collective-permute-start.17 = (bf16[4,128,512]{2,1,0:T(8,128)(2,1)}, bf16[4,128,512]{2,1,0:T(8,128)(2,1)}, u32[]{:S(2)}, u32[]{:S(2)}) collective-permute-start(bf16[4,128,512]{2,1,0:T(8,128)(2,1)} %collective-permute-done.16.refs_2_), channel_id=1, source_target_pairs={{0,1},{1,0},{2,3},{3,2},{4,5},{5,4},{6,7},{7,6},{8,9},{9,8},{10,11... | collective-permute-start | bytes 1572872 | tf_op jit(solution)/shard_map/ppermute | solution.py:141
  76.1 15.1 %copy-start.10 = (bf16[128,512]{1,0:T(8,128)(2,1)}, bf16[128,512]{1,0:T(8,128)(2,1)S(1)}, u32[]{:S(2)}) copy-start(bf16[128,512]{1,0:T(8,128)(2,1)S(1)} %collective-permute-done.8.refs_2_) | copy-start | bytes 393220
  79.1 12.2 %copy-start.11 = (bf16[128,512]{1,0:T(8,128)(2,1)}, bf16[128,512]{1,0:T(8,128)(2,1)S(1)}, u32[]{:S(2)}) copy-start(bf16[128,512]{1,0:T(8,128)(2,1)S(1)} %collective-permute-done.9.refs_3_) | copy-start | bytes 393220
  79.1 16.7 %collective-permute-start.10 = (bf16[4,128,512]{2,1,0:T(8,128)(2,1)S(1)}, bf16[4,128,512]{2,1,0:T(8,128)(2,1)}, u32[]{:S(2)}, u32[]{:S(2)}) collective-permute-start(bf16[4,128,512]{2,1,0:T(8,128)(2,1)S(1)} %pad_maximum_fusion), channel_id=1, source_target_pairs={{0,1},{1,0},{2,3},{3,2},{4,5},{5,4},{6,7},{7,6},{8,9},{9,8},{10,11... | collective-permute-start | bytes 1572872 | tf_op jit(solution)/shard_map/ppermute | solution.py:141
  79.2 5.9 %collective-permute-start.11 = (bf16[128,512]{1,0:T(8,128)(2,1)S(1)}, bf16[128,512]{1,0:T(8,128)(2,1)S(1)}, u32[]{:S(2)}, u32[]{:S(2)}) collective-permute-start(bf16[128,512]{1,0:T(8,128)(2,1)S(1)} %get-tuple-element.6.refs_0_), channel_id=1, source_target_pairs={{0,16},{16,0},{1,17},{17,1},{2,18},{18,2},{3,19},{19,3},{4,20},{20... | collective-permute-start | bytes 393224 | tf_op jit(solution)/shard_map/ppermute | solution.py:186
  85.1 0.7 copy-start.3
  91.3 0.8 copy-start.4

commit v3 on v0

v3 whole, which is shorter than its diff:
```python
import math

import jax
import jax.numpy as jnp
from jax import lax
from jax.sharding import PartitionSpec as P

DRIFT = 0.01
DATA_RATIO = 900.0
NOISE_SCALE = math.sqrt(0.02)
NT = (((1,), (1,)), ((), ()))
TN = (((0,), (0,)), ((), ()))


def shards(coupling, noise, bias, responses, indices):
    couple = coupling[0]
    item_dev = couple.shape[0]
    pool, batch = responses.shape[0], indices.shape[0]
    n_resp = lax.axis_size("resp")
    n_item = lax.axis_size("item")
    sub_len = item_dev // n_resp
    n_line = n_item // 4
    width = 8 * sub_len
    inv_root = 1.0 / math.sqrt(item_dev * n_item)
    resp_idx = lax.axis_index("resp")
    item_idx = lax.axis_index("item")
    line_idx, near_idx, core_idx = item_idx // 4, item_idx // 2 % 2, item_idx % 2
    low_idx, high_idx = item_idx % 8, item_idx // 8
    own_start = resp_idx * sub_len

    def swap(array, bits):
        return lax.ppermute(array, "item", [(i, i ^ bits) for i in range(n_item)])

    def take_rows(array, index, blocks, length):
        parts = array.reshape(-1, blocks, length, array.shape[1])
        part = lax.dynamic_index_in_dim(parts, index, 1, keepdims=False)
        return part.reshape(-1, array.shape[1])

    def in_order(blocks):
        joined = jnp.zeros((8, sub_len, batch), jnp.bfloat16)
        for low, block in enumerate(blocks):
            joined = lax.dynamic_update_index_in_dim(joined, block, low_idx ^ low, 0)
        return joined.reshape(width, batch)

    by_core = couple.reshape(item_dev, -1, 2, sub_len)
    kept = lax.dynamic_index_in_dim(by_core, core_idx, 2, keepdims=False)
    given = lax.dynamic_index_in_dim(by_core, 1 - core_idx, 2, keepdims=False)
    got = swap(given.reshape(item_dev, -1), 1)
    kept = kept.reshape(item_dev, -1)

    pool_ids = lax.broadcasted_iota(jnp.int32, (pool, batch), 0)
    picks = (pool_ids == indices[None]).astype(jnp.bfloat16)
    pool_spins = (2 * responses - 1).astype(jnp.bfloat16)
    spins = lax.dot_general(pool_spins, picks, TN, preferred_element_type=jnp.float32)
    spins = spins.astype(jnp.bfloat16)
    peer_spins = swap(spins, 1)
    own_spins = lax.dynamic_slice_in_dim(spins, own_start, sub_len, 0)

    partial = lax.dot_general(
        kept, spins, TN, preferred_element_type=jnp.float32
    ) + lax.dot_general(got, peer_spins, TN, preferred_element_type=jnp.float32)

    came = swap(take_rows(partial, 1 - near_idx, 2, sub_len).astype(jnp.bfloat16), 2)
    line = [own_spins] + [swap(own_spins, 4 * step) for step in range(1, n_line)]
    came, line = lax.optimization_barrier((came, line))
    held = take_rows(partial, near_idx, 2, sub_len) + came.astype(jnp.float32)
    pieces = [
        swap(take_rows(held, line_idx ^ step, n_line, sub_len).astype(jnp.bfloat16), 4 * step)
        for step in range(1, n_line)
    ]
    line_spins = jnp.concatenate(line)
    near_spins, peer_line = swap(line_spins, 2), swap(line_spins, 1)
    pieces, near_spins, peer_line = lax.optimization_barrier((pieces, near_spins, peer_line))
    spin_groups = [line_spins, peer_line, near_spins, swap(near_spins, 1)]
    total = take_rows(held, line_idx, n_line, sub_len)
    for piece in pieces:
        total = total + piece.astype(jnp.float32)

    diag_block = lax.dynamic_slice(couple, (own_start, item_idx * sub_len), (sub_len, sub_len))
    row_ids = lax.broadcasted_iota(jnp.int32, (sub_len, sub_len), 0)
    col_ids = lax.broadcasted_iota(jnp.int32, (sub_len, sub_len), 1)
    self_weight = jnp.sum(
        jnp.where(row_ids == col_ids, diag_block.astype(jnp.float32), 0.0), axis=1, keepdims=True
    )
    own_spin = own_spins.astype(jnp.float32)
    fields = (total - self_weight * own_spin) * inv_root + bias[0][:, None]
    residual = (0.5 * (own_spin + 1.0) - jax.nn.sigmoid(fields)).astype(jnp.bfloat16)

    row_res = lax.dynamic_update_slice_in_dim(
        jnp.zeros((item_dev, batch), jnp.bfloat16), residual, own_start, 0
    )
    for step in range(1, n_resp):
        ring = [(i, (i + step) % n_resp) for i in range(n_resp)]
        other = lax.ppermute(residual, "resp", ring)
        source = (resp_idx - step) % n_resp
        row_res = lax.dynamic_update_slice_in_dim(row_res, other, source * sub_len, 0)

    row_ids = lax.broadcasted_iota(jnp.int32, (item_dev, width), 0) - own_start
    col_ids = lax.broadcasted_iota(jnp.int32, (item_dev, width), 1) - low_idx * sub_len
    on_diag = (row_ids == col_ids) & (row_ids >= 0) & (row_ids < sub_len)

    def product(left, right, step):
        grad = lax.dot_general(left, right, NT, preferred_element_type=jnp.float32)
        return jnp.where(on_diag, 0.0, grad) if step == 0 else grad

    out = jnp.zeros(couple.shape, jnp.bfloat16)
    for step in range(n_item // 8):
        start = swap(residual, 8 * step) if step else residual
        blocks = [start] + [swap(start, bits) for bits in (2, 4, 6)]
        peers = swap(jnp.stack(blocks), 1)
        all_res = in_order([x for pair in zip(blocks, peers) for x in pair])
        all_spins = in_order(
            [
                lax.slice_in_dim(group, k * sub_len, (k + 1) * sub_len, axis=0)
                for k in (2 * step, 2 * step + 1)
                for group in spin_groups
            ]
        )
        first_col = (high_idx ^ step) * width
        current = lax.dynamic_slice_in_dim(couple, first_col, width, 1).astype(jnp.float32)
        shake = lax.dynamic_slice_in_dim(noise[0], first_col, width, 1).astype(jnp.float32)
        mirror = product(row_res, all_spins, step) * inv_root
        base = current + DRIFT * (DATA_RATIO * mirror - current) + NOISE_SCALE * shake
        base = lax.optimization_barrier(base)
        part = base + (DRIFT * DATA_RATIO * inv_root) * product(spins, all_res, step)
        out = lax.dynamic_update_slice_in_dim(out, part.astype(jnp.bfloat16), first_col, 1)
    return out[None]


def solution(mesh):
    return jax.shard_map(
        shards,
        mesh=mesh,
        in_specs=(
            P("resp", "item", None),
            P("resp", "item", None),
            P("item", "resp"),
            P(None, "item"),
            P(),
        ),
        out_specs=P("resp", "item", None),
        check_vma=False,
    )
```

time: 248 us -> 75.9 us (0.31)
  the two profiles are of different devices: /device:TPU:11 before, /device:TPU:0 now
where the time goes in v3:
time: 75.9 us; the launch traced here: 75.5 us
  waiting for transfers between devices  31.6 us (42%)
  starting transfers between devices  23.4 us (31%)
  local copies, waits for them, and re-layouts  11.1 us (15%)
  matrix products  7.01 us (9%)
  other arithmetic  1.89 us (2%)
    ppermute x21, waiting for transfers between devices, swap(): return lax.ppermute(array, 'item', [(i, i ^ bits) for i in range(n_item)])  31.6 us
    ppermute x21, starting transfers between devices, swap(): return lax.ppermute(array, 'item', [(i, i ^ bits) for i in range(n_item)])  21.9 us
    unnamed x16, local copies, waits for them, and re-layouts  5.37 us
    dynamic_update_slice x27, local copies, waits for them, and re-layouts, in_order(): joined = lax.dynamic_update_index_in_dim(joined, block, low_idx ^ low, 0)  3.17 us
    dot_general x4, matrix products, product(): grad = lax.dot_general(left, right, NT, preferred_element_type=jnp.float32)  3.1 us
    dot_general x1, matrix products, shards(): lax.dot_general(pool_spins, picks, TN, preferred_element_type=jnp.float32)  1.94 us
    dot_general x1, matrix products, shards(): lax.dot_general(got, peer_spins, TN, preferred_element_type=jnp.float32)  1.54 us
    ppermute x1, starting transfers between devices, shards(): other = lax.ppermute(residual, 'resp', ring)  1.52 us
  transfers between devices with their start and end apart: 22, of which 12 were waited for; matrix products, arithmetic and copies ran while one was open for 9% of the time, Pallas kernels for 0%

profile of v3, /device:TPU:0, one launch (start us, length us, event | category | flops | bytes accessed | tf_op | source)
XLA Modules:
  0.0 75.5 jit_solution(6242225007349030417)
XLA Ops:
  0.0 1.5 %copy.6 = bf16[1,256,2048]{1,2,0:T(8,128)(2,1)S(1)} copy(bf16[1,256,2048]{2,1,0:T(8,128)(2,1)} %param.5) | data formatting | bytes 2097152 | tf_op args[0]
  1.5 0.1 constant_dynamic-slice_fusion.1
  1.6 0.5 collective-permute-start
  2.1 1.9 %fusion.15 = bf16[256,512]{1,0:T(8,128)(2,1)S(1)} fusion(s32[512]{0:T(512)S(1)} %copy-done.5, s32[1024,256]{1,0:T(8,128)} %param.8), kind=kOutput, calls=%fused_computation.21 | convolution fusion | flops 269877248 | bytes 1312768 | tf_op jit(solution)/shard_map/dot_general | solution.py:54
  4.1 0.1 collective-permute-start.1
  4.2 0.4 fusion.46
  4.6 1.0 %collective-permute-done.1 = bf16[256,512]{1,0:T(8,128)(2,1)S(1)} collective-permute-done((bf16[256,512]{1,0:T(8,128)(2,1)S(1)}, bf16[256,512]{1,0:T(8,128)(2,1)S(1)}, u32[]{:S(2)}, u32[]{:S(2)}) %collective-permute-start.1) | collective-permute-done | bytes 262176 | tf_op jit(solution)/shard_map/ppermute | solution.py:32
  5.7 0.7 copy-done.2
  6.4 1.5 %convolution_add_fusion = f32[1024,512]{1,0:T(8,128)S(1)} fusion(f32[1024,512]{1,0:T(8,128)S(1)} %fusion.46, bf16[256,1024]{0,1:T(8,128)(2,1)} %collective-permute-done, bf16[256,512]{1,0:T(8,128)(2,1)} %copy-done.2), kind=kOutput, calls=%fused_computation.2 | convolution fusion | flops 268959744 | bytes 4980736 | tf_op jit(solution)/shard_map/dot_general | solution.py:61
  7.9 0.9 %dynamic-slice_convert_fusion = bf16[4,1,128,512]{3,2,1,0:T(8,128)(2,1)} fusion(f32[4,2,128,512]{3,2,1,0:T(8,128)S(1)} %bitcast.117, s32[]{:T(128)S(6)} %select_n.147), kind=kLoop, calls=%fused_computation.24 | loop fusion | bytes 1048580 | tf_op jit(solution)/shard_map/convert_element_type | solution.py:63
  8.8 2.6 %collective-permute-start.2 = (bf16[512,512]{1,0:T(8,128)(2,1)}, bf16[512,512]{1,0:T(8,128)(2,1)}, u32[]{:S(2)}, u32[]{:S(2)}) collective-permute-start(bf16[512,512]{1,0:T(8,128)(2,1)} %bitcast.6), channel_id=1, source_target_pairs={{0,2},{1,3},{2,0},{3,1},{4,6},{5,7},{6,4},{7,5},{8,10},{9,11},{10,... | collective-permute-start | bytes 1572872 | tf_op jit(solution)/shard_map/ppermute | solution.py:32
  11.4 1.6 %collective-permute-start.3 = (bf16[128,512]{1,0:T(8,128)(2,1)S(1)}, bf16[128,512]{1,0:T(8,128)(2,1)}, u32[]{:S(2)}, u32[]{:S(2)}) collective-permute-start(bf16[128,512]{1,0:T(8,128)(2,1)S(1)} %constant_dynamic-slice_fusion.3), channel_id=1, source_target_pairs={{0,4},{1,5},{2,6},{3,7},{4,0},{5,1},{6,2},{7,3},{8,12},{9,13},{10,... | collective-permute-start | bytes 393224 | tf_op jit(solution)/shard_map/ppermute | solution.py:32
  13.1 2.6 %collective-permute-start.4 = (bf16[128,512]{1,0:T(8,128)(2,1)S(1)}, bf16[128,512]{1,0:T(8,128)(2,1)}, u32[]{:S(2)}, u32[]{:S(2)}) collective-permute-start(bf16[128,512]{1,0:T(8,128)(2,1)S(1)} %constant_dynamic-slice_fusion.3), channel_id=1, source_target_pairs={{0,8},{1,9},{2,10},{3,11},{4,12},{5,13},{6,14},{7,15},{8,0},{9,1},... | collective-permute-start | bytes 393224 | tf_op jit(solution)/shard_map/ppermute | solution.py:32
  15.7 0.2 collective-permute-start.5
  15.9 0.1 fusion.40
  16.0 0.1 constant_dynamic-slice_fusion
  16.1 2.8 %collective-permute-done.3 = bf16[128,512]{1,0:T(8,128)(2,1)} collective-permute-done((bf16[128,512]{1,0:T(8,128)(2,1)S(1)}, bf16[128,512]{1,0:T(8,128)(2,1)}, u32[]{:S(2)}, u32[]{:S(2)}) %collective-permute-start.3) | collective-permute-done | bytes 131104 | tf_op jit(solution)/shard_map/ppermute | solution.py:32
  19.0 7.1 %collective-permute-done.4 = bf16[128,512]{1,0:T(8,128)(2,1)} collective-permute-done((bf16[128,512]{1,0:T(8,128)(2,1)S(1)}, bf16[128,512]{1,0:T(8,128)(2,1)}, u32[]{:S(2)}, u32[]{:S(2)}) %collective-permute-start.4) | collective-permute-done | bytes 131104 | tf_op jit(solution)/shard_map/ppermute | solution.py:32
  26.1 0.9 %constant_dynamic-update-slice_fusion.12 = bf16[512,512]{1,0:T(8,128)(2,1)S(1)} fusion(bf16[512,512]{1,0:T(8,128)(2,1)S(1)} %constant_dynamic-update-slice_fusion.13, bf16[128,512]{1,0:T(8,128)(2,1)} %collective-permute-done.3), kind=kLoop, calls=%fused_computation.102 | loop fusion | bytes 262144
  27.0 0.9 %constant_dynamic-update-slice_fusion.11 = bf16[512,512]{1,0:T(8,128)(2,1)S(1)} fusion(bf16[512,512]{1,0:T(8,128)(2,1)S(1)} %constant_dynamic-update-slice_fusion.12, bf16[128,512]{1,0:T(8,128)(2,1)} %collective-permute-done.4), kind=kLoop, calls=%fused_computation.101 | loop fusion | bytes 262144
  28.0 0.9 %constant_dynamic-update-slice_fusion.10 = bf16[512,512]{1,0:T(8,128)(2,1)S(1)} fusion(bf16[512,512]{1,0:T(8,128)(2,1)S(1)} %constant_dynamic-update-slice_fusion.11, bf16[128,512]{1,0:T(8,128)(2,1)} %collective-permute-done.5), kind=kLoop, calls=%fused_computation.100 | loop fusion | bytes 262144 | tf_op jit(solution)/shard_map/concatenate | solution.py:71
  28.9 0.1 collective-permute-start.10
  28.9 0.6 collective-permute-start.9
  29.6 1.2 %bitcast_add_fusion = f32[512,512]{1,0:T(8,128)S(1)} fusion(f32[4,1,128,512]{3,2,1,0:T(8,128)S(1)} %constant_dynamic-slice_fusion, bf16[512,512]{1,0:T(8,128)(2,1)} %collective-permute-done.2), kind=kLoop, calls=%fused_computation.22 | loop fusion | flops 524288 | bytes 2621440 | tf_op jit(solution)/shard_map/add | solution.py:66
  30.8 0.1 fusion.35
  30.9 2.3 %collective-permute-start.6 = (bf16[128,512]{1,0:T(8,128)(2,1)S(1)}, bf16[128,512]{1,0:T(8,128)(2,1)S(1)}, u32[]{:S(2)}, u32[]{:S(2)}) collective-permute-start(bf16[128,512]{1,0:T(8,128)(2,1)S(1)} %get-tuple-element.29), channel_id=1, source_target_pairs={{0,4},{1,5},{2,6},{3,7},{4,0},{5,1},{6,2},{7,3},{8,12},{9,13},{10,... | collective-permute-start | bytes 393224 | tf_op jit(solution)/shard_map/ppermute | solution.py:32
  33.2 1.2 %collective-permute-start.7 = (bf16[128,512]{1,0:T(8,128)(2,1)S(1)}, bf16[128,512]{1,0:T(8,128)(2,1)S(1)}, u32[]{:S(2)}, u32[]{:S(2)}) collective-permute-start(bf16[128,512]{1,0:T(8,128)(2,1)S(1)} %get-tuple-element.28), channel_id=1, source_target_pairs={{0,8},{1,9},{2,10},{3,11},{4,12},{5,13},{6,14},{7,15},{8,0},{9,1},... | collective-permute-start | bytes 393224 | tf_op jit(solution)/shard_map/ppermute | solution.py:32
  34.4 1.2 %collective-permute-start.8 = (bf16[128,512]{1,0:T(8,128)(2,1)S(1)}, bf16[128,512]{1,0:T(8,128)(2,1)S(1)}, u32[]{:S(2)}, u32[]{:S(2)}) collective-permute-start(bf16[128,512]{1,0:T(8,128)(2,1)S(1)} %get-tuple-element.27), channel_id=1, source_target_pairs={{0,12},{1,13},{2,14},{3,15},{4,8},{5,9},{6,10},{7,11},{8,4},{9,5},... | collective-permute-start | bytes 393224 | tf_op jit(solution)/shard_map/ppermute | solution.py:32
  35.7 0.1 broadcast.46.clone.1
  35.7 0.9 %bitcast_dynamic-update-slice_fusion.5 = bf16[8,128,512]{2,1,0:T(8,128)(2,1)S(1)} fusion(bf16[8,128,512]{2,1,0:T(8,128)(2,1)S(1)} %broadcast.46.clone.1, s32[]{:T(128)S(6)} %select_n.157, bf16[128,512]{1,0:T(8,128)(2,1)} %collective-permute-done.4), kind=kLoop, calls=%fused_computation.76 | loop fusion | bytes 262148 | tf_op jit(solution)/shard_map/jit(dynamic_update_index_in_dim)/dynamic_update_slice | solution.py:42
  36.7 0.1 broadcast.46.clone.2
  36.8 2.1 %collective-permute-done.6 = bf16[128,512]{1,0:T(8,128)(2,1)S(1)} collective-permute-done((bf16[128,512]{1,0:T(8,128)(2,1)S(1)}, bf16[128,512]{1,0:T(8,128)(2,1)S(1)}, u32[]{:S(2)}, u32[]{:S(2)}) %collective-permute-start.6) | collective-permute-done | bytes 131104 | tf_op jit(solution)/shard_map/ppermute | solution.py:32
  38.9 7.2 %collective-permute-done.7 = bf16[128,512]{1,0:T(8,128)(2,1)S(1)} collective-permute-done((bf16[128,512]{1,0:T(8,128)(2,1)S(1)}, bf16[128,512]{1,0:T(8,128)(2,1)S(1)}, u32[]{:S(2)}, u32[]{:S(2)}) %collective-permute-start.7) | collective-permute-done | bytes 131104 | tf_op jit(solution)/shard_map/ppermute | solution.py:32
  46.1 0.1 broadcast.46.clone
  46.2 0.2 constant_dynamic-update-slice_fusion.7
  46.4 3.4 %collective-permute-start.17 = (bf16[128,512]{1,0:T(8,128)(2,1)S(1)}, bf16[128,512]{1,0:T(8,128)(2,1)S(1)}, u32[]{:S(2)}, u32[]{:S(2)}) collective-permute-start(bf16[128,512]{1,0:T(8,128)(2,1)S(1)} %get-tuple-element.26), channel_id=1, source_target_pairs={{0,8},{1,9},{2,10},{3,11},{4,12},{5,13},{6,14},{7,15},{8,0},{9,1},... | collective-permute-start | bytes 393224 | tf_op jit(solution)/shard_map/ppermute | solution.py:32
  49.8 1.5 %collective-permute-start.11 = (bf16[128,512]{1,0:T(8,128)(2,1)S(1)}, bf16[128,512]{1,0:T(8,128)(2,1)S(1)}, u32[]{:S(2)}, u32[]{:S(2)}) collective-permute-start(bf16[128,512]{1,0:T(8,128)(2,1)S(1)} %get-tuple-element.26), channel_id=1, source_target_pairs={{0,16},{16,0},{1,17},{17,1},{2,18},{18,2},{3,19},{19,3},{4,20},{20... | collective-permute-start | bytes 393224 | tf_op jit(solution)/shard_map/ppermute | solution.py:94
  51.3 1.5 %collective-permute-start.13 = (bf16[128,512]{1,0:T(8,128)(2,1)S(1)}, bf16[128,512]{1,0:T(8,128)(2,1)S(1)}, u32[]{:S(2)}, u32[]{:S(2)}) collective-permute-start(bf16[128,512]{1,0:T(8,128)(2,1)S(1)} %get-tuple-element.26), channel_id=1, source_target_pairs={{0,2},{1,3},{2,0},{3,1},{4,6},{5,7},{6,4},{7,5},{8,10},{9,11},{10,... | collective-permute-start | bytes 393224 | tf_op jit(solution)/shard_map/ppermute | solution.py:32
  52.9 2.7 %collective-permute-done.17 = bf16[128,512]{1,0:T(8,128)(2,1)S(1)} collective-permute-done((bf16[128,512]{1,0:T(8,128)(2,1)S(1)}, bf16[128,512]{1,0:T(8,128)(2,1)S(1)}, u32[]{:S(2)}, u32[]{:S(2)}) %collective-permute-start.17) | collective-permute-done | bytes 131104 | tf_op jit(solution)/shard_map/ppermute | solution.py:32
  55.5 1.3 %collective-permute-start.15 = (bf16[128,512]{1,0:T(8,128)(2,1)S(1)}, bf16[128,512]{1,0:T(8,128)(2,1)S(1)}, u32[]{:S(2)}, u32[]{:S(2)}) collective-permute-start(bf16[128,512]{1,0:T(8,128)(2,1)S(1)} %get-tuple-element.26), channel_id=1, source_target_pairs={{0,6},{1,7},{2,4},{3,5},{4,2},{5,3},{6,0},{7,1},{8,14},{9,15},{10,... | collective-permute-start | bytes 393224 | tf_op jit(solution)/shard_map/ppermute | solution.py:32
  56.9 0.1 broadcast.46.clone.3
  57.0 0.7 collective-permute-start.18
  57.7 1.1 %collective-permute-done.14 = bf16[128,512]{1,0:T(8,128)(2,1)S(1)} collective-permute-done((bf16[128,512]{1,0:T(8,128)(2,1)S(1)}, bf16[128,512]{1,0:T(8,128)(2,1)S(1)}, u32[]{:S(2)}, u32[]{:S(2)}) %collective-permute-start.14) | collective-permute-done | bytes 131104 | tf_op jit(solution)/shard_map/ppermute | solution.py:32
  58.9 0.4 collective-permute-start.19
  59.2 2.9 %collective-permute-done.15 = bf16[128,512]{1,0:T(8,128)(2,1)S(1)} collective-permute-done((bf16[128,512]{1,0:T(8,128)(2,1)S(1)}, bf16[128,512]{1,0:T(8,128)(2,1)S(1)}, u32[]{:S(2)}, u32[]{:S(2)}) %collective-permute-start.15) | collective-permute-done | bytes 131104 | tf_op jit(solution)/shard_map/ppermute | solution.py:32
  62.2 1.3 %collective-permute-start.20 = (bf16[128,512]{1,0:T(8,128)(2,1)S(1)}, bf16[128,512]{1,0:T(8,128)(2,1)S(1)}, u32[]{:S(2)}, u32[]{:S(2)}) collective-permute-start(bf16[128,512]{1,0:T(8,128)(2,1)S(1)} %collective-permute-done.17), channel_id=1, source_target_pairs={{0,6},{1,7},{2,4},{3,5},{4,2},{5,3},{6,0},{7,1},{8,14},{9,15},{10,... | collective-permute-start | bytes 393224 | tf_op jit(solution)/shard_map/ppermute | solution.py:32
  63.4 0.1 pad_maximum_fusion
  63.5 0.1 collective-permute-start.16
  63.6 0.5 collective-permute-done.18
  64.1 1.0 %collective-permute-done.19 = bf16[128,512]{1,0:T(8,128)(2,1)S(1)} collective-permute-done((bf16[128,512]{1,0:T(8,128)(2,1)S(1)}, bf16[128,512]{1,0:T(8,128)(2,1)S(1)}, u32[]{:S(2)}, u32[]{:S(2)}) %collective-permute-start.19) | collective-permute-done | bytes 131104 | tf_op jit(solution)/shard_map/ppermute | solution.py:32
  65.1 3.0 %collective-permute-done.20 = bf16[128,512]{1,0:T(8,128)(2,1)S(1)} collective-permute-done((bf16[128,512]{1,0:T(8,128)(2,1)S(1)}, bf16[128,512]{1,0:T(8,128)(2,1)S(1)}, u32[]{:S(2)}, u32[]{:S(2)}) %collective-permute-start.20) | collective-permute-done | bytes 131104 | tf_op jit(solution)/shard_map/ppermute | solution.py:32
  68.0 0.1 pad_maximum_fusion.1
  68.1 0.1 collective-permute-start.21
  68.2 0.9 %bitcast_dynamic-update-slice_fusion.2 = bf16[8,128,512]{2,1,0:T(8,128)(2,1)S(1)} fusion(bf16[8,128,512]{2,1,0:T(8,128)(2,1)S(1)} %fusion.37, s32[]{:T(128)S(6)} %select_n.161, bf16[128,512]{1,0:T(8,128)(2,1)} %collective-permute-done.5), kind=kLoop, calls=%fused_computation.73 | loop fusion | bytes 262148 | tf_op jit(solution)/shard_map/jit(dynamic_update_index_in_dim)/dynamic_update_slice | solution.py:42
  69.4 0.5 fusion.11
  69.9 0.2 collective-permute-done.21
  70.2 0.4 copy-done.4
  70.6 0.6 fusion.5
  71.2 0.9 %bitcast_dynamic-update-slice_fusion.8 = bf16[8,128,512]{2,1,0:T(8,128)(2,1)S(1)} fusion(bf16[8,128,512]{2,1,0:T(8,128)(2,1)S(1)} %get-tuple-element.33, s32[]{:T(128)S(6)} %select_n.161, bf16[128,512]{1,0:T(8,128)(2,1)} %collective-permute-done.3), kind=kLoop, calls=%fused_computation.79 | loop fusion | bytes 262148 | tf_op jit(solution)/shard_map/jit(dynamic_update_index_in_dim)/dynamic_update_slice | solution.py:42
  72.2 0.7 fusion.10
  72.9 0.1 broadcast_in_dim.91
  73.0 0.2 fusion.18
  73.3 0.9 %copy-done.1 = bf16[1,256,2048]{2,1,0:T(8,128)(2,1)} copy-done((bf16[1,256,2048]{2,1,0:T(8,128)(2,1)}, bf16[1,256,2048]{2,1,0:T(8,128)(2,1)S(1)}, u32[]{:S(2)}) %copy-start.1) | copy-done | bytes 1048600
  74.2 1.3 %fusion.14 = bf16[1,256,2048]{2,1,0:T(8,128)(2,1)} fusion(bf16[1,256,2048]{2,1,0:T(8,128)(2,1)} %copy-done.1, s32[]{:T(128)S(6)} %select_n.167, f32[256,1024]{1,0:T(8,128)S(1)} %fusion.5, bf16[256,512]{1,0:T(8,128)(2,1)S(1)} %fusion.15, bf16[1024,512]{1,0:T(8,128)(2,1)S(1)} %bitcast.119), kind=kOutput, calls=%fused_computation.20 | convolution fusion | flops 269221888 | bytes 2883588 | tf_op jit(solution)/shard_map/dot_general | solution.py:103
  (53 shorter events, 0.6 us)
Async XLA Ops:
  0.0 2.1 %copy-start.5 = (s32[512]{0:T(512)S(1)}, s32[512]{0:T(512)}, u32[]{:S(2)}) copy-start(s32[512]{0:T(512)} %param.9) | copy-start | bytes 6148
  1.6 4.8 %collective-permute-start = (bf16[256,1024]{0,1:T(8,128)(2,1)S(1)}, bf16[256,1024]{0,1:T(8,128)(2,1)}, u32[]{:S(2)}, u32[]{:S(2)}) collective-permute-start(bf16[256,1024]{0,1:T(8,128)(2,1)S(1)} %bitcast.128), channel_id=1, source_target_pairs={{0,1},{1,0},{2,3},{3,2},{4,5},{5,4},{6,7},{7,6},{8,9},{9,8},{10,11... | collective-permute-start | bytes 1572872 | tf_op jit(solution)/shard_map/ppermute | solution.py:32
  4.1 1.6 %collective-permute-start.1 = (bf16[256,512]{1,0:T(8,128)(2,1)S(1)}, bf16[256,512]{1,0:T(8,128)(2,1)S(1)}, u32[]{:S(2)}, u32[]{:S(2)}) collective-permute-start(bf16[256,512]{1,0:T(8,128)(2,1)S(1)} %fusion.15), channel_id=1, source_target_pairs={{0,1},{1,0},{2,3},{3,2},{4,5},{5,4},{6,7},{7,6},{8,9},{9,8},{10,11... | collective-permute-start | bytes 786440 | tf_op jit(solution)/shard_map/ppermute | solution.py:32
  4.6 11.3 %copy-start = (bf16[1,256,2048]{2,1,0:T(8,128)(2,1)S(1)}, bf16[1,256,2048]{2,1,0:T(8,128)(2,1)}, u32[]{:S(2)}) copy-start(bf16[1,256,2048]{2,1,0:T(8,128)(2,1)} %param.5) | copy-start | bytes 3145732
  5.7 0.7 copy-start.2
  8.8 17.3 %collective-permute-start.2 = (bf16[512,512]{1,0:T(8,128)(2,1)}, bf16[512,512]{1,0:T(8,128)(2,1)}, u32[]{:S(2)}, u32[]{:S(2)}) collective-permute-start(bf16[512,512]{1,0:T(8,128)(2,1)} %bitcast.6), channel_id=1, source_target_pairs={{0,2},{1,3},{2,0},{3,1},{4,6},{5,7},{6,4},{7,5},{8,10},{9,11},{10,... | collective-permute-start | bytes 1572872 | tf_op jit(solution)/shard_map/ppermute | solution.py:32
  11.4 7.5 %collective-permute-start.3 = (bf16[128,512]{1,0:T(8,128)(2,1)S(1)}, bf16[128,512]{1,0:T(8,128)(2,1)}, u32[]{:S(2)}, u32[]{:S(2)}) collective-permute-start(bf16[128,512]{1,0:T(8,128)(2,1)S(1)} %constant_dynamic-slice_fusion.3), channel_id=1, source_target_pairs={{0,4},{1,5},{2,6},{3,7},{4,0},{5,1},{6,2},{7,3},{8,12},{9,13},{10,... | collective-permute-start | bytes 393224 | tf_op jit(solution)/shard_map/ppermute | solution.py:32
  13.1 13.0 %collective-permute-start.4 = (bf16[128,512]{1,0:T(8,128)(2,1)S(1)}, bf16[128,512]{1,0:T(8,128)(2,1)}, u32[]{:S(2)}, u32[]{:S(2)}) collective-permute-start(bf16[128,512]{1,0:T(8,128)(2,1)S(1)} %constant_dynamic-slice_fusion.3), channel_id=1, source_target_pairs={{0,8},{1,9},{2,10},{3,11},{4,12},{5,13},{6,14},{7,15},{8,0},{9,1},... | collective-permute-start | bytes 393224 | tf_op jit(solution)/shard_map/ppermute | solution.py:32
  15.7 10.4 %collective-permute-start.5 = (bf16[128,512]{1,0:T(8,128)(2,1)S(1)}, bf16[128,512]{1,0:T(8,128)(2,1)}, u32[]{:S(2)}, u32[]{:S(2)}) collective-permute-start(bf16[128,512]{1,0:T(8,128)(2,1)S(1)} %constant_dynamic-slice_fusion.3), channel_id=1, source_target_pairs={{0,12},{1,13},{2,14},{3,15},{4,8},{5,9},{6,10},{7,11},{8,4},{9,5},... | collective-permute-start | bytes 393224 | tf_op jit(solution)/shard_map/ppermute | solution.py:32
  28.9 17.2 %collective-permute-start.10 = (bf16[512,512]{1,0:T(8,128)(2,1)S(1)}, bf16[512,512]{1,0:T(8,128)(2,1)S(1)}, u32[]{:S(2)}, u32[]{:S(2)}) collective-permute-start(bf16[512,512]{1,0:T(8,128)(2,1)S(1)} %constant_dynamic-update-slice_fusion.10), channel_id=1, source_target_pairs={{0,1},{1,0},{2,3},{3,2},{4,5},{5,4},{6,7},{7,6},{8,9},{9,8},{10,11... | collective-permute-start | bytes 1572872 | tf_op jit(solution)/shard_map/ppermute | solution.py:32
  28.9 17.1 %collective-permute-start.9 = (bf16[512,512]{1,0:T(8,128)(2,1)S(1)}, bf16[512,512]{1,0:T(8,128)(2,1)S(1)}, u32[]{:S(2)}, u32[]{:S(2)}) collective-permute-start(bf16[512,512]{1,0:T(8,128)(2,1)S(1)} %constant_dynamic-update-slice_fusion.10), channel_id=1, source_target_pairs={{0,2},{1,3},{2,0},{3,1},{4,6},{5,7},{6,4},{7,5},{8,10},{9,11},{10,... | collective-permute-start | bytes 1572872 | tf_op jit(solution)/shard_map/ppermute | solution.py:32
  30.8 15.4 %copy-start.3 = (f32[1,128]{1,0:T(1,128)S(1)}, f32[1,128]{1,0:T(1,128)}, u32[]{:S(2)}) copy-start(f32[1,128]{1,0:T(1,128)} %param.7) | copy-start | bytes 1540
  30.9 8.0 %collective-permute-start.6 = (bf16[128,512]{1,0:T(8,128)(2,1)S(1)}, bf16[128,512]{1,0:T(8,128)(2,1)S(1)}, u32[]{:S(2)}, u32[]{:S(2)}) collective-permute-start(bf16[128,512]{1,0:T(8,128)(2,1)S(1)} %get-tuple-element.29), channel_id=1, source_target_pairs={{0,4},{1,5},{2,6},{3,7},{4,0},{5,1},{6,2},{7,3},{8,12},{9,13},{10,... | collective-permute-start | bytes 393224 | tf_op jit(solution)/shard_map/ppermute | solution.py:32
  33.2 12.9 %collective-permute-start.7 = (bf16[128,512]{1,0:T(8,128)(2,1)S(1)}, bf16[128,512]{1,0:T(8,128)(2,1)S(1)}, u32[]{:S(2)}, u32[]{:S(2)}) collective-permute-start(bf16[128,512]{1,0:T(8,128)(2,1)S(1)} %get-tuple-element.28), channel_id=1, source_target_pairs={{0,8},{1,9},{2,10},{3,11},{4,12},{5,13},{6,14},{7,15},{8,0},{9,1},... | collective-permute-start | bytes 393224 | tf_op jit(solution)/shard_map/ppermute | solution.py:32
  34.4 11.7 %collective-permute-start.8 = (bf16[128,512]{1,0:T(8,128)(2,1)S(1)}, bf16[128,512]{1,0:T(8,128)(2,1)S(1)}, u32[]{:S(2)}, u32[]{:S(2)}) collective-permute-start(bf16[128,512]{1,0:T(8,128)(2,1)S(1)} %get-tuple-element.27), channel_id=1, source_target_pairs={{0,12},{1,13},{2,14},{3,15},{4,8},{5,9},{6,10},{7,11},{8,4},{9,5},... | collective-permute-start | bytes 393224 | tf_op jit(solution)/shard_map/ppermute | solution.py:32
  46.4 9.1 %collective-permute-start.17 = (bf16[128,512]{1,0:T(8,128)(2,1)S(1)}, bf16[128,512]{1,0:T(8,128)(2,1)S(1)}, u32[]{:S(2)}, u32[]{:S(2)}) collective-permute-start(bf16[128,512]{1,0:T(8,128)(2,1)S(1)} %get-tuple-element.26), channel_id=1, source_target_pairs={{0,8},{1,9},{2,10},{3,11},{4,12},{5,13},{6,14},{7,15},{8,0},{9,1},... | collective-permute-start | bytes 393224 | tf_op jit(solution)/shard_map/ppermute | solution.py:32
  49.8 13.7 %collective-permute-start.11 = (bf16[128,512]{1,0:T(8,128)(2,1)S(1)}, bf16[128,512]{1,0:T(8,128)(2,1)S(1)}, u32[]{:S(2)}, u32[]{:S(2)}) collective-permute-start(bf16[128,512]{1,0:T(8,128)(2,1)S(1)} %get-tuple-element.26), channel_id=1, source_target_pairs={{0,16},{16,0},{1,17},{17,1},{2,18},{18,2},{3,19},{19,3},{4,20},{20... | collective-permute-start | bytes 393224 | tf_op jit(solution)/shard_map/ppermute | solution.py:94
  51.3 5.7 %collective-permute-start.13 = (bf16[128,512]{1,0:T(8,128)(2,1)S(1)}, bf16[128,512]{1,0:T(8,128)(2,1)S(1)}, u32[]{:S(2)}, u32[]{:S(2)}) collective-permute-start(bf16[128,512]{1,0:T(8,128)(2,1)S(1)} %get-tuple-element.26), channel_id=1, source_target_pairs={{0,2},{1,3},{2,0},{3,1},{4,6},{5,7},{6,4},{7,5},{8,10},{9,11},{10,... | collective-permute-start | bytes 393224 | tf_op jit(solution)/shard_map/ppermute | solution.py:32
  52.8 6.1 %collective-permute-start.14 = (bf16[128,512]{1,0:T(8,128)(2,1)S(1)}, bf16[128,512]{1,0:T(8,128)(2,1)S(1)}, u32[]{:S(2)}, u32[]{:S(2)}) collective-permute-start(bf16[128,512]{1,0:T(8,128)(2,1)S(1)} %get-tuple-element.26), channel_id=1, source_target_pairs={{0,4},{1,5},{2,6},{3,7},{4,0},{5,1},{6,2},{7,3},{8,12},{9,13},{10,... | collective-permute-start | bytes 393224 | tf_op jit(solution)/shard_map/ppermute | solution.py:32
  52.8 15.4 %collective-permute-start.12 = (bf16[512,512]{1,0:T(8,128)(2,1)S(1)}, bf16[512,512]{1,0:T(8,128)(2,1)S(1)}, u32[]{:S(2)}, u32[]{:S(2)}) collective-permute-start(bf16[512,512]{1,0:T(8,128)(2,1)S(1)} %collective-permute-done.9), channel_id=1, source_target_pairs={{0,1},{1,0},{2,3},{3,2},{4,5},{5,4},{6,7},{7,6},{8,9},{9,8},{10,11... | collective-permute-start | bytes 1572872 | tf_op jit(solution)/shard_map/ppermute | solution.py:32
  55.5 6.6 %collective-permute-start.15 = (bf16[128,512]{1,0:T(8,128)(2,1)S(1)}, bf16[128,512]{1,0:T(8,128)(2,1)S(1)}, u32[]{:S(2)}, u32[]{:S(2)}) collective-permute-start(bf16[128,512]{1,0:T(8,128)(2,1)S(1)} %get-tuple-element.26), channel_id=1, source_target_pairs={{0,6},{1,7},{2,4},{3,5},{4,2},{5,3},{6,0},{7,1},{8,14},{9,15},{10,... | collective-permute-start | bytes 393224 | tf_op jit(solution)/shard_map/ppermute | solution.py:32
  57.0 7.1 %collective-permute-start.18 = (bf16[128,512]{1,0:T(8,128)(2,1)S(1)}, bf16[128,512]{1,0:T(8,128)(2,1)S(1)}, u32[]{:S(2)}, u32[]{:S(2)}) collective-permute-start(bf16[128,512]{1,0:T(8,128)(2,1)S(1)} %collective-permute-done.17), channel_id=1, source_target_pairs={{0,2},{1,3},{2,0},{3,1},{4,6},{5,7},{6,4},{7,5},{8,10},{9,11},{10,... | collective-permute-start | bytes 393224 | tf_op jit(solution)/shard_map/ppermute | solution.py:32
  58.9 6.2 %collective-permute-start.19 = (bf16[128,512]{1,0:T(8,128)(2,1)S(1)}, bf16[128,512]{1,0:T(8,128)(2,1)S(1)}, u32[]{:S(2)}, u32[]{:S(2)}) collective-permute-start(bf16[128,512]{1,0:T(8,128)(2,1)S(1)} %collective-permute-done.17), channel_id=1, source_target_pairs={{0,4},{1,5},{2,6},{3,7},{4,0},{5,1},{6,2},{7,3},{8,12},{9,13},{10,... | collective-permute-start | bytes 393224 | tf_op jit(solution)/shard_map/ppermute | solution.py:32
  62.2 5.9 %collective-permute-start.20 = (bf16[128,512]{1,0:T(8,128)(2,1)S(1)}, bf16[128,512]{1,0:T(8,128)(2,1)S(1)}, u32[]{:S(2)}, u32[]{:S(2)}) collective-permute-start(bf16[128,512]{1,0:T(8,128)(2,1)S(1)} %collective-permute-done.17), channel_id=1, source_target_pairs={{0,6},{1,7},{2,4},{3,5},{4,2},{5,3},{6,0},{7,1},{8,14},{9,15},{10,... | collective-permute-start | bytes 393224 | tf_op jit(solution)/shard_map/ppermute | solution.py:32
  63.5 5.7 %collective-permute-start.16 = (bf16[4,128,512]{2,1,0:T(8,128)(2,1)S(1)}, bf16[4,128,512]{2,1,0:T(8,128)(2,1)S(1)}, u32[]{:S(2)}, u32[]{:S(2)}) collective-permute-start(bf16[4,128,512]{2,1,0:T(8,128)(2,1)S(1)} %pad_maximum_fusion), channel_id=1, source_target_pairs={{0,1},{1,0},{2,3},{3,2},{4,5},{5,4},{6,7},{7,6},{8,9},{9,8},{10,11... | collective-permute-start | bytes 1572872 | tf_op jit(solution)/shard_map/ppermute | solution.py:32
  68.1 2.0 %collective-permute-start.21 = (bf16[4,128,512]{2,1,0:T(8,128)(2,1)S(1)}, bf16[4,128,512]{2,1,0:T(8,128)(2,1)S(1)}, u32[]{:S(2)}, u32[]{:S(2)}) collective-permute-start(bf16[4,128,512]{2,1,0:T(8,128)(2,1)S(1)} %pad_maximum_fusion.1), channel_id=1, source_target_pairs={{0,1},{1,0},{2,3},{3,2},{4,5},{5,4},{6,7},{7,6},{8,9},{9,8},{10,11... | collective-permute-start | bytes 1572872 | tf_op jit(solution)/shard_map/ppermute | solution.py:32
  69.4 1.2 %copy-start.4 = (bf16[1,256,2048]{2,1,0:T(8,128)(2,1)S(1)}, bf16[1,256,2048]{2,1,0:T(8,128)(2,1)}, u32[]{:S(2)}) copy-start(bf16[1,256,2048]{2,1,0:T(8,128)(2,1)} %param.6) | copy-start | bytes 3145732
  73.2 1.0 %copy-start.1 = (bf16[1,256,2048]{2,1,0:T(8,128)(2,1)}, bf16[1,256,2048]{2,1,0:T(8,128)(2,1)S(1)}, u32[]{:S(2)}) copy-start(bf16[1,256,2048]{2,1,0:T(8,128)(2,1)S(1)} %fusion.18) | copy-start | bytes 3145732

commit v4 on v3

v4 whole, which is shorter than its diff:
```python
import math

import jax
import jax.numpy as jnp
from jax import lax
from jax.sharding import PartitionSpec as P

DRIFT = 0.01
DATA_RATIO = 900.0
NOISE_SCALE = math.sqrt(0.02)
NT = (((1,), (1,)), ((), ()))
TN = (((0,), (0,)), ((), ()))


def shards(coupling, noise, bias, responses, indices):
    couple = coupling[0]
    item_dev = couple.shape[0]
    pool, batch = responses.shape[0], indices.shape[0]
    n_resp = lax.axis_size("resp")
    n_item = lax.axis_size("item")
    sub_len = item_dev // n_resp
    n_line = n_item // 4
    width = 8 * sub_len
    n_high = n_item // 8
    inv_root = 1.0 / math.sqrt(item_dev * n_item)
    resp_idx = lax.axis_index("resp")
    item_idx = lax.axis_index("item")

    core_idx, near_idx, line_idx, high_idx = item_idx % 2, item_idx // 2 % 2, item_idx // 4, item_idx // 8
    where = dict(
        core=core_idx,
        other_core=1 - core_idx,
        near=near_idx,
        other_near=1 - near_idx,
        line=[line_idx ^ step for step in range(n_line)],
        quad=[item_idx // 2 % 4 ^ step for step in range(4)],
        high=[high_idx ^ step for step in range(n_high)],
        is_high=[[high_idx ^ step == block for block in range(n_high)] for step in range(n_high)],
        source=[(resp_idx - step) % n_resp for step in range(n_resp)],
        own_start=resp_idx * sub_len,
        item_col=item_idx * sub_len,
        low_col=item_idx % 8 * sub_len,
    )
    indices, where = lax.optimization_barrier((indices, where))
    own_start = where["own_start"]

    def swap(array, bits):
        return lax.ppermute(array, "item", [(i, i ^ bits) for i in range(n_item)])

    def take(array, index, axis):
        return lax.dynamic_index_in_dim(array, index, axis, False, allow_negative_indices=False)

    def put_at(array, part, *starts):
        starts = starts + (0,) * (array.ndim - len(starts))
        return lax.dynamic_update_slice(array, part, starts, allow_negative_indices=False)

    by_core = couple.reshape(item_dev, -1, 2, sub_len)
    kept = take(by_core, where["core"], 2).reshape(item_dev, -1)
    given = take(by_core, where["other_core"], 2).reshape(item_dev, -1)
    got = swap(given, 1)

    pool_ids = lax.broadcasted_iota(jnp.int32, (pool, batch), 0)
    picks = (pool_ids == indices[None]).astype(jnp.bfloat16)
    pool_spins = (2 * responses - 1).astype(jnp.bfloat16)
    spins = lax.dot_general(pool_spins, picks, TN, preferred_element_type=jnp.float32)
    spins = spins.astype(jnp.bfloat16)
    peer_spins = swap(spins, 1)
    own_spins = take(spins.reshape(n_resp, sub_len, batch), where["source"][0], 0)

    partial = lax.dot_general(
        kept, spins, TN, preferred_element_type=jnp.float32
    ) + lax.dot_general(got, peer_spins, TN, preferred_element_type=jnp.float32)

    by_near = partial.reshape(n_line, 2, sub_len, batch)
    sent = take(by_near, where["other_near"], 1).astype(jnp.bfloat16)
    sent, own_spins = lax.optimization_barrier((sent, own_spins))
    came = swap(sent, 2)
    line = [swap(own_spins, 4 * step) for step in range(1, n_line)]
    came, line = lax.optimization_barrier((came, line))
    held = take(by_near, where["near"], 1) + came.astype(jnp.float32)
    pieces = [take(held, index, 0).astype(jnp.bfloat16) for index in where["line"][1:]]
    line_spins = jnp.zeros((n_line, sub_len, batch), jnp.bfloat16)
    for index, block in zip(where["line"], [own_spins] + line):
        line_spins = put_at(line_spins, block[None], index)
    pieces, line_spins = lax.optimization_barrier((pieces, line_spins))
    pieces = [swap(piece, 4 * step) for step, piece in enumerate(pieces, 1)]
    near_spins, peer_line = swap(line_spins, 2), swap(line_spins, 1)
    pieces, near_spins, peer_line = lax.optimization_barrier((pieces, near_spins, peer_line))
    all_spins = jnp.zeros((n_line, 2, 2, sub_len, batch), jnp.bfloat16)
    for near, core, group in (
        ("near", "core", line_spins),
        ("near", "other_core", peer_line),
        ("other_near", "core", near_spins),
        ("other_near", "other_core", swap(near_spins, 1)),
    ):
        all_spins = put_at(all_spins, group[:, None, None], 0, where[near], where[core])
    all_spins = all_spins.reshape(n_high, width, batch)
    total = take(held, where["line"][0], 0)
    for piece in pieces:
        total = total + piece.astype(jnp.float32)

    row_ids = lax.broadcasted_iota(jnp.int32, couple.shape, 0) - own_start
    col_ids = lax.broadcasted_iota(jnp.int32, couple.shape, 1) - where["item_col"]
    self_weight = jnp.sum(
        jnp.where(row_ids == col_ids, couple.astype(jnp.float32), 0.0), axis=1
    ).reshape(n_resp, sub_len, 1)
    self_weight = take(self_weight, where["source"][0], 0)
    own_spin = own_spins.astype(jnp.float32)
    fields = (total - self_weight * own_spin) * inv_root + bias[0][:, None]
    residual = (0.5 * (own_spin + 1.0) - jax.nn.sigmoid(fields)).astype(jnp.bfloat16)

    far = [swap(residual, 8 * step) for step in range(1, n_high)]
    others = []
    for step in range(1, n_resp):
        ring = [(i, (i + step) % n_resp) for i in range(n_resp)]
        others.append(lax.ppermute(residual, "resp", ring))
    near = [swap(residual, bits) for bits in (2, 4, 6)]
    far, others, near = lax.optimization_barrier((far, others, near))
    row_res = jnp.zeros((n_resp, sub_len, batch), jnp.bfloat16)
    for index, block in zip(where["source"], [residual] + others):
        row_res = put_at(row_res, block[None], index)
    row_res = row_res.reshape(item_dev, batch)

    row_ids = lax.broadcasted_iota(jnp.int32, (item_dev, width), 0) - own_start
    col_ids = lax.broadcasted_iota(jnp.int32, (item_dev, width), 1) - where["low_col"]
    on_diag = (row_ids == col_ids) & (row_ids >= 0) & (row_ids < sub_len)

    def product(left, right, step):
        grad = lax.dot_general(left, right, NT, preferred_element_type=jnp.float32)
        return jnp.where(on_diag, 0.0, grad) if step == 0 else grad

    def pick(blocks, step):
        picked = blocks[0]
        for index in range(1, n_high):
            picked = jnp.where(where["is_high"][step][index], blocks[index], picked)
        return picked

    def pick_part(parts, block):
        picked = parts[0]
        for step in range(1, n_high):
            picked = jnp.where(where["is_high"][step][block], parts[step], picked)
        return picked

    couple_blocks = jnp.split(couple, n_high, axis=1)
    noise_blocks = jnp.split(noise[0], n_high, axis=1)
    parts = []
    for step in range(n_high):
        current = pick(couple_blocks, step).astype(jnp.float32)
        shake = pick(noise_blocks, step).astype(jnp.float32)
        mirror = product(row_res, take(all_spins, where["high"][step], 0), step) * inv_root
        base = current + DRIFT * (DATA_RATIO * mirror - current) + NOISE_SCALE * shake

        if step:
            blocks = [far[step - 1]] + [swap(far[step - 1], bits) for bits in (2, 4, 6)]
        else:
            blocks = [residual] + near
        if step == n_high - 1:
            blocks, base, parts = lax.optimization_barrier((blocks, base, parts))
        quad = jnp.zeros((4, sub_len, batch), jnp.bfloat16)
        for index, block in zip(where["quad"], blocks):
            quad = put_at(quad, block[None], index)
        peers = swap(quad, 1)
        all_res = jnp.zeros((4, 2, sub_len, batch), jnp.bfloat16)
        all_res = put_at(all_res, quad[:, None], 0, where["core"])
        all_res = put_at(all_res, peers[:, None], 0, where["other_core"])
        part = product(spins, all_res.reshape(width, batch), step)
        part = base + (DRIFT * DATA_RATIO * inv_root) * part
        parts.append(part.astype(jnp.bfloat16))
    return jnp.concatenate([pick_part(parts, i) for i in range(n_high)], axis=1)[None]


def solution(mesh):
    return jax.shard_map(
        shards,
        mesh=mesh,
        in_specs=(
            P("resp", "item", None),
            P("resp", "item", None),
            P("item", "resp"),
            P(None, "item"),
            P(),
        ),
        out_specs=P("resp", "item", None),
        check_vma=False,
    )
```

time: 75.9 us -> 65.8 us (0.87)
  local copies, waits for them, and re-layouts: 11.1 us -> 3.73 us
  matrix products: 7.01 us -> 4.13 us
  starting transfers between devices: 23.4 us -> 25.2 us
  waiting for transfers between devices: 31.6 us -> 29.9 us
    unnamed x16 -> x11, local copies, waits for them, and re-layouts: 5.37 us -> 2.43 us
    dynamic_update_slice x29 -> x21, local copies, waits for them, and re-layouts: 3.2 us -> 0.55 us  [put_at(): lax.dynamic_update_slice(array, part, starts, allow_negative_indices=False)]
    ppermute x21, starting transfers between devices: 21.9 us -> 23.7 us  [swap(): return lax.ppermute(array, 'item', [(i, i ^ bits) for i in range(n_item)])]
    ppermute x21, waiting for transfers between devices: 31.6 us -> 29.9 us  [swap(): return lax.ppermute(array, 'item', [(i, i ^ bits) for i in range(n_item)])]
    dot_general x1, matrix products: 1.94 us -> 0.72 us  [shards(): lax.dot_general(pool_spins, picks, TN, preferred_element_type=jnp.float32)]
    dot_general x1, matrix products: 1.54 us -> 0.43 us  [shards(): lax.dot_general(got, peer_spins, TN, preferred_element_type=jnp.float32)]
    add x1, other arithmetic: 1.25 us -> 0.18 us  [shards(): held = take(by_near, where['near'], 1) + came.astype(jnp.float32)]
    broadcast_in_dim x0 -> x1, other arithmetic: none -> 1.06 us  [shards(): jnp.concatenate([pick_part(parts, i) for i in range(n_high)], axis=1)[None]]
  transfers between devices with their start and end apart: 22 -> 22, of which waited for: 12 -> 11; matrix products, arithmetic and copies ran while one was open for 9% -> 7% of each run, Pallas kernels for 0% -> 0%
where the time goes in v4:
time: 65.8 us; the launch traced here: 65.7 us
  waiting for transfers between devices  29.9 us (45%)
  starting transfers between devices  25.2 us (38%)
  matrix products  4.13 us (6%)
  local copies, waits for them, and re-layouts  3.73 us (6%)
  other arithmetic  2.24 us (3%)
    ppermute x21, waiting for transfers between devices, swap(): return lax.ppermute(array, 'item', [(i, i ^ bits) for i in range(n_item)])  29.9 us
    ppermute x21, starting transfers between devices, swap(): return lax.ppermute(array, 'item', [(i, i ^ bits) for i in range(n_item)])  23.7 us
    dot_general x4, matrix products, product(): grad = lax.dot_general(left, right, NT, preferred_element_type=jnp.float32)  2.55 us
    unnamed x11, local copies, waits for them, and re-layouts  2.43 us
    ppermute x1, starting transfers between devices, shards(): others.append(lax.ppermute(residual, 'resp', ring))  1.52 us
  transfers between devices with their start and end apart: 22, of which 11 were waited for; matrix products, arithmetic and copies ran while one was open for 7% of the time, Pallas kernels for 0%

profile of v4, /device:TPU:0, one launch (start us, length us, event | category | flops | bytes accessed | tf_op | source)
XLA Modules:
  0.0 65.7 jit_solution(18027403232238399427)
XLA Ops:
  0.0 1.6 %copy.14 = bf16[1,256,2048]{1,2,0:T(8,128)(2,1)S(1)} copy(bf16[1,256,2048]{2,1,0:T(8,128)(2,1)} %param.5) | data formatting | bytes 2097152 | tf_op args[0]
  1.6 0.1 constant_dynamic-slice_fusion.1
  1.7 0.5 collective-permute-start
  2.2 0.7 %fusion.13 = bf16[256,512]{1,0:T(8,128)(2,1)S(1)} fusion(s32[512]{0:T(512)S(1)} %copy-done.4, s32[1024,256]{1,0:T(8,128)S(1)} %copy-done.2), kind=kOutput, calls=%fused_computation.20 | convolution fusion | flops 269877248 | bytes 1312768 | tf_op jit(solution)/shard_map/dot_general | solution.py:65
  2.9 0.1 collective-permute-start.1
  3.1 0.4 fusion.45
  3.5 0.0 copy-start
  3.5 1.0 %collective-permute-done.1 = bf16[256,512]{1,0:T(8,128)(2,1)S(1)} collective-permute-done((bf16[256,512]{1,0:T(8,128)(2,1)S(1)}, bf16[256,512]{1,0:T(8,128)(2,1)S(1)}, u32[]{:S(2)}, u32[]{:S(2)}) %collective-permute-start.1) | collective-permute-done | bytes 262176 | tf_op jit(solution)/shard_map/ppermute | solution.py:48
  4.5 0.4 convolution_add_fusion
  5.0 0.1 fusion.19
  5.1 2.7 %collective-permute-start.2 = (bf16[4,128,512]{2,1,0:T(8,128)(2,1)S(1)}, bf16[4,128,512]{2,1,0:T(8,128)(2,1)S(1)}, u32[]{:S(2)}, u32[]{:S(2)}) collective-permute-start(bf16[4,128,512]{2,1,0:T(8,128)(2,1)S(1)} %fusion.19), channel_id=1, source_target_pairs={{0,2},{1,3},{2,0},{3,1},{4,6},{5,7},{6,4},{7,5},{8,10},{9,11},{10,... | collective-permute-start | bytes 1572872 | tf_op jit(solution)/shard_map/ppermute | solution.py:48
  7.8 0.4 select_reduce_fusion
  8.2 1.6 %collective-permute-start.3 = (bf16[128,512]{1,0:T(8,128)(2,1)S(1)}, bf16[128,512]{1,0:T(8,128)(2,1)S(1)}, u32[]{:S(2)}, u32[]{:S(2)}) collective-permute-start(bf16[128,512]{1,0:T(8,128)(2,1)S(1)} %dynamic-slice_bitcast_fusion), channel_id=1, source_target_pairs={{0,4},{1,5},{2,6},{3,7},{4,0},{5,1},{6,2},{7,3},{8,12},{9,13},{10,... | collective-permute-start | bytes 393224 | tf_op jit(solution)/shard_map/ppermute | solution.py:48
  9.8 2.6 %collective-permute-start.4 = (bf16[128,512]{1,0:T(8,128)(2,1)S(1)}, bf16[128,512]{1,0:T(8,128)(2,1)S(1)}, u32[]{:S(2)}, u32[]{:S(2)}) collective-permute-start(bf16[128,512]{1,0:T(8,128)(2,1)S(1)} %dynamic-slice_bitcast_fusion), channel_id=1, source_target_pairs={{0,8},{1,9},{2,10},{3,11},{4,12},{5,13},{6,14},{7,15},{8,0},{9,1},... | collective-permute-start | bytes 393224 | tf_op jit(solution)/shard_map/ppermute | solution.py:48
  12.4 0.2 collective-permute-start.5
  12.7 2.9 %collective-permute-done.3 = bf16[128,512]{1,0:T(8,128)(2,1)S(1)} collective-permute-done((bf16[128,512]{1,0:T(8,128)(2,1)S(1)}, bf16[128,512]{1,0:T(8,128)(2,1)S(1)}, u32[]{:S(2)}, u32[]{:S(2)}) %collective-permute-start.3) | collective-permute-done | bytes 131104 | tf_op jit(solution)/shard_map/ppermute | solution.py:48
  15.6 7.1 %collective-permute-done.4 = bf16[128,512]{1,0:T(8,128)(2,1)S(1)} collective-permute-done((bf16[128,512]{1,0:T(8,128)(2,1)S(1)}, bf16[128,512]{1,0:T(8,128)(2,1)S(1)}, u32[]{:S(2)}, u32[]{:S(2)}) %collective-permute-start.4) | collective-permute-done | bytes 131104 | tf_op jit(solution)/shard_map/ppermute | solution.py:48
  22.7 0.0 collective-permute-done.5
  22.7 0.0 collective-permute-done.2
  22.7 0.2 bitcast_add_fusion
  23.0 0.1 fusion.36
  23.0 0.0 copy-start.1
  23.1 0.1 collective-permute-start.10
  23.1 0.6 collective-permute-start.9
  23.8 2.3 %collective-permute-start.6 = (bf16[128,512]{1,0:T(8,128)(2,1)S(1)}, bf16[128,512]{1,0:T(8,128)(2,1)S(1)}, u32[]{:S(2)}, u32[]{:S(2)}) collective-permute-start(bf16[128,512]{1,0:T(8,128)(2,1)S(1)} %get-tuple-element.71), channel_id=1, source_target_pairs={{0,4},{1,5},{2,6},{3,7},{4,0},{5,1},{6,2},{7,3},{8,12},{9,13},{10,... | collective-permute-start | bytes 393224 | tf_op jit(solution)/shard_map/ppermute | solution.py:48
  26.1 1.1 %collective-permute-start.7 = (bf16[128,512]{1,0:T(8,128)(2,1)S(1)}, bf16[128,512]{1,0:T(8,128)(2,1)S(1)}, u32[]{:S(2)}, u32[]{:S(2)}) collective-permute-start(bf16[128,512]{1,0:T(8,128)(2,1)S(1)} %get-tuple-element.72), channel_id=1, source_target_pairs={{0,8},{1,9},{2,10},{3,11},{4,12},{5,13},{6,14},{7,15},{8,0},{9,1},... | collective-permute-start | bytes 393224 | tf_op jit(solution)/shard_map/ppermute | solution.py:48
  27.2 1.4 %collective-permute-start.8 = (bf16[128,512]{1,0:T(8,128)(2,1)S(1)}, bf16[128,512]{1,0:T(8,128)(2,1)S(1)}, u32[]{:S(2)}, u32[]{:S(2)}) collective-permute-start(bf16[128,512]{1,0:T(8,128)(2,1)S(1)} %get-tuple-element.73), channel_id=1, source_target_pairs={{0,12},{1,13},{2,14},{3,15},{4,8},{5,9},{6,10},{7,11},{8,4},{9,5},... | collective-permute-start | bytes 393224 | tf_op jit(solution)/shard_map/ppermute | solution.py:48
  28.5 0.2 broadcast_in_dim.91
  28.8 3.0 %collective-permute-done.6 = bf16[128,512]{1,0:T(8,128)(2,1)S(1)} collective-permute-done((bf16[128,512]{1,0:T(8,128)(2,1)S(1)}, bf16[128,512]{1,0:T(8,128)(2,1)S(1)}, u32[]{:S(2)}, u32[]{:S(2)}) %collective-permute-start.6) | collective-permute-done | bytes 131104 | tf_op jit(solution)/shard_map/ppermute | solution.py:48
  31.8 7.2 %collective-permute-done.7 = bf16[128,512]{1,0:T(8,128)(2,1)S(1)} collective-permute-done((bf16[128,512]{1,0:T(8,128)(2,1)S(1)}, bf16[128,512]{1,0:T(8,128)(2,1)S(1)}, u32[]{:S(2)}, u32[]{:S(2)}) %collective-permute-start.7) | collective-permute-done | bytes 131104 | tf_op jit(solution)/shard_map/ppermute | solution.py:48
  39.0 0.0 collective-permute-done.8
  39.0 0.0 collective-permute-done.10
  39.0 0.0 collective-permute-done.9
  39.0 0.2 bitcast_dynamic-update-slice_fusion.16
  39.2 3.4 %collective-permute-start.11 = (bf16[128,512]{1,0:T(8,128)(2,1)S(1)}, bf16[128,512]{1,0:T(8,128)(2,1)S(1)}, u32[]{:S(2)}, u32[]{:S(2)}) collective-permute-start(bf16[128,512]{1,0:T(8,128)(2,1)S(1)} %get-tuple-element.106), channel_id=1, source_target_pairs={{0,8},{1,9},{2,10},{3,11},{4,12},{5,13},{6,14},{7,15},{8,0},{9,1},... | collective-permute-start | bytes 393224 | tf_op jit(solution)/shard_map/ppermute | solution.py:48
  42.6 1.5 %collective-permute-start.12 = (bf16[128,512]{1,0:T(8,128)(2,1)S(1)}, bf16[128,512]{1,0:T(8,128)(2,1)S(1)}, u32[]{:S(2)}, u32[]{:S(2)}) collective-permute-start(bf16[128,512]{1,0:T(8,128)(2,1)S(1)} %get-tuple-element.106), channel_id=1, source_target_pairs={{0,16},{16,0},{1,17},{17,1},{2,18},{18,2},{3,19},{19,3},{4,20},{20... | collective-permute-start | bytes 393224 | tf_op jit(solution)/shard_map/ppermute | solution.py:116
  44.1 1.5 %collective-permute-start.13 = (bf16[128,512]{1,0:T(8,128)(2,1)S(1)}, bf16[128,512]{1,0:T(8,128)(2,1)S(1)}, u32[]{:S(2)}, u32[]{:S(2)}) collective-permute-start(bf16[128,512]{1,0:T(8,128)(2,1)S(1)} %get-tuple-element.106), channel_id=1, source_target_pairs={{0,2},{1,3},{2,0},{3,1},{4,6},{5,7},{6,4},{7,5},{8,10},{9,11},{10,... | collective-permute-start | bytes 393224 | tf_op jit(solution)/shard_map/ppermute | solution.py:48
  45.6 0.0 collective-permute-start.14
  45.6 2.0 %collective-permute-start.15 = (bf16[128,512]{1,0:T(8,128)(2,1)S(1)}, bf16[128,512]{1,0:T(8,128)(2,1)S(1)}, u32[]{:S(2)}, u32[]{:S(2)}) collective-permute-start(bf16[128,512]{1,0:T(8,128)(2,1)S(1)} %get-tuple-element.106), channel_id=1, source_target_pairs={{0,6},{1,7},{2,4},{3,5},{4,2},{5,3},{6,0},{7,1},{8,14},{9,15},{10,... | collective-permute-start | bytes 393224 | tf_op jit(solution)/shard_map/ppermute | solution.py:48
  47.7 0.6 collective-permute-done.11
  48.4 0.0 collective-permute-start.19
  48.4 0.0 collective-permute-done.12
  48.4 0.7 %collective-permute-done.13 = bf16[128,512]{1,0:T(8,128)(2,1)S(1)} collective-permute-done((bf16[128,512]{1,0:T(8,128)(2,1)S(1)}, bf16[128,512]{1,0:T(8,128)(2,1)S(1)}, u32[]{:S(2)}, u32[]{:S(2)}) %collective-permute-start.13) | collective-permute-done | bytes 131104 | tf_op jit(solution)/shard_map/ppermute | solution.py:48
  49.1 2.9 %collective-permute-done.14 = bf16[128,512]{1,0:T(8,128)(2,1)S(1)} collective-permute-done((bf16[128,512]{1,0:T(8,128)(2,1)S(1)}, bf16[128,512]{1,0:T(8,128)(2,1)S(1)}, u32[]{:S(2)}, u32[]{:S(2)}) %collective-permute-start.14) | collective-permute-done | bytes 131104 | tf_op jit(solution)/shard_map/ppermute | solution.py:48
  52.0 1.5 %collective-permute-done.15 = bf16[128,512]{1,0:T(8,128)(2,1)S(1)} collective-permute-done((bf16[128,512]{1,0:T(8,128)(2,1)S(1)}, bf16[128,512]{1,0:T(8,128)(2,1)S(1)}, u32[]{:S(2)}, u32[]{:S(2)}) %collective-permute-start.15) | collective-permute-done | bytes 131104 | tf_op jit(solution)/shard_map/ppermute | solution.py:48
  53.4 1.4 %collective-permute-start.16 = (bf16[128,512]{1,0:T(8,128)(2,1)S(1)}, bf16[128,512]{1,0:T(8,128)(2,1)S(1)}, u32[]{:S(2)}, u32[]{:S(2)}) collective-permute-start(bf16[128,512]{1,0:T(8,128)(2,1)S(1)} %collective-permute-done.11), channel_id=1, source_target_pairs={{0,2},{1,3},{2,0},{3,1},{4,6},{5,7},{6,4},{7,5},{8,10},{9,11},{10,... | collective-permute-start | bytes 393224 | tf_op jit(solution)/shard_map/ppermute | solution.py:48
  54.8 0.0 collective-permute-start.17
  54.8 2.1 %collective-permute-start.18 = (bf16[128,512]{1,0:T(8,128)(2,1)S(1)}, bf16[128,512]{1,0:T(8,128)(2,1)S(1)}, u32[]{:S(2)}, u32[]{:S(2)}) collective-permute-start(bf16[128,512]{1,0:T(8,128)(2,1)S(1)} %collective-permute-done.11), channel_id=1, source_target_pairs={{0,6},{1,7},{2,4},{3,5},{4,2},{5,3},{6,0},{7,1},{8,14},{9,15},{10,... | collective-permute-start | bytes 393224 | tf_op jit(solution)/shard_map/ppermute | solution.py:48
  57.0 0.1 collective-permute-start.20
  57.1 0.1 broadcast.52.clone
  57.2 0.0 collective-permute-done.19
  57.3 0.8 %copy-done.3 = bf16[1,256,2048]{2,1,0:T(8,128)(2,1)S(1)} copy-done((bf16[1,256,2048]{2,1,0:T(8,128)(2,1)S(1)}, bf16[1,256,2048]{2,1,0:T(8,128)(2,1)}, u32[]{:S(2)}) %copy-start.3) | copy-done | bytes 1048600
  58.1 0.7 fusion.4
  58.8 0.9 %fusion.9 = f32[256,1024]{1,0:T(8,128)S(1)} fusion(bf16[256,512]{1,0:T(8,128)(2,1)S(1)} %bitcast.129, bf16[2,1024,512]{2,1,0:T(8,128)(2,1)S(1)} %bitcast.123, s32[]{:T(128)S(6)} %select_n.91, s32[1024]{0:T(1024)S(1)} %iota_subtract_fusion.1, s32[256]{0:T(256)S(1)} %iota_subtract_fusion.2, pred[256]{0:T(512)(128)(4,1)S(1)} %get-tuple-element.112, ...), kind=kOutput, calls=%fused_computation.16 | convolution fusion | flops 272105472 | bytes 4462597 | tf_op jit(solution)/shard_map/dot_general | solution.py:129
  59.7 0.0 collective-permute-done.20
  59.7 0.6 fusion.12
  60.3 1.3 %collective-permute-done.18 = bf16[128,512]{1,0:T(8,128)(2,1)S(1)} collective-permute-done((bf16[128,512]{1,0:T(8,128)(2,1)S(1)}, bf16[128,512]{1,0:T(8,128)(2,1)S(1)}, u32[]{:S(2)}, u32[]{:S(2)}) %collective-permute-start.18) | collective-permute-done | bytes 131104 | tf_op jit(solution)/shard_map/ppermute | solution.py:48
  61.7 0.1 collective-permute-start.21
  61.8 0.1 broadcast.52
  62.0 1.8 %collective-permute-done.21 = bf16[4,128,512]{2,1,0:T(8,128)(2,1)S(1)} collective-permute-done((bf16[4,128,512]{2,1,0:T(8,128)(2,1)S(1)}, bf16[4,128,512]{2,1,0:T(8,128)(2,1)S(1)}, u32[]{:S(2)}, u32[]{:S(2)}) %collective-permute-start.21) | collective-permute-done | bytes 524320 | tf_op jit(solution)/shard_map/ppermute | solution.py:48
  63.8 0.5 convolution_multiply_fusion
  64.2 0.3 broadcast_select_fusion.1
  64.6 0.1 broadcast_select_fusion
  64.6 1.1 %maximum_bitcast_fusion = bf16[1,256,2048]{2,1,0:T(8,128)(2,1)} fusion(bf16[256,1024]{1,0:T(8,128)(2,1)S(1)} %broadcast_select_fusion, bf16[256,1024]{1,0:T(8,128)(2,1)S(1)} %get-tuple-element.103), kind=kLoop, calls=%fused_computation.21 | loop fusion | flops 2097152 | bytes 2097152 | tf_op jit(solution)/shard_map/broadcast_in_dim | solution.py:169
  (41 shorter events, 0.7 us)
Async XLA Ops:
  0.0 2.2 %copy-start.2 = (s32[1024,256]{1,0:T(8,128)S(1)}, s32[1024,256]{1,0:T(8,128)}, u32[]{:S(2)}) copy-start(s32[1024,256]{1,0:T(8,128)} %param.8) | copy-start | bytes 3145732
  0.0 2.2 %copy-start.4 = (s32[512]{0:T(512)S(1)}, s32[512]{0:T(512)}, u32[]{:S(2)}) copy-start(s32[512]{0:T(512)} %param.9) | copy-start | bytes 6148
  1.7 2.9 %collective-permute-start = (bf16[256,1024]{0,1:T(8,128)(2,1)S(1)}, bf16[256,1024]{0,1:T(8,128)(2,1)S(1)}, u32[]{:S(2)}, u32[]{:S(2)}) collective-permute-start(bf16[256,1024]{0,1:T(8,128)(2,1)S(1)} %bitcast.127), channel_id=1, source_target_pairs={{0,1},{1,0},{2,3},{3,2},{4,5},{5,4},{6,7},{7,6},{8,9},{9,8},{10,11... | collective-permute-start | bytes 1572872 | tf_op jit(solution)/shard_map/ppermute | solution.py:48
  2.9 1.6 %collective-permute-start.1 = (bf16[256,512]{1,0:T(8,128)(2,1)S(1)}, bf16[256,512]{1,0:T(8,128)(2,1)S(1)}, u32[]{:S(2)}, u32[]{:S(2)}) collective-permute-start(bf16[256,512]{1,0:T(8,128)(2,1)S(1)} %fusion.13), channel_id=1, source_target_pairs={{0,1},{1,0},{2,3},{3,2},{4,5},{5,4},{6,7},{7,6},{8,9},{9,8},{10,11... | collective-permute-start | bytes 786440 | tf_op jit(solution)/shard_map/ppermute | solution.py:48
  3.5 4.3 %copy-start = (bf16[1,256,2048]{2,1,0:T(8,128)(2,1)S(1)}, bf16[1,256,2048]{2,1,0:T(8,128)(2,1)}, u32[]{:S(2)}) copy-start(bf16[1,256,2048]{2,1,0:T(8,128)(2,1)} %param.5) | copy-start | bytes 3145732
  5.1 17.7 %collective-permute-start.2 = (bf16[4,128,512]{2,1,0:T(8,128)(2,1)S(1)}, bf16[4,128,512]{2,1,0:T(8,128)(2,1)S(1)}, u32[]{:S(2)}, u32[]{:S(2)}) collective-permute-start(bf16[4,128,512]{2,1,0:T(8,128)(2,1)S(1)} %fusion.19), channel_id=1, source_target_pairs={{0,2},{1,3},{2,0},{3,1},{4,6},{5,7},{6,4},{7,5},{8,10},{9,11},{10,... | collective-permute-start | bytes 1572872 | tf_op jit(solution)/shard_map/ppermute | solution.py:48
  8.2 7.4 %collective-permute-start.3 = (bf16[128,512]{1,0:T(8,128)(2,1)S(1)}, bf16[128,512]{1,0:T(8,128)(2,1)S(1)}, u32[]{:S(2)}, u32[]{:S(2)}) collective-permute-start(bf16[128,512]{1,0:T(8,128)(2,1)S(1)} %dynamic-slice_bitcast_fusion), channel_id=1, source_target_pairs={{0,4},{1,5},{2,6},{3,7},{4,0},{5,1},{6,2},{7,3},{8,12},{9,13},{10,... | collective-permute-start | bytes 393224 | tf_op jit(solution)/shard_map/ppermute | solution.py:48
  9.8 12.9 %collective-permute-start.4 = (bf16[128,512]{1,0:T(8,128)(2,1)S(1)}, bf16[128,512]{1,0:T(8,128)(2,1)S(1)}, u32[]{:S(2)}, u32[]{:S(2)}) collective-permute-start(bf16[128,512]{1,0:T(8,128)(2,1)S(1)} %dynamic-slice_bitcast_fusion), channel_id=1, source_target_pairs={{0,8},{1,9},{2,10},{3,11},{4,12},{5,13},{6,14},{7,15},{8,0},{9,1},... | collective-permute-start | bytes 393224 | tf_op jit(solution)/shard_map/ppermute | solution.py:48
  12.4 10.3 %collective-permute-start.5 = (bf16[128,512]{1,0:T(8,128)(2,1)S(1)}, bf16[128,512]{1,0:T(8,128)(2,1)S(1)}, u32[]{:S(2)}, u32[]{:S(2)}) collective-permute-start(bf16[128,512]{1,0:T(8,128)(2,1)S(1)} %dynamic-slice_bitcast_fusion), channel_id=1, source_target_pairs={{0,12},{1,13},{2,14},{3,15},{4,8},{5,9},{6,10},{7,11},{8,4},{9,5},... | collective-permute-start | bytes 393224 | tf_op jit(solution)/shard_map/ppermute | solution.py:48
  23.0 16.0 %copy-start.1 = (f32[1,128]{1,0:T(1,128)S(1)}, f32[1,128]{1,0:T(1,128)}, u32[]{:S(2)}) copy-start(f32[1,128]{1,0:T(1,128)} %param.7) | copy-start | bytes 1540
  23.1 15.9 %collective-permute-start.10 = (bf16[4,128,512]{2,1,0:T(8,128)(2,1)S(1)}, bf16[4,128,512]{2,1,0:T(8,128)(2,1)S(1)}, u32[]{:S(2)}, u32[]{:S(2)}) collective-permute-start(bf16[4,128,512]{2,1,0:T(8,128)(2,1)S(1)} %bitcast_dynamic-update-slice_fusion.18), channel_id=1, source_target_pairs={{0,1},{1,0},{2,3},{3,2},{4,5},{5,4},{6,7},{7,6},{8,9},{9,8},{10,11... | collective-permute-start | bytes 1572872 | tf_op jit(solution)/shard_map/ppermute | solution.py:48
  23.1 15.8 %collective-permute-start.9 = (bf16[4,128,512]{2,1,0:T(8,128)(2,1)S(1)}, bf16[4,128,512]{2,1,0:T(8,128)(2,1)S(1)}, u32[]{:S(2)}, u32[]{:S(2)}) collective-permute-start(bf16[4,128,512]{2,1,0:T(8,128)(2,1)S(1)} %bitcast_dynamic-update-slice_fusion.18), channel_id=1, source_target_pairs={{0,2},{1,3},{2,0},{3,1},{4,6},{5,7},{6,4},{7,5},{8,10},{9,11},{10,... | collective-permute-start | bytes 1572872 | tf_op jit(solution)/shard_map/ppermute | solution.py:48
  23.8 8.0 %collective-permute-start.6 = (bf16[128,512]{1,0:T(8,128)(2,1)S(1)}, bf16[128,512]{1,0:T(8,128)(2,1)S(1)}, u32[]{:S(2)}, u32[]{:S(2)}) collective-permute-start(bf16[128,512]{1,0:T(8,128)(2,1)S(1)} %get-tuple-element.71), channel_id=1, source_target_pairs={{0,4},{1,5},{2,6},{3,7},{4,0},{5,1},{6,2},{7,3},{8,12},{9,13},{10,... | collective-permute-start | bytes 393224 | tf_op jit(solution)/shard_map/ppermute | solution.py:48
  26.1 12.9 %collective-permute-start.7 = (bf16[128,512]{1,0:T(8,128)(2,1)S(1)}, bf16[128,512]{1,0:T(8,128)(2,1)S(1)}, u32[]{:S(2)}, u32[]{:S(2)}) collective-permute-start(bf16[128,512]{1,0:T(8,128)(2,1)S(1)} %get-tuple-element.72), channel_id=1, source_target_pairs={{0,8},{1,9},{2,10},{3,11},{4,12},{5,13},{6,14},{7,15},{8,0},{9,1},... | collective-permute-start | bytes 393224 | tf_op jit(solution)/shard_map/ppermute | solution.py:48
  27.2 11.8 %collective-permute-start.8 = (bf16[128,512]{1,0:T(8,128)(2,1)S(1)}, bf16[128,512]{1,0:T(8,128)(2,1)S(1)}, u32[]{:S(2)}, u32[]{:S(2)}) collective-permute-start(bf16[128,512]{1,0:T(8,128)(2,1)S(1)} %get-tuple-element.73), channel_id=1, source_target_pairs={{0,12},{1,13},{2,14},{3,15},{4,8},{5,9},{6,10},{7,11},{8,4},{9,5},... | collective-permute-start | bytes 393224 | tf_op jit(solution)/shard_map/ppermute | solution.py:48
  39.2 9.1 %collective-permute-start.11 = (bf16[128,512]{1,0:T(8,128)(2,1)S(1)}, bf16[128,512]{1,0:T(8,128)(2,1)S(1)}, u32[]{:S(2)}, u32[]{:S(2)}) collective-permute-start(bf16[128,512]{1,0:T(8,128)(2,1)S(1)} %get-tuple-element.106), channel_id=1, source_target_pairs={{0,8},{1,9},{2,10},{3,11},{4,12},{5,13},{6,14},{7,15},{8,0},{9,1},... | collective-permute-start | bytes 393224 | tf_op jit(solution)/shard_map/ppermute | solution.py:48
  42.6 5.8 %collective-permute-start.12 = (bf16[128,512]{1,0:T(8,128)(2,1)S(1)}, bf16[128,512]{1,0:T(8,128)(2,1)S(1)}, u32[]{:S(2)}, u32[]{:S(2)}) collective-permute-start(bf16[128,512]{1,0:T(8,128)(2,1)S(1)} %get-tuple-element.106), channel_id=1, source_target_pairs={{0,16},{16,0},{1,17},{17,1},{2,18},{18,2},{3,19},{19,3},{4,20},{20... | collective-permute-start | bytes 393224 | tf_op jit(solution)/shard_map/ppermute | solution.py:116
  44.1 5.0 %collective-permute-start.13 = (bf16[128,512]{1,0:T(8,128)(2,1)S(1)}, bf16[128,512]{1,0:T(8,128)(2,1)S(1)}, u32[]{:S(2)}, u32[]{:S(2)}) collective-permute-start(bf16[128,512]{1,0:T(8,128)(2,1)S(1)} %get-tuple-element.106), channel_id=1, source_target_pairs={{0,2},{1,3},{2,0},{3,1},{4,6},{5,7},{6,4},{7,5},{8,10},{9,11},{10,... | collective-permute-start | bytes 393224 | tf_op jit(solution)/shard_map/ppermute | solution.py:48
  45.6 6.4 %collective-permute-start.14 = (bf16[128,512]{1,0:T(8,128)(2,1)S(1)}, bf16[128,512]{1,0:T(8,128)(2,1)S(1)}, u32[]{:S(2)}, u32[]{:S(2)}) collective-permute-start(bf16[128,512]{1,0:T(8,128)(2,1)S(1)} %get-tuple-element.106), channel_id=1, source_target_pairs={{0,4},{1,5},{2,6},{3,7},{4,0},{5,1},{6,2},{7,3},{8,12},{9,13},{10,... | collective-permute-start | bytes 393224 | tf_op jit(solution)/shard_map/ppermute | solution.py:48
  45.6 7.8 %collective-permute-start.15 = (bf16[128,512]{1,0:T(8,128)(2,1)S(1)}, bf16[128,512]{1,0:T(8,128)(2,1)S(1)}, u32[]{:S(2)}, u32[]{:S(2)}) collective-permute-start(bf16[128,512]{1,0:T(8,128)(2,1)S(1)} %get-tuple-element.106), channel_id=1, source_target_pairs={{0,6},{1,7},{2,4},{3,5},{4,2},{5,3},{6,0},{7,1},{8,14},{9,15},{10,... | collective-permute-start | bytes 393224 | tf_op jit(solution)/shard_map/ppermute | solution.py:48
  48.4 8.9 %collective-permute-start.19 = (bf16[4,128,512]{2,1,0:T(8,128)(2,1)S(1)}, bf16[4,128,512]{2,1,0:T(8,128)(2,1)S(1)}, u32[]{:S(2)}, u32[]{:S(2)}) collective-permute-start(bf16[4,128,512]{2,1,0:T(8,128)(2,1)S(1)} %collective-permute-done.9), channel_id=1, source_target_pairs={{0,1},{1,0},{2,3},{3,2},{4,5},{5,4},{6,7},{7,6},{8,9},{9,8},{10,11... | collective-permute-start | bytes 1572872 | tf_op jit(solution)/shard_map/ppermute | solution.py:48
  53.4 6.9 %collective-permute-start.16 = (bf16[128,512]{1,0:T(8,128)(2,1)S(1)}, bf16[128,512]{1,0:T(8,128)(2,1)S(1)}, u32[]{:S(2)}, u32[]{:S(2)}) collective-permute-start(bf16[128,512]{1,0:T(8,128)(2,1)S(1)} %collective-permute-done.11), channel_id=1, source_target_pairs={{0,2},{1,3},{2,0},{3,1},{4,6},{5,7},{6,4},{7,5},{8,10},{9,11},{10,... | collective-permute-start | bytes 393224 | tf_op jit(solution)/shard_map/ppermute | solution.py:48
  54.8 5.5 %collective-permute-start.17 = (bf16[128,512]{1,0:T(8,128)(2,1)S(1)}, bf16[128,512]{1,0:T(8,128)(2,1)S(1)}, u32[]{:S(2)}, u32[]{:S(2)}) collective-permute-start(bf16[128,512]{1,0:T(8,128)(2,1)S(1)} %collective-permute-done.11), channel_id=1, source_target_pairs={{0,4},{1,5},{2,6},{3,7},{4,0},{5,1},{6,2},{7,3},{8,12},{9,13},{10,... | collective-permute-start | bytes 393224 | tf_op jit(solution)/shard_map/ppermute | solution.py:48
  54.8 6.8 %collective-permute-start.18 = (bf16[128,512]{1,0:T(8,128)(2,1)S(1)}, bf16[128,512]{1,0:T(8,128)(2,1)S(1)}, u32[]{:S(2)}, u32[]{:S(2)}) collective-permute-start(bf16[128,512]{1,0:T(8,128)(2,1)S(1)} %collective-permute-done.11), channel_id=1, source_target_pairs={{0,6},{1,7},{2,4},{3,5},{4,2},{5,3},{6,0},{7,1},{8,14},{9,15},{10,... | collective-permute-start | bytes 393224 | tf_op jit(solution)/shard_map/ppermute | solution.py:48
  56.9 1.2 %copy-start.3 = (bf16[1,256,2048]{2,1,0:T(8,128)(2,1)S(1)}, bf16[1,256,2048]{2,1,0:T(8,128)(2,1)}, u32[]{:S(2)}) copy-start(bf16[1,256,2048]{2,1,0:T(8,128)(2,1)} %param.6) | copy-start | bytes 3145732
  57.0 2.7 %collective-permute-start.20 = (bf16[4,128,512]{2,1,0:T(8,128)(2,1)S(1)}, bf16[4,128,512]{2,1,0:T(8,128)(2,1)S(1)}, u32[]{:S(2)}, u32[]{:S(2)}) collective-permute-start(bf16[4,128,512]{2,1,0:T(8,128)(2,1)S(1)} %bitcast_dynamic-update-slice_fusion.12), channel_id=1, source_target_pairs={{0,1},{1,0},{2,3},{3,2},{4,5},{5,4},{6,7},{7,6},{8,9},{9,8},{10,11... | collective-permute-start | bytes 1572872 | tf_op jit(solution)/shard_map/ppermute | solution.py:48
  61.7 2.0 %collective-permute-start.21 = (bf16[4,128,512]{2,1,0:T(8,128)(2,1)S(1)}, bf16[4,128,512]{2,1,0:T(8,128)(2,1)S(1)}, u32[]{:S(2)}, u32[]{:S(2)}) collective-permute-start(bf16[4,128,512]{2,1,0:T(8,128)(2,1)S(1)} %bitcast_dynamic-update-slice_fusion.8), channel_id=1, source_target_pairs={{0,1},{1,0},{2,3},{3,2},{4,5},{5,4},{6,7},{7,6},{8,9},{9,8},{10,11... | collective-permute-start | bytes 1572872 | tf_op jit(solution)/shard_map/ppermute | solution.py:48

commit v5 on v4

--- a/solution.py
+++ b/solution.py
@@ -73,19 +73,35 @@
 
     by_near = partial.reshape(n_line, 2, sub_len, batch)
     sent = take(by_near, where["other_near"], 1).astype(jnp.bfloat16)
-    sent, own_spins = lax.optimization_barrier((sent, own_spins))
-    came = swap(sent, 2)
+    mine = take(by_near, where["near"], 1)
+    sent, mine, own_spins = lax.optimization_barrier((sent, mine, own_spins))
+    distant, close = list(range(2, n_line)), [1, 0]
+
+    def across(steps):
+        return jnp.stack([take(sent, where["line"][step], 0) for step in steps])
+
+    def added(steps, came):
+        kept = jnp.stack([take(mine, where["line"][step], 0) for step in steps])
+        return kept + came.astype(jnp.float32)
+
+    groups = lax.optimization_barrier((across(distant), across(close)))
+    came = [swap(group, 2) for group in groups]
     line = [swap(own_spins, 4 * step) for step in range(1, n_line)]
-    came, line = lax.optimization_barrier((came, line))
-    held = take(by_near, where["near"], 1) + came.astype(jnp.float32)
-    pieces = [take(held, index, 0).astype(jnp.bfloat16) for index in where["line"][1:]]
+    distant_sums = added(distant, came[0]).astype(jnp.bfloat16)
+    pieces = [swap(block, 4 * step) for step, block in zip(distant, distant_sums)]
+    came_close, _ = lax.optimization_barrier((came[1], distant_sums))
+    close_sums = added(close, came_close)
+    close_piece = swap(close_sums[0].astype(jnp.bfloat16), 4)
+    line, _ = lax.optimization_barrier((line, close_sums))
     line_spins = jnp.zeros((n_line, sub_len, batch), jnp.bfloat16)
     for index, block in zip(where["line"], [own_spins] + line):
         line_spins = put_at(line_spins, block[None], index)
-    pieces, line_spins = lax.optimization_barrier((pieces, line_spins))
-    pieces = [swap(piece, 4 * step) for step, piece in enumerate(pieces, 1)]
     near_spins, peer_line = swap(line_spins, 2), swap(line_spins, 1)
-    pieces, near_spins, peer_line = lax.optimization_barrier((pieces, near_spins, peer_line))
+    total = close_sums[1]
+    for piece in pieces:
+        total = total + piece.astype(jnp.float32)
+    total, near_spins, peer_line = lax.optimization_barrier((total, near_spins, peer_line))
+    total = total + close_piece.astype(jnp.float32)
     all_spins = jnp.zeros((n_line, 2, 2, sub_len, batch), jnp.bfloat16)
     for near, core, group in (
         ("near", "core", line_spins),
@@ -95,10 +111,6 @@
     ):
         all_spins = put_at(all_spins, group[:, None, None], 0, where[near], where[core])
     all_spins = all_spins.reshape(n_high, width, batch)
-    total = take(held, where["line"][0], 0)
-    for piece in pieces:
-        total = total + piece.astype(jnp.float32)
-
     row_ids = lax.broadcasted_iota(jnp.int32, couple.shape, 0) - own_start
     col_ids = lax.broadcasted_iota(jnp.int32, couple.shape, 1) - where["item_col"]
     self_weight = jnp.sum(
@@ -115,7 +127,7 @@
         ring = [(i, (i + step) % n_resp) for i in range(n_resp)]
         others.append(lax.ppermute(residual, "resp", ring))
     near = [swap(residual, bits) for bits in (2, 4, 6)]
-    far, others, near = lax.optimization_barrier((far, others, near))
+    far, near[:2] = lax.optimization_barrier((far, near[:2]))
     row_res = jnp.zeros((n_resp, sub_len, batch), jnp.bfloat16)
     for index, block in zip(where["source"], [residual] + others):
         row_res = put_at(row_res, block[None], index)

time: 65.8 us -> 61.1 us (0.929)
  waiting for transfers between devices: 29.9 us -> 24.7 us
  starting transfers between devices: 25.2 us -> 26.3 us
  local copies, waits for them, and re-layouts: 3.73 us -> 3.06 us
    ppermute x21 -> x22, waiting for transfers between devices: 29.9 us -> 24.7 us  [swap(): return lax.ppermute(array, 'item', [(i, i ^ bits) for i in range(n_item)])]
    ppermute x21 -> x22, starting transfers between devices: 23.7 us -> 24.7 us  [swap(): return lax.ppermute(array, 'item', [(i, i ^ bits) for i in range(n_item)])]
    unnamed x11, local copies, waits for them, and re-layouts: 2.43 us -> 1.58 us
  transfers between devices with their start and end apart: 22 -> 23, of which waited for: 11 -> 11; matrix products, arithmetic and copies ran while one was open for 7% -> 8% of each run, Pallas kernels for 0% -> 0%
where the time goes in v5:
time: 61.1 us; the launch traced here: 61 us
  starting transfers between devices  26.3 us (43%)
  waiting for transfers between devices  24.7 us (40%)
  matrix products  4.16 us (7%)
  local copies, waits for them, and re-layouts  3.06 us (5%)
  other arithmetic  2.31 us (4%)
    ppermute x22, starting transfers between devices, swap(): return lax.ppermute(array, 'item', [(i, i ^ bits) for i in range(n_item)])  24.7 us
    ppermute x22, waiting for transfers between devices, swap(): return lax.ppermute(array, 'item', [(i, i ^ bits) for i in range(n_item)])  24.7 us
    dot_general x4, matrix products, product(): grad = lax.dot_general(left, right, NT, preferred_element_type=jnp.float32)  2.58 us
    unnamed x11, local copies, waits for them, and re-layouts  1.58 us
    ppermute x1, starting transfers between devices, shards(): others.append(lax.ppermute(residual, 'resp', ring))  1.53 us
  transfers between devices with their start and end apart: 23, of which 11 were waited for; matrix products, arithmetic and copies ran while one was open for 8% of the time, Pallas kernels for 0%

profile of v5, /device:TPU:0, one launch (start us, length us, event | category | flops | bytes accessed | tf_op | source)
XLA Modules:
  0.0 61.0 jit_solution(588012812789668255)
XLA Ops:
  0.0 1.6 %copy.14 = bf16[1,256,2048]{1,2,0:T(8,128)(2,1)S(1)} copy(bf16[1,256,2048]{2,1,0:T(8,128)(2,1)} %param.5) | data formatting | bytes 2097152 | tf_op args[0]
  1.6 0.0 copy-start
  1.6 0.1 constant_dynamic-slice_fusion.9
  1.7 0.5 collective-permute-start
  2.2 0.7 %fusion.13 = bf16[256,512]{1,0:T(8,128)(2,1)S(1)} fusion(s32[512]{0:T(512)S(1)} %copy-done.4, s32[1024,256]{1,0:T(8,128)S(1)} %copy-done.2), kind=kOutput, calls=%fused_computation.20 | convolution fusion | flops 269877248 | bytes 1312768 | tf_op jit(solution)/shard_map/dot_general | solution.py:65
  2.9 0.1 collective-permute-start.1
  3.1 0.4 select_reduce_fusion
  3.5 0.4 fusion.44
  4.0 0.6 collective-permute-done.1
  4.5 0.0 collective-permute-done
  4.5 0.4 convolution_add_fusion
  5.0 0.1 dynamic-slice_bitcast_fusion
  5.1 0.1 fusion.19
  5.2 0.1 constant_dynamic-slice_fusion.4
  5.3 2.7 %collective-permute-start.3 = (bf16[2,128,512]{2,1,0:T(8,128)(2,1)S(1)}, bf16[2,128,512]{2,1,0:T(8,128)(2,1)S(1)}, u32[]{:S(2)}, u32[]{:S(2)}) collective-permute-start(bf16[2,128,512]{2,1,0:T(8,128)(2,1)S(1)} %pad_maximum_fusion), channel_id=1, source_target_pairs={{0,2},{1,3},{2,0},{3,1},{4,6},{5,7},{6,4},{7,5},{8,10},{9,11},{10,... | collective-permute-start | bytes 786440 | tf_op jit(solution)/shard_map/ppermute | solution.py:48
  8.0 1.6 %collective-permute-start.6 = (bf16[128,512]{1,0:T(8,128)(2,1)S(1)}, bf16[128,512]{1,0:T(8,128)(2,1)S(1)}, u32[]{:S(2)}, u32[]{:S(2)}) collective-permute-start(bf16[128,512]{1,0:T(8,128)(2,1)S(1)} %dynamic-slice_bitcast_fusion.1), channel_id=1, source_target_pairs={{0,4},{1,5},{2,6},{3,7},{4,0},{5,1},{6,2},{7,3},{8,12},{9,13},{10,... | collective-permute-start | bytes 393224 | tf_op jit(solution)/shard_map/ppermute | solution.py:48
  9.6 2.6 %collective-permute-start.7 = (bf16[128,512]{1,0:T(8,128)(2,1)S(1)}, bf16[128,512]{1,0:T(8,128)(2,1)S(1)}, u32[]{:S(2)}, u32[]{:S(2)}) collective-permute-start(bf16[128,512]{1,0:T(8,128)(2,1)S(1)} %dynamic-slice_bitcast_fusion.1), channel_id=1, source_target_pairs={{0,8},{1,9},{2,10},{3,11},{4,12},{5,13},{6,14},{7,15},{8,0},{9,1},... | collective-permute-start | bytes 393224 | tf_op jit(solution)/shard_map/ppermute | solution.py:48
  12.2 0.2 collective-permute-start.8
  12.4 0.3 collective-permute-start.2
  12.7 0.1 constant_dynamic-slice_fusion.2
  12.8 2.3 %collective-permute-done.3 = bf16[2,128,512]{2,1,0:T(8,128)(2,1)S(1)} collective-permute-done((bf16[2,128,512]{2,1,0:T(8,128)(2,1)S(1)}, bf16[2,128,512]{2,1,0:T(8,128)(2,1)S(1)}, u32[]{:S(2)}, u32[]{:S(2)}) %collective-permute-start.3) | collective-permute-done | bytes 262176 | tf_op jit(solution)/shard_map/ppermute | solution.py:48
  15.2 0.1 fusion.20
  15.3 5.2 %collective-permute-done.2 = bf16[2,128,512]{2,1,0:T(8,128)(2,1)S(1)} collective-permute-done((bf16[2,128,512]{2,1,0:T(8,128)(2,1)S(1)}, bf16[2,128,512]{2,1,0:T(8,128)(2,1)S(1)}, u32[]{:S(2)}, u32[]{:S(2)}) %collective-permute-start.2) | collective-permute-done | bytes 262176 | tf_op jit(solution)/shard_map/ppermute | solution.py:48
  20.5 0.1 maximum_add_fusion
  20.6 0.0 collective-permute-done.6
  20.6 1.9 %collective-permute-done.7 = bf16[128,512]{1,0:T(8,128)(2,1)S(1)} collective-permute-done((bf16[128,512]{1,0:T(8,128)(2,1)S(1)}, bf16[128,512]{1,0:T(8,128)(2,1)S(1)}, u32[]{:S(2)}, u32[]{:S(2)}) %collective-permute-start.7) | collective-permute-done | bytes 131104 | tf_op jit(solution)/shard_map/ppermute | solution.py:48
  22.5 0.0 collective-permute-done.8
  22.6 0.1 collective-permute-start.10
  22.7 0.6 collective-permute-start.9
  23.3 3.3 %collective-permute-start.4 = (bf16[128,512]{1,0:T(8,128)(2,1)S(1)}, bf16[128,512]{1,0:T(8,128)(2,1)S(1)}, u32[]{:S(2)}, u32[]{:S(2)}) collective-permute-start(bf16[128,512]{1,0:T(8,128)(2,1)S(1)} %get-tuple-element.107), channel_id=1, source_target_pairs={{0,8},{1,9},{2,10},{3,11},{4,12},{5,13},{6,14},{7,15},{8,0},{9,1},... | collective-permute-start | bytes 393224 | tf_op jit(solution)/shard_map/ppermute | solution.py:48
  26.6 1.4 %collective-permute-start.5 = (bf16[128,512]{1,0:T(8,128)(2,1)S(1)}, bf16[128,512]{1,0:T(8,128)(2,1)S(1)}, u32[]{:S(2)}, u32[]{:S(2)}) collective-permute-start(bf16[128,512]{1,0:T(8,128)(2,1)S(1)} %get-tuple-element.108), channel_id=1, source_target_pairs={{0,12},{1,13},{2,14},{3,15},{4,8},{5,9},{6,10},{7,11},{8,4},{9,5},... | collective-permute-start | bytes 393224 | tf_op jit(solution)/shard_map/ppermute | solution.py:48
  28.0 0.0 collective-permute-start.11
  28.0 0.2 broadcast_in_dim.91
  28.2 8.3 %collective-permute-done.4 = bf16[128,512]{1,0:T(8,128)(2,1)S(1)} collective-permute-done((bf16[128,512]{1,0:T(8,128)(2,1)S(1)}, bf16[128,512]{1,0:T(8,128)(2,1)S(1)}, u32[]{:S(2)}, u32[]{:S(2)}) %collective-permute-start.4) | collective-permute-done | bytes 131104 | tf_op jit(solution)/shard_map/ppermute | solution.py:48
  36.6 0.0 collective-permute-done.5
  36.6 0.0 collective-permute-done.10
  36.6 0.4 collective-permute-done.9
  37.0 0.4 collective-permute-done.11
  37.5 0.2 bitcast_dynamic-update-slice_fusion.16
  37.7 3.0 %collective-permute-start.12 = (bf16[128,512]{1,0:T(8,128)(2,1)S(1)}, bf16[128,512]{1,0:T(8,128)(2,1)S(1)}, u32[]{:S(2)}, u32[]{:S(2)}) collective-permute-start(bf16[128,512]{1,0:T(8,128)(2,1)S(1)} %get-tuple-element.96), channel_id=1, source_target_pairs={{0,8},{1,9},{2,10},{3,11},{4,12},{5,13},{6,14},{7,15},{8,0},{9,1},... | collective-permute-start | bytes 393224 | tf_op jit(solution)/shard_map/ppermute | solution.py:48
  40.7 1.0 %collective-permute-start.13 = (bf16[128,512]{1,0:T(8,128)(2,1)S(1)}, bf16[128,512]{1,0:T(8,128)(2,1)S(1)}, u32[]{:S(2)}, u32[]{:S(2)}) collective-permute-start(bf16[128,512]{1,0:T(8,128)(2,1)S(1)} %get-tuple-element.96), channel_id=1, source_target_pairs={{0,2},{1,3},{2,0},{3,1},{4,6},{5,7},{6,4},{7,5},{8,10},{9,11},{10,... | collective-permute-start | bytes 393224 | tf_op jit(solution)/shard_map/ppermute | solution.py:48
  41.7 2.4 %collective-permute-start.20 = (bf16[128,512]{1,0:T(8,128)(2,1)S(1)}, bf16[128,512]{1,0:T(8,128)(2,1)S(1)}, u32[]{:S(2)}, u32[]{:S(2)}) collective-permute-start(bf16[128,512]{1,0:T(8,128)(2,1)S(1)} %get-tuple-element.96), channel_id=1, source_target_pairs={{0,6},{1,7},{2,4},{3,5},{4,2},{5,3},{6,0},{7,1},{8,14},{9,15},{10,... | collective-permute-start | bytes 393224 | tf_op jit(solution)/shard_map/ppermute | solution.py:48
  44.4 2.4 %collective-permute-done.12 = bf16[128,512]{1,0:T(8,128)(2,1)S(1)} collective-permute-done((bf16[128,512]{1,0:T(8,128)(2,1)S(1)}, bf16[128,512]{1,0:T(8,128)(2,1)S(1)}, u32[]{:S(2)}, u32[]{:S(2)}) %collective-permute-start.12) | collective-permute-done | bytes 131104 | tf_op jit(solution)/shard_map/ppermute | solution.py:48
  46.8 1.5 %collective-permute-start.18 = (bf16[128,512]{1,0:T(8,128)(2,1)S(1)}, bf16[128,512]{1,0:T(8,128)(2,1)S(1)}, u32[]{:S(2)}, u32[]{:S(2)}) collective-permute-start(bf16[128,512]{1,0:T(8,128)(2,1)S(1)} %get-tuple-element.96), channel_id=1, source_target_pairs={{0,16},{16,0},{1,17},{17,1},{2,18},{18,2},{3,19},{19,3},{4,20},{20... | collective-permute-start | bytes 393224 | tf_op jit(solution)/shard_map/ppermute | solution.py:128
  48.3 0.3 collective-permute-done.14
  48.7 0.9 %collective-permute-start.15 = (bf16[128,512]{1,0:T(8,128)(2,1)S(1)}, bf16[128,512]{1,0:T(8,128)(2,1)S(1)}, u32[]{:S(2)}, u32[]{:S(2)}) collective-permute-start(bf16[128,512]{1,0:T(8,128)(2,1)S(1)} %collective-permute-done.12), channel_id=1, source_target_pairs={{0,2},{1,3},{2,0},{3,1},{4,6},{5,7},{6,4},{7,5},{8,10},{9,11},{10,... | collective-permute-start | bytes 393224 | tf_op jit(solution)/shard_map/ppermute | solution.py:48
  49.5 1.2 %collective-permute-start.16 = (bf16[128,512]{1,0:T(8,128)(2,1)S(1)}, bf16[128,512]{1,0:T(8,128)(2,1)S(1)}, u32[]{:S(2)}, u32[]{:S(2)}) collective-permute-start(bf16[128,512]{1,0:T(8,128)(2,1)S(1)} %collective-permute-done.12), channel_id=1, source_target_pairs={{0,4},{1,5},{2,6},{3,7},{4,0},{5,1},{6,2},{7,3},{8,12},{9,13},{10,... | collective-permute-start | bytes 393224 | tf_op jit(solution)/shard_map/ppermute | solution.py:48
  50.8 0.0 collective-permute-done.20
  50.8 2.5 %collective-permute-start.17 = (bf16[128,512]{1,0:T(8,128)(2,1)S(1)}, bf16[128,512]{1,0:T(8,128)(2,1)S(1)}, u32[]{:S(2)}, u32[]{:S(2)}) collective-permute-start(bf16[128,512]{1,0:T(8,128)(2,1)S(1)} %collective-permute-done.12), channel_id=1, source_target_pairs={{0,6},{1,7},{2,4},{3,5},{4,2},{5,3},{6,0},{7,1},{8,14},{9,15},{10,... | collective-permute-start | bytes 393224 | tf_op jit(solution)/shard_map/ppermute | solution.py:48
  53.3 0.1 collective-permute-start.21
  53.4 0.1 broadcast.52.clone
  53.7 0.7 %fusion.4 = f32[256,1024]{1,0:T(8,128)S(1)} fusion(bf16[256,512]{1,0:T(8,128)(2,1)S(1)} %bitcast.125, bf16[2,1024,512]{2,1,0:T(8,128)(2,1)S(1)} %bitcast.119, s32[]{:T(128)S(6)} %xor.23, pred[]{:T(512)S(6)} %eq.36, bf16[256,2048]{1,0:T(8,128)(2,1)S(1)} %bitcast.129, bf16[256,2048]{1,0:T(8,128)(2,1)S(1)} %bitcast.115), kind=kOutput, calls=%fused_computation.11 | convolution fusion | flops 271056896 | bytes 4456453 | tf_op jit(solution)/shard_map/dot_general | solution.py:141
  54.3 1.0 %collective-permute-done.21 = bf16[4,128,512]{2,1,0:T(8,128)(2,1)S(1)} collective-permute-done((bf16[4,128,512]{2,1,0:T(8,128)(2,1)S(1)}, bf16[4,128,512]{2,1,0:T(8,128)(2,1)S(1)}, u32[]{:S(2)}, u32[]{:S(2)}) %collective-permute-start.21) | collective-permute-done | bytes 524320 | tf_op jit(solution)/shard_map/ppermute | solution.py:48
  55.4 0.5 fusion.11
  55.9 0.9 %fusion.12 = bf16[256,1024]{1,0:T(8,128)(2,1)S(1)} fusion(f32[256,1024]{1,0:T(8,128)S(1)} %fusion.11, bf16[256,512]{1,0:T(8,128)(2,1)S(1)} %bitcast.126, bf16[2,1024,512]{2,1,0:T(8,128)(2,1)S(1)} %bitcast.120, s32[]{:T(128)S(6)} %select_n.91, s32[1024]{0:T(1024)S(1)} %iota_subtract_fusion.1, s32[256]{0:T(256)S(1)} %iota_subtract_fusion.2, ...), kind=kOutput, calls=%fused_computation.19 | convolution fusion | flops 272629760 | bytes 4986885 | tf_op jit(solution)/shard_map/dot_general | solution.py:141
  56.8 0.0 collective-permute-done.15
  56.8 0.0 collective-permute-done.17
  57.0 0.2 collective-permute-start.22
  57.2 0.1 broadcast.52
  57.4 1.6 %collective-permute-done.22 = bf16[4,128,512]{2,1,0:T(8,128)(2,1)S(1)} collective-permute-done((bf16[4,128,512]{2,1,0:T(8,128)(2,1)S(1)}, bf16[4,128,512]{2,1,0:T(8,128)(2,1)S(1)}, u32[]{:S(2)}, u32[]{:S(2)}) %collective-permute-start.22) | collective-permute-done | bytes 524320 | tf_op jit(solution)/shard_map/ppermute | solution.py:48
  59.0 0.5 convolution_multiply_fusion
  59.5 0.3 broadcast_select_fusion.1
  59.8 0.1 broadcast_select_fusion
  59.9 1.1 %maximum_bitcast_fusion = bf16[1,256,2048]{2,1,0:T(8,128)(2,1)} fusion(bf16[256,1024]{1,0:T(8,128)(2,1)S(1)} %broadcast_select_fusion, bf16[256,1024]{1,0:T(8,128)(2,1)S(1)} %get-tuple-element.93), kind=kLoop, calls=%fused_computation.21 | loop fusion | flops 2097152 | bytes 2097152 | tf_op jit(solution)/shard_map/broadcast_in_dim | solution.py:181
  (50 shorter events, 0.9 us)
Async XLA Ops:
  0.0 2.2 %copy-start.2 = (s32[1024,256]{1,0:T(8,128)S(1)}, s32[1024,256]{1,0:T(8,128)}, u32[]{:S(2)}) copy-start(s32[1024,256]{1,0:T(8,128)} %param.8) | copy-start | bytes 3145732
  0.0 2.2 %copy-start.4 = (s32[512]{0:T(512)S(1)}, s32[512]{0:T(512)}, u32[]{:S(2)}) copy-start(s32[512]{0:T(512)} %param.9) | copy-start | bytes 6148
  1.6 1.5 %copy-start = (bf16[1,256,2048]{2,1,0:T(8,128)(2,1)S(1)}, bf16[1,256,2048]{2,1,0:T(8,128)(2,1)}, u32[]{:S(2)}) copy-start(bf16[1,256,2048]{2,1,0:T(8,128)(2,1)} %param.5) | copy-start | bytes 3145732
  1.7 2.9 %collective-permute-start = (bf16[256,1024]{0,1:T(8,128)(2,1)S(1)}, bf16[256,1024]{0,1:T(8,128)(2,1)S(1)}, u32[]{:S(2)}, u32[]{:S(2)}) collective-permute-start(bf16[256,1024]{0,1:T(8,128)(2,1)S(1)} %bitcast.124), channel_id=1, source_target_pairs={{0,1},{1,0},{2,3},{3,2},{4,5},{5,4},{6,7},{7,6},{8,9},{9,8},{10,11... | collective-permute-start | bytes 1572872 | tf_op jit(solution)/shard_map/ppermute | solution.py:48
  2.9 1.6 %collective-permute-start.1 = (bf16[256,512]{1,0:T(8,128)(2,1)S(1)}, bf16[256,512]{1,0:T(8,128)(2,1)S(1)}, u32[]{:S(2)}, u32[]{:S(2)}) collective-permute-start(bf16[256,512]{1,0:T(8,128)(2,1)S(1)} %fusion.13), channel_id=1, source_target_pairs={{0,1},{1,0},{2,3},{3,2},{4,5},{5,4},{6,7},{7,6},{8,9},{9,8},{10,11... | collective-permute-start | bytes 786440 | tf_op jit(solution)/shard_map/ppermute | solution.py:48
  5.3 9.8 %collective-permute-start.3 = (bf16[2,128,512]{2,1,0:T(8,128)(2,1)S(1)}, bf16[2,128,512]{2,1,0:T(8,128)(2,1)S(1)}, u32[]{:S(2)}, u32[]{:S(2)}) collective-permute-start(bf16[2,128,512]{2,1,0:T(8,128)(2,1)S(1)} %pad_maximum_fusion), channel_id=1, source_target_pairs={{0,2},{1,3},{2,0},{3,1},{4,6},{5,7},{6,4},{7,5},{8,10},{9,11},{10,... | collective-permute-start | bytes 786440 | tf_op jit(solution)/shard_map/ppermute | solution.py:48
  8.0 12.5 %collective-permute-start.6 = (bf16[128,512]{1,0:T(8,128)(2,1)S(1)}, bf16[128,512]{1,0:T(8,128)(2,1)S(1)}, u32[]{:S(2)}, u32[]{:S(2)}) collective-permute-start(bf16[128,512]{1,0:T(8,128)(2,1)S(1)} %dynamic-slice_bitcast_fusion.1), channel_id=1, source_target_pairs={{0,4},{1,5},{2,6},{3,7},{4,0},{5,1},{6,2},{7,3},{8,12},{9,13},{10,... | collective-permute-start | bytes 393224 | tf_op jit(solution)/shard_map/ppermute | solution.py:48
  9.6 12.9 %collective-permute-start.7 = (bf16[128,512]{1,0:T(8,128)(2,1)S(1)}, bf16[128,512]{1,0:T(8,128)(2,1)S(1)}, u32[]{:S(2)}, u32[]{:S(2)}) collective-permute-start(bf16[128,512]{1,0:T(8,128)(2,1)S(1)} %dynamic-slice_bitcast_fusion.1), channel_id=1, source_target_pairs={{0,8},{1,9},{2,10},{3,11},{4,12},{5,13},{6,14},{7,15},{8,0},{9,1},... | collective-permute-start | bytes 393224 | tf_op jit(solution)/shard_map/ppermute | solution.py:48
  12.2 10.3 %collective-permute-start.8 = (bf16[128,512]{1,0:T(8,128)(2,1)S(1)}, bf16[128,512]{1,0:T(8,128)(2,1)S(1)}, u32[]{:S(2)}, u32[]{:S(2)}) collective-permute-start(bf16[128,512]{1,0:T(8,128)(2,1)S(1)} %dynamic-slice_bitcast_fusion.1), channel_id=1, source_target_pairs={{0,12},{1,13},{2,14},{3,15},{4,8},{5,9},{6,10},{7,11},{8,4},{9,5},... | collective-permute-start | bytes 393224 | tf_op jit(solution)/shard_map/ppermute | solution.py:48
  12.4 8.1 %collective-permute-start.2 = (bf16[2,128,512]{2,1,0:T(8,128)(2,1)S(1)}, bf16[2,128,512]{2,1,0:T(8,128)(2,1)S(1)}, u32[]{:S(2)}, u32[]{:S(2)}) collective-permute-start(bf16[2,128,512]{2,1,0:T(8,128)(2,1)S(1)} %pad_maximum_fusion.1), channel_id=1, source_target_pairs={{0,2},{1,3},{2,0},{3,1},{4,6},{5,7},{6,4},{7,5},{8,10},{9,11},{10,... | collective-permute-start | bytes 786440 | tf_op jit(solution)/shard_map/ppermute | solution.py:48
  22.6 14.0 %collective-permute-start.10 = (bf16[4,128,512]{2,1,0:T(8,128)(2,1)S(1)}, bf16[4,128,512]{2,1,0:T(8,128)(2,1)S(1)}, u32[]{:S(2)}, u32[]{:S(2)}) collective-permute-start(bf16[4,128,512]{2,1,0:T(8,128)(2,1)S(1)} %bitcast_dynamic-update-slice_fusion.18), channel_id=1, source_target_pairs={{0,1},{1,0},{2,3},{3,2},{4,5},{5,4},{6,7},{7,6},{8,9},{9,8},{10,11... | collective-permute-start | bytes 1572872 | tf_op jit(solution)/shard_map/ppermute | solution.py:48
  22.7 14.3 %collective-permute-start.9 = (bf16[4,128,512]{2,1,0:T(8,128)(2,1)S(1)}, bf16[4,128,512]{2,1,0:T(8,128)(2,1)S(1)}, u32[]{:S(2)}, u32[]{:S(2)}) collective-permute-start(bf16[4,128,512]{2,1,0:T(8,128)(2,1)S(1)} %bitcast_dynamic-update-slice_fusion.18), channel_id=1, source_target_pairs={{0,2},{1,3},{2,0},{3,1},{4,6},{5,7},{6,4},{7,5},{8,10},{9,11},{10,... | collective-permute-start | bytes 1572872 | tf_op jit(solution)/shard_map/ppermute | solution.py:48
  23.3 13.2 %collective-permute-start.4 = (bf16[128,512]{1,0:T(8,128)(2,1)S(1)}, bf16[128,512]{1,0:T(8,128)(2,1)S(1)}, u32[]{:S(2)}, u32[]{:S(2)}) collective-permute-start(bf16[128,512]{1,0:T(8,128)(2,1)S(1)} %get-tuple-element.107), channel_id=1, source_target_pairs={{0,8},{1,9},{2,10},{3,11},{4,12},{5,13},{6,14},{7,15},{8,0},{9,1},... | collective-permute-start | bytes 393224 | tf_op jit(solution)/shard_map/ppermute | solution.py:48
  26.6 10.9 %copy-start.1 = (f32[1,128]{1,0:T(1,128)S(1)}, f32[1,128]{1,0:T(1,128)}, u32[]{:S(2)}) copy-start(f32[1,128]{1,0:T(1,128)} %param.7) | copy-start | bytes 1540
  26.6 9.9 %collective-permute-start.5 = (bf16[128,512]{1,0:T(8,128)(2,1)S(1)}, bf16[128,512]{1,0:T(8,128)(2,1)S(1)}, u32[]{:S(2)}, u32[]{:S(2)}) collective-permute-start(bf16[128,512]{1,0:T(8,128)(2,1)S(1)} %get-tuple-element.108), channel_id=1, source_target_pairs={{0,12},{1,13},{2,14},{3,15},{4,8},{5,9},{6,10},{7,11},{8,4},{9,5},... | collective-permute-start | bytes 393224 | tf_op jit(solution)/shard_map/ppermute | solution.py:48
  28.0 9.5 %collective-permute-start.11 = (bf16[128,512]{1,0:T(8,128)(2,1)S(1)}, bf16[128,512]{1,0:T(8,128)(2,1)S(1)}, u32[]{:S(2)}, u32[]{:S(2)}) collective-permute-start(bf16[128,512]{1,0:T(8,128)(2,1)S(1)} %fusion.35), channel_id=1, source_target_pairs={{0,4},{1,5},{2,6},{3,7},{4,0},{5,1},{6,2},{7,3},{8,12},{9,13},{10,... | collective-permute-start | bytes 393224 | tf_op jit(solution)/shard_map/ppermute | solution.py:48
  37.7 9.1 %collective-permute-start.12 = (bf16[128,512]{1,0:T(8,128)(2,1)S(1)}, bf16[128,512]{1,0:T(8,128)(2,1)S(1)}, u32[]{:S(2)}, u32[]{:S(2)}) collective-permute-start(bf16[128,512]{1,0:T(8,128)(2,1)S(1)} %get-tuple-element.96), channel_id=1, source_target_pairs={{0,8},{1,9},{2,10},{3,11},{4,12},{5,13},{6,14},{7,15},{8,0},{9,1},... | collective-permute-start | bytes 393224 | tf_op jit(solution)/shard_map/ppermute | solution.py:48
  40.7 7.6 %collective-permute-start.13 = (bf16[128,512]{1,0:T(8,128)(2,1)S(1)}, bf16[128,512]{1,0:T(8,128)(2,1)S(1)}, u32[]{:S(2)}, u32[]{:S(2)}) collective-permute-start(bf16[128,512]{1,0:T(8,128)(2,1)S(1)} %get-tuple-element.96), channel_id=1, source_target_pairs={{0,2},{1,3},{2,0},{3,1},{4,6},{5,7},{6,4},{7,5},{8,10},{9,11},{10,... | collective-permute-start | bytes 393224 | tf_op jit(solution)/shard_map/ppermute | solution.py:48
  41.7 6.9 %collective-permute-start.14 = (bf16[128,512]{1,0:T(8,128)(2,1)S(1)}, bf16[128,512]{1,0:T(8,128)(2,1)S(1)}, u32[]{:S(2)}, u32[]{:S(2)}) collective-permute-start(bf16[128,512]{1,0:T(8,128)(2,1)S(1)} %get-tuple-element.96), channel_id=1, source_target_pairs={{0,4},{1,5},{2,6},{3,7},{4,0},{5,1},{6,2},{7,3},{8,12},{9,13},{10,... | collective-permute-start | bytes 393224 | tf_op jit(solution)/shard_map/ppermute | solution.py:48
  41.7 9.1 %collective-permute-start.20 = (bf16[128,512]{1,0:T(8,128)(2,1)S(1)}, bf16[128,512]{1,0:T(8,128)(2,1)S(1)}, u32[]{:S(2)}, u32[]{:S(2)}) collective-permute-start(bf16[128,512]{1,0:T(8,128)(2,1)S(1)} %get-tuple-element.96), channel_id=1, source_target_pairs={{0,6},{1,7},{2,4},{3,5},{4,2},{5,3},{6,0},{7,1},{8,14},{9,15},{10,... | collective-permute-start | bytes 393224 | tf_op jit(solution)/shard_map/ppermute | solution.py:48
  44.2 9.4 %collective-permute-start.19 = (bf16[4,128,512]{2,1,0:T(8,128)(2,1)S(1)}, bf16[4,128,512]{2,1,0:T(8,128)(2,1)S(1)}, u32[]{:S(2)}, u32[]{:S(2)}) collective-permute-start(bf16[4,128,512]{2,1,0:T(8,128)(2,1)S(1)} %collective-permute-done.9), channel_id=1, source_target_pairs={{0,1},{1,0},{2,3},{3,2},{4,5},{5,4},{6,7},{7,6},{8,9},{9,8},{10,11... | collective-permute-start | bytes 1572872 | tf_op jit(solution)/shard_map/ppermute | solution.py:48
  46.8 6.5 %collective-permute-start.18 = (bf16[128,512]{1,0:T(8,128)(2,1)S(1)}, bf16[128,512]{1,0:T(8,128)(2,1)S(1)}, u32[]{:S(2)}, u32[]{:S(2)}) collective-permute-start(bf16[128,512]{1,0:T(8,128)(2,1)S(1)} %get-tuple-element.96), channel_id=1, source_target_pairs={{0,16},{16,0},{1,17},{17,1},{2,18},{18,2},{3,19},{19,3},{4,20},{20... | collective-permute-start | bytes 393224 | tf_op jit(solution)/shard_map/ppermute | solution.py:128
  48.7 8.2 %collective-permute-start.15 = (bf16[128,512]{1,0:T(8,128)(2,1)S(1)}, bf16[128,512]{1,0:T(8,128)(2,1)S(1)}, u32[]{:S(2)}, u32[]{:S(2)}) collective-permute-start(bf16[128,512]{1,0:T(8,128)(2,1)S(1)} %collective-permute-done.12), channel_id=1, source_target_pairs={{0,2},{1,3},{2,0},{3,1},{4,6},{5,7},{6,4},{7,5},{8,10},{9,11},{10,... | collective-permute-start | bytes 393224 | tf_op jit(solution)/shard_map/ppermute | solution.py:48
  49.5 7.3 %collective-permute-start.16 = (bf16[128,512]{1,0:T(8,128)(2,1)S(1)}, bf16[128,512]{1,0:T(8,128)(2,1)S(1)}, u32[]{:S(2)}, u32[]{:S(2)}) collective-permute-start(bf16[128,512]{1,0:T(8,128)(2,1)S(1)} %collective-permute-done.12), channel_id=1, source_target_pairs={{0,4},{1,5},{2,6},{3,7},{4,0},{5,1},{6,2},{7,3},{8,12},{9,13},{10,... | collective-permute-start | bytes 393224 | tf_op jit(solution)/shard_map/ppermute | solution.py:48
  50.7 2.9 %copy-start.3 = (bf16[1,256,2048]{2,1,0:T(8,128)(2,1)S(1)}, bf16[1,256,2048]{2,1,0:T(8,128)(2,1)}, u32[]{:S(2)}) copy-start(bf16[1,256,2048]{2,1,0:T(8,128)(2,1)} %param.6) | copy-start | bytes 3145732
  50.8 6.0 %collective-permute-start.17 = (bf16[128,512]{1,0:T(8,128)(2,1)S(1)}, bf16[128,512]{1,0:T(8,128)(2,1)S(1)}, u32[]{:S(2)}, u32[]{:S(2)}) collective-permute-start(bf16[128,512]{1,0:T(8,128)(2,1)S(1)} %collective-permute-done.12), channel_id=1, source_target_pairs={{0,6},{1,7},{2,4},{3,5},{4,2},{5,3},{6,0},{7,1},{8,14},{9,15},{10,... | collective-permute-start | bytes 393224 | tf_op jit(solution)/shard_map/ppermute | solution.py:48
  53.3 2.0 %collective-permute-start.21 = (bf16[4,128,512]{2,1,0:T(8,128)(2,1)S(1)}, bf16[4,128,512]{2,1,0:T(8,128)(2,1)S(1)}, u32[]{:S(2)}, u32[]{:S(2)}) collective-permute-start(bf16[4,128,512]{2,1,0:T(8,128)(2,1)S(1)} %bitcast_dynamic-update-slice_fusion.12), channel_id=1, source_target_pairs={{0,1},{1,0},{2,3},{3,2},{4,5},{5,4},{6,7},{7,6},{8,9},{9,8},{10,11... | collective-permute-start | bytes 1572872 | tf_op jit(solution)/shard_map/ppermute | solution.py:48
  57.0 2.0 %collective-permute-start.22 = (bf16[4,128,512]{2,1,0:T(8,128)(2,1)S(1)}, bf16[4,128,512]{2,1,0:T(8,128)(2,1)S(1)}, u32[]{:S(2)}, u32[]{:S(2)}) collective-permute-start(bf16[4,128,512]{2,1,0:T(8,128)(2,1)S(1)} %bitcast_dynamic-update-slice_fusion.8), channel_id=1, source_target_pairs={{0,1},{1,0},{2,3},{3,2},{4,5},{5,4},{6,7},{7,6},{8,9},{9,8},{10,11... | collective-permute-start | bytes 1572872 | tf_op jit(solution)/shard_map/ppermute | solution.py:48

commit v6 on v5

--- a/solution.py
+++ b/solution.py
@@ -75,7 +75,7 @@
     sent = take(by_near, where["other_near"], 1).astype(jnp.bfloat16)
     mine = take(by_near, where["near"], 1)
     sent, mine, own_spins = lax.optimization_barrier((sent, mine, own_spins))
-    distant, close = list(range(2, n_line)), [1, 0]
+    given_steps, kept_steps = list(range(1, n_line, 2)), list(range(0, n_line, 2))
 
     def across(steps):
         return jnp.stack([take(sent, where["line"][step], 0) for step in steps])
@@ -84,33 +84,26 @@
         kept = jnp.stack([take(mine, where["line"][step], 0) for step in steps])
         return kept + came.astype(jnp.float32)
 
-    groups = lax.optimization_barrier((across(distant), across(close)))
+    groups = lax.optimization_barrier((across(given_steps), across(kept_steps)))
     came = [swap(group, 2) for group in groups]
     line = [swap(own_spins, 4 * step) for step in range(1, n_line)]
-    distant_sums = added(distant, came[0]).astype(jnp.bfloat16)
-    pieces = [swap(block, 4 * step) for step, block in zip(distant, distant_sums)]
-    came_close, _ = lax.optimization_barrier((came[1], distant_sums))
-    close_sums = added(close, came_close)
-    close_piece = swap(close_sums[0].astype(jnp.bfloat16), 4)
-    line, _ = lax.optimization_barrier((line, close_sums))
+    given_sums = added(given_steps, came[0]).astype(jnp.bfloat16)
+    passed = swap(given_sums, 4)
+    came_kept, _ = lax.optimization_barrier((came[1], given_sums))
+    line, _ = lax.optimization_barrier((line, came_kept))
+    kept_sums = added(kept_steps, came_kept)
     line_spins = jnp.zeros((n_line, sub_len, batch), jnp.bfloat16)
     for index, block in zip(where["line"], [own_spins] + line):
         line_spins = put_at(line_spins, block[None], index)
     near_spins, peer_line = swap(line_spins, 2), swap(line_spins, 1)
-    total = close_sums[1]
+    kept_sums = kept_sums + passed.astype(jnp.float32)
+    pieces = [
+        swap(kept_sums[step].astype(jnp.bfloat16), 8 * step) for step in range(1, n_high)
+    ]
+    total = kept_sums[0]
+    pieces, peer_line = lax.optimization_barrier((pieces, peer_line))
     for piece in pieces:
         total = total + piece.astype(jnp.float32)
-    total, near_spins, peer_line = lax.optimization_barrier((total, near_spins, peer_line))
-    total = total + close_piece.astype(jnp.float32)
-    all_spins = jnp.zeros((n_line, 2, 2, sub_len, batch), jnp.bfloat16)
-    for near, core, group in (
-        ("near", "core", line_spins),
-        ("near", "other_core", peer_line),
-        ("other_near", "core", near_spins),
-        ("other_near", "other_core", swap(near_spins, 1)),
-    ):
-        all_spins = put_at(all_spins, group[:, None, None], 0, where[near], where[core])
-    all_spins = all_spins.reshape(n_high, width, batch)
     row_ids = lax.broadcasted_iota(jnp.int32, couple.shape, 0) - own_start
     col_ids = lax.broadcasted_iota(jnp.int32, couple.shape, 1) - where["item_col"]
     self_weight = jnp.sum(
@@ -127,7 +120,16 @@
         ring = [(i, (i + step) % n_resp) for i in range(n_resp)]
         others.append(lax.ppermute(residual, "resp", ring))
     near = [swap(residual, bits) for bits in (2, 4, 6)]
-    far, near[:2] = lax.optimization_barrier((far, near[:2]))
+    far, near[:2], near_spins = lax.optimization_barrier((far, near[:2], near_spins))
+    all_spins = jnp.zeros((n_line, 2, 2, sub_len, batch), jnp.bfloat16)
+    for side, core, group in (
+        ("near", "core", line_spins),
+        ("near", "other_core", peer_line),
+        ("other_near", "core", near_spins),
+        ("other_near", "other_core", swap(near_spins, 1)),
+    ):
+        all_spins = put_at(all_spins, group[:, None, None], 0, where[side], where[core])
+    all_spins = all_spins.reshape(n_high, width, batch)
     row_res = jnp.zeros((n_resp, sub_len, batch), jnp.bfloat16)
     for index, block in zip(where["source"], [residual] + others):
         row_res = put_at(row_res, block[None], index)

time: 61.1 us -> 59 us (0.966)
  starting transfers between devices: 26.3 us -> 23.6 us
    ppermute x22 -> x21, starting transfers between devices: 24.7 us -> 22 us  [swap(): return lax.ppermute(array, 'item', [(i, i ^ bits) for i in range(n_item)])]
    ppermute x22 -> x21, waiting for transfers between devices: 24.7 us -> 24.8 us  [swap(): return lax.ppermute(array, 'item', [(i, i ^ bits) for i in range(n_item)])]
  transfers between devices with their start and end apart: 23 -> 22, of which waited for: 11 -> 12; matrix products, arithmetic and copies ran while one was open for 8% -> 8% of each run, Pallas kernels for 0% -> 0%
where the time goes in v6:
time: 59 us; the launch traced here: 58.8 us
  waiting for transfers between devices  24.8 us (42%)
  starting transfers between devices  23.6 us (40%)
  matrix products  4.13 us (7%)
  local copies, waits for them, and re-layouts  3.51 us (6%)
  other arithmetic  2.29 us (4%)
    ppermute x21, waiting for transfers between devices, swap(): return lax.ppermute(array, 'item', [(i, i ^ bits) for i in range(n_item)])  24.8 us
    ppermute x21, starting transfers between devices, swap(): return lax.ppermute(array, 'item', [(i, i ^ bits) for i in range(n_item)])  22 us
    dot_general x4, matrix products, product(): grad = lax.dot_general(left, right, NT, preferred_element_type=jnp.float32)  2.56 us
    unnamed x11, local copies, waits for them, and re-layouts  2.06 us
    ppermute x1, starting transfers between devices, shards(): others.append(lax.ppermute(residual, 'resp', ring))  1.61 us
  transfers between devices with their start and end apart: 22, of which 12 were waited for; matrix products, arithmetic and copies ran while one was open for 8% of the time, Pallas kernels for 0%

profile of v6, /device:TPU:0, one launch (start us, length us, event | category | flops | bytes accessed | tf_op | source)
XLA Modules:
  0.0 58.8 jit_solution(6736485585604240219)
XLA Ops:
  0.0 1.6 %copy.14 = bf16[1,256,2048]{1,2,0:T(8,128)(2,1)S(1)} copy(bf16[1,256,2048]{2,1,0:T(8,128)(2,1)} %param.5) | data formatting | bytes 2097152 | tf_op args[0]
  1.6 0.0 copy-start
  1.6 0.1 constant_dynamic-slice_fusion.9
  1.7 0.5 collective-permute-start
  2.2 0.7 %fusion.13 = bf16[256,512]{1,0:T(8,128)(2,1)S(1)} fusion(s32[512]{0:T(512)S(1)} %copy-done.4, s32[1024,256]{1,0:T(8,128)S(1)} %copy-done.2), kind=kOutput, calls=%fused_computation.20 | convolution fusion | flops 269877248 | bytes 1312768 | tf_op jit(solution)/shard_map/dot_general | solution.py:65
  2.9 0.1 collective-permute-start.1
  3.1 0.4 select_reduce_fusion
  3.5 0.4 fusion.44
  4.0 0.6 collective-permute-done.1
  4.5 0.4 convolution_add_fusion
  5.0 0.1 dynamic-slice_bitcast_fusion
  5.1 0.1 fusion.19
  5.2 0.1 constant_dynamic-slice_fusion.4
  5.3 2.7 %collective-permute-start.3 = (bf16[2,128,512]{2,1,0:T(8,128)(2,1)S(1)}, bf16[2,128,512]{2,1,0:T(8,128)(2,1)S(1)}, u32[]{:S(2)}, u32[]{:S(2)}) collective-permute-start(bf16[2,128,512]{2,1,0:T(8,128)(2,1)S(1)} %pad_maximum_fusion), channel_id=1, source_target_pairs={{0,2},{1,3},{2,0},{3,1},{4,6},{5,7},{6,4},{7,5},{8,10},{9,11},{10,... | collective-permute-start | bytes 786440 | tf_op jit(solution)/shard_map/ppermute | solution.py:48
  8.0 1.6 %collective-permute-start.6 = (bf16[128,512]{1,0:T(8,128)(2,1)S(1)}, bf16[128,512]{1,0:T(8,128)(2,1)S(1)}, u32[]{:S(2)}, u32[]{:S(2)}) collective-permute-start(bf16[128,512]{1,0:T(8,128)(2,1)S(1)} %dynamic-slice_bitcast_fusion.1), channel_id=1, source_target_pairs={{0,4},{1,5},{2,6},{3,7},{4,0},{5,1},{6,2},{7,3},{8,12},{9,13},{10,... | collective-permute-start | bytes 393224 | tf_op jit(solution)/shard_map/ppermute | solution.py:48
  9.6 2.6 %collective-permute-start.7 = (bf16[128,512]{1,0:T(8,128)(2,1)S(1)}, bf16[128,512]{1,0:T(8,128)(2,1)S(1)}, u32[]{:S(2)}, u32[]{:S(2)}) collective-permute-start(bf16[128,512]{1,0:T(8,128)(2,1)S(1)} %dynamic-slice_bitcast_fusion.1), channel_id=1, source_target_pairs={{0,8},{1,9},{2,10},{3,11},{4,12},{5,13},{6,14},{7,15},{8,0},{9,1},... | collective-permute-start | bytes 393224 | tf_op jit(solution)/shard_map/ppermute | solution.py:48
  12.2 0.2 collective-permute-start.8
  12.4 0.3 collective-permute-start.2
  12.7 0.1 constant_dynamic-slice_fusion.2
  12.8 2.3 %collective-permute-done.3 = bf16[2,128,512]{2,1,0:T(8,128)(2,1)S(1)} collective-permute-done((bf16[2,128,512]{2,1,0:T(8,128)(2,1)S(1)}, bf16[2,128,512]{2,1,0:T(8,128)(2,1)S(1)}, u32[]{:S(2)}, u32[]{:S(2)}) %collective-permute-start.3) | collective-permute-done | bytes 262176 | tf_op jit(solution)/shard_map/ppermute | solution.py:48
  15.2 0.1 fusion.21
  15.3 2.1 %collective-permute-start.4 = (bf16[2,128,512]{2,1,0:T(8,128)(2,1)S(1)}, bf16[2,128,512]{2,1,0:T(8,128)(2,1)S(1)}, u32[]{:S(2)}, u32[]{:S(2)}) collective-permute-start(bf16[2,128,512]{2,1,0:T(8,128)(2,1)S(1)} %fusion.21), channel_id=1, source_target_pairs={{0,4},{1,5},{2,6},{3,7},{4,0},{5,1},{6,2},{7,3},{8,12},{9,13},{10,... | collective-permute-start | bytes 786440 | tf_op jit(solution)/shard_map/ppermute | solution.py:48
  17.4 3.1 %collective-permute-done.2 = bf16[2,128,512]{2,1,0:T(8,128)(2,1)S(1)} collective-permute-done((bf16[2,128,512]{2,1,0:T(8,128)(2,1)S(1)}, bf16[2,128,512]{2,1,0:T(8,128)(2,1)S(1)}, u32[]{:S(2)}, u32[]{:S(2)}) %collective-permute-start.2) | collective-permute-done | bytes 262176 | tf_op jit(solution)/shard_map/ppermute | solution.py:48
  20.5 2.1 %collective-permute-done.7 = bf16[128,512]{1,0:T(8,128)(2,1)S(1)} collective-permute-done((bf16[128,512]{1,0:T(8,128)(2,1)S(1)}, bf16[128,512]{1,0:T(8,128)(2,1)S(1)}, u32[]{:S(2)}, u32[]{:S(2)}) %collective-permute-start.7) | collective-permute-done | bytes 131104 | tf_op jit(solution)/shard_map/ppermute | solution.py:48
  22.6 0.1 collective-permute-start.9
  22.7 0.6 %collective-permute-start.13 = (bf16[4,128,512]{2,1,0:T(8,128)(2,1)S(1)}, bf16[4,128,512]{2,1,0:T(8,128)(2,1)S(1)}, u32[]{:S(2)}, u32[]{:S(2)}) collective-permute-start(bf16[4,128,512]{2,1,0:T(8,128)(2,1)S(1)} %bitcast_dynamic-update-slice_fusion.18), channel_id=1, source_target_pairs={{0,2},{1,3},{2,0},{3,1},{4,6},{5,7},{6,4},{7,5},{8,10},{9,11},{10,... | collective-permute-start | bytes 1572872 | tf_op jit(solution)/shard_map/ppermute | solution.py:48
  23.3 3.1 %collective-permute-done.4 = bf16[2,128,512]{2,1,0:T(8,128)(2,1)S(1)} collective-permute-done((bf16[2,128,512]{2,1,0:T(8,128)(2,1)S(1)}, bf16[2,128,512]{2,1,0:T(8,128)(2,1)S(1)}, u32[]{:S(2)}, u32[]{:S(2)}) %collective-permute-start.4) | collective-permute-done | bytes 262176 | tf_op jit(solution)/shard_map/ppermute | solution.py:48
  26.5 0.1 fusion.20
  26.6 0.0 copy-start.1
  26.6 1.2 %collective-permute-start.5 = (bf16[128,512]{1,0:T(8,128)(2,1)S(1)}, bf16[128,512]{1,0:T(8,128)(2,1)S(1)}, u32[]{:S(2)}, u32[]{:S(2)}) collective-permute-start(bf16[128,512]{1,0:T(8,128)(2,1)S(1)} %fusion.35), channel_id=1, source_target_pairs={{0,8},{1,9},{2,10},{3,11},{4,12},{5,13},{6,14},{7,15},{8,0},{9,1},... | collective-permute-start | bytes 393224 | tf_op jit(solution)/shard_map/ppermute | solution.py:48
  27.8 0.2 broadcast_in_dim.91
  28.0 7.0 %collective-permute-done.5 = bf16[128,512]{1,0:T(8,128)(2,1)S(1)} collective-permute-done((bf16[128,512]{1,0:T(8,128)(2,1)S(1)}, bf16[128,512]{1,0:T(8,128)(2,1)S(1)}, u32[]{:S(2)}, u32[]{:S(2)}) %collective-permute-start.5) | collective-permute-done | bytes 131104 | tf_op jit(solution)/shard_map/ppermute | solution.py:48
  35.0 0.0 collective-permute-done.9
  35.0 0.2 bitcast_dynamic-update-slice_fusion.16
  35.2 0.1 collective-permute-start.10
  35.3 1.2 %collective-permute-start.11 = (bf16[128,512]{1,0:T(8,128)(2,1)S(1)}, bf16[128,512]{1,0:T(8,128)(2,1)S(1)}, u32[]{:S(2)}, u32[]{:S(2)}) collective-permute-start(bf16[128,512]{1,0:T(8,128)(2,1)S(1)} %get-tuple-element.96), channel_id=1, source_target_pairs={{0,2},{1,3},{2,0},{3,1},{4,6},{5,7},{6,4},{7,5},{8,10},{9,11},{10,... | collective-permute-start | bytes 393224 | tf_op jit(solution)/shard_map/ppermute | solution.py:48
  36.5 2.7 %collective-permute-start.12 = (bf16[128,512]{1,0:T(8,128)(2,1)S(1)}, bf16[128,512]{1,0:T(8,128)(2,1)S(1)}, u32[]{:S(2)}, u32[]{:S(2)}) collective-permute-start(bf16[128,512]{1,0:T(8,128)(2,1)S(1)} %get-tuple-element.96), channel_id=1, source_target_pairs={{0,4},{1,5},{2,6},{3,7},{4,0},{5,1},{6,2},{7,3},{8,12},{9,13},{10,... | collective-permute-start | bytes 393224 | tf_op jit(solution)/shard_map/ppermute | solution.py:48
  39.3 0.8 %collective-permute-start.19 = (bf16[128,512]{1,0:T(8,128)(2,1)S(1)}, bf16[128,512]{1,0:T(8,128)(2,1)S(1)}, u32[]{:S(2)}, u32[]{:S(2)}) collective-permute-start(bf16[128,512]{1,0:T(8,128)(2,1)S(1)} %get-tuple-element.96), channel_id=1, source_target_pairs={{0,6},{1,7},{2,4},{3,5},{4,2},{5,3},{6,0},{7,1},{8,14},{9,15},{10,... | collective-permute-start | bytes 393224 | tf_op jit(solution)/shard_map/ppermute | solution.py:48
  40.2 0.0 collective-permute-done.13
  40.2 1.6 %collective-permute-start.17 = (bf16[128,512]{1,0:T(8,128)(2,1)S(1)}, bf16[128,512]{1,0:T(8,128)(2,1)S(1)}, u32[]{:S(2)}, u32[]{:S(2)}) collective-permute-start(bf16[128,512]{1,0:T(8,128)(2,1)S(1)} %get-tuple-element.96), channel_id=1, source_target_pairs={{0,16},{16,0},{1,17},{17,1},{2,18},{18,2},{3,19},{19,3},{4,20},{20... | collective-permute-start | bytes 393224 | tf_op jit(solution)/shard_map/ppermute | solution.py:121
  41.8 1.6 %collective-permute-done.10 = bf16[128,512]{1,0:T(8,128)(2,1)S(1)} collective-permute-done((bf16[128,512]{1,0:T(8,128)(2,1)S(1)}, bf16[128,512]{1,0:T(8,128)(2,1)S(1)}, u32[]{:S(2)}, u32[]{:S(2)}) %collective-permute-start.10) | collective-permute-done | bytes 131104 | tf_op jit(solution)/shard_map/ppermute | solution.py:48
  43.3 0.0 collective-permute-done.11
  43.3 1.3 %collective-permute-done.12 = bf16[128,512]{1,0:T(8,128)(2,1)S(1)} collective-permute-done((bf16[128,512]{1,0:T(8,128)(2,1)S(1)}, bf16[128,512]{1,0:T(8,128)(2,1)S(1)}, u32[]{:S(2)}, u32[]{:S(2)}) %collective-permute-start.12) | collective-permute-done | bytes 131104 | tf_op jit(solution)/shard_map/ppermute | solution.py:48
  44.7 2.9 %collective-permute-start.14 = (bf16[128,512]{1,0:T(8,128)(2,1)S(1)}, bf16[128,512]{1,0:T(8,128)(2,1)S(1)}, u32[]{:S(2)}, u32[]{:S(2)}) collective-permute-start(bf16[128,512]{1,0:T(8,128)(2,1)S(1)} %collective-permute-done.10), channel_id=1, source_target_pairs={{0,2},{1,3},{2,0},{3,1},{4,6},{5,7},{6,4},{7,5},{8,10},{9,11},{10,... | collective-permute-start | bytes 393224 | tf_op jit(solution)/shard_map/ppermute | solution.py:48
  47.6 1.5 %collective-permute-start.16 = (bf16[128,512]{1,0:T(8,128)(2,1)S(1)}, bf16[128,512]{1,0:T(8,128)(2,1)S(1)}, u32[]{:S(2)}, u32[]{:S(2)}) collective-permute-start(bf16[128,512]{1,0:T(8,128)(2,1)S(1)} %collective-permute-done.10), channel_id=1, source_target_pairs={{0,6},{1,7},{2,4},{3,5},{4,2},{5,3},{6,0},{7,1},{8,14},{9,15},{10,... | collective-permute-start | bytes 393224 | tf_op jit(solution)/shard_map/ppermute | solution.py:48
  49.1 0.7 %collective-permute-done.19 = bf16[128,512]{1,0:T(8,128)(2,1)S(1)} collective-permute-done((bf16[128,512]{1,0:T(8,128)(2,1)S(1)}, bf16[128,512]{1,0:T(8,128)(2,1)S(1)}, u32[]{:S(2)}, u32[]{:S(2)}) %collective-permute-start.19) | collective-permute-done | bytes 131104 | tf_op jit(solution)/shard_map/ppermute | solution.py:48
  49.9 0.1 collective-permute-start.20
  49.9 0.0 collective-permute-done.17
  49.9 0.5 collective-permute-start.18
  50.4 0.1 broadcast.52.clone
  50.6 1.2 %collective-permute-done.20 = bf16[4,128,512]{2,1,0:T(8,128)(2,1)S(1)} collective-permute-done((bf16[4,128,512]{2,1,0:T(8,128)(2,1)S(1)}, bf16[4,128,512]{2,1,0:T(8,128)(2,1)S(1)}, u32[]{:S(2)}, u32[]{:S(2)}) %collective-permute-start.20) | collective-permute-done | bytes 524320 | tf_op jit(solution)/shard_map/ppermute | solution.py:48
  51.9 0.0 copy-start.3
  51.9 0.5 fusion.11
  52.4 0.2 collective-permute-done.18
  52.6 0.5 copy-done.3
  53.1 0.9 %fusion.12 = bf16[256,1024]{1,0:T(8,128)(2,1)S(1)} fusion(f32[256,1024]{1,0:T(8,128)S(1)} %fusion.11, bf16[256,512]{1,0:T(8,128)(2,1)S(1)} %bitcast.122, bf16[2,1024,512]{2,1,0:T(8,128)(2,1)S(1)} %bitcast.116, s32[]{:T(128)S(6)} %select_n.91, s32[1024]{0:T(1024)S(1)} %iota_subtract_fusion.1, s32[256]{0:T(256)S(1)} %iota_subtract_fusion.2, ...), kind=kOutput, calls=%fused_computation.19 | convolution fusion | flops 272629760 | bytes 4986885 | tf_op jit(solution)/shard_map/dot_general | solution.py:143
  54.0 0.7 %fusion.4 = f32[256,1024]{1,0:T(8,128)S(1)} fusion(bf16[256,512]{1,0:T(8,128)(2,1)S(1)} %bitcast.123, bf16[2,1024,512]{2,1,0:T(8,128)(2,1)S(1)} %bitcast.117, s32[]{:T(128)S(6)} %xor.23, pred[]{:T(512)S(6)} %eq.36, bf16[256,2048]{1,0:T(8,128)(2,1)S(1)} %bitcast.127, bf16[256,2048]{1,0:T(8,128)(2,1)S(1)} %bitcast.113), kind=kOutput, calls=%fused_computation.11 | convolution fusion | flops 271056896 | bytes 4456453 | tf_op jit(solution)/shard_map/dot_general | solution.py:143
  54.9 0.2 collective-permute-start.21
  55.1 0.1 broadcast.52
  55.2 1.6 %collective-permute-done.21 = bf16[4,128,512]{2,1,0:T(8,128)(2,1)S(1)} collective-permute-done((bf16[4,128,512]{2,1,0:T(8,128)(2,1)S(1)}, bf16[4,128,512]{2,1,0:T(8,128)(2,1)S(1)}, u32[]{:S(2)}, u32[]{:S(2)}) %collective-permute-start.21) | collective-permute-done | bytes 524320 | tf_op jit(solution)/shard_map/ppermute | solution.py:48
  56.9 0.5 convolution_multiply_fusion
  57.4 0.3 broadcast_select_fusion.1
  57.7 0.1 broadcast_select_fusion
  57.8 1.1 %maximum_bitcast_fusion = bf16[1,256,2048]{2,1,0:T(8,128)(2,1)} fusion(bf16[256,1024]{1,0:T(8,128)(2,1)S(1)} %broadcast_select_fusion, bf16[256,1024]{1,0:T(8,128)(2,1)S(1)} %get-tuple-element.93), kind=kLoop, calls=%fused_computation.21 | loop fusion | flops 2097152 | bytes 2097152 | tf_op jit(solution)/shard_map/broadcast_in_dim | solution.py:183
  (46 shorter events, 0.8 us)
Async XLA Ops:
  0.0 2.2 %copy-start.2 = (s32[1024,256]{1,0:T(8,128)S(1)}, s32[1024,256]{1,0:T(8,128)}, u32[]{:S(2)}) copy-start(s32[1024,256]{1,0:T(8,128)} %param.8) | copy-start | bytes 3145732
  0.0 2.2 %copy-start.4 = (s32[512]{0:T(512)S(1)}, s32[512]{0:T(512)}, u32[]{:S(2)}) copy-start(s32[512]{0:T(512)} %param.9) | copy-start | bytes 6148
  1.6 1.5 %copy-start = (bf16[1,256,2048]{2,1,0:T(8,128)(2,1)S(1)}, bf16[1,256,2048]{2,1,0:T(8,128)(2,1)}, u32[]{:S(2)}) copy-start(bf16[1,256,2048]{2,1,0:T(8,128)(2,1)} %param.5) | copy-start | bytes 3145732
  1.7 2.9 %collective-permute-start = (bf16[256,1024]{0,1:T(8,128)(2,1)S(1)}, bf16[256,1024]{0,1:T(8,128)(2,1)S(1)}, u32[]{:S(2)}, u32[]{:S(2)}) collective-permute-start(bf16[256,1024]{0,1:T(8,128)(2,1)S(1)} %bitcast.121), channel_id=1, source_target_pairs={{0,1},{1,0},{2,3},{3,2},{4,5},{5,4},{6,7},{7,6},{8,9},{9,8},{10,11... | collective-permute-start | bytes 1572872 | tf_op jit(solution)/shard_map/ppermute | solution.py:48
  2.9 1.6 %collective-permute-start.1 = (bf16[256,512]{1,0:T(8,128)(2,1)S(1)}, bf16[256,512]{1,0:T(8,128)(2,1)S(1)}, u32[]{:S(2)}, u32[]{:S(2)}) collective-permute-start(bf16[256,512]{1,0:T(8,128)(2,1)S(1)} %fusion.13), channel_id=1, source_target_pairs={{0,1},{1,0},{2,3},{3,2},{4,5},{5,4},{6,7},{7,6},{8,9},{9,8},{10,11... | collective-permute-start | bytes 786440 | tf_op jit(solution)/shard_map/ppermute | solution.py:48
  5.3 9.8 %collective-permute-start.3 = (bf16[2,128,512]{2,1,0:T(8,128)(2,1)S(1)}, bf16[2,128,512]{2,1,0:T(8,128)(2,1)S(1)}, u32[]{:S(2)}, u32[]{:S(2)}) collective-permute-start(bf16[2,128,512]{2,1,0:T(8,128)(2,1)S(1)} %pad_maximum_fusion), channel_id=1, source_target_pairs={{0,2},{1,3},{2,0},{3,1},{4,6},{5,7},{6,4},{7,5},{8,10},{9,11},{10,... | collective-permute-start | bytes 786440 | tf_op jit(solution)/shard_map/ppermute | solution.py:48
  8.0 12.4 %collective-permute-start.6 = (bf16[128,512]{1,0:T(8,128)(2,1)S(1)}, bf16[128,512]{1,0:T(8,128)(2,1)S(1)}, u32[]{:S(2)}, u32[]{:S(2)}) collective-permute-start(bf16[128,512]{1,0:T(8,128)(2,1)S(1)} %dynamic-slice_bitcast_fusion.1), channel_id=1, source_target_pairs={{0,4},{1,5},{2,6},{3,7},{4,0},{5,1},{6,2},{7,3},{8,12},{9,13},{10,... | collective-permute-start | bytes 393224 | tf_op jit(solution)/shard_map/ppermute | solution.py:48
  9.6 12.9 %collective-permute-start.7 = (bf16[128,512]{1,0:T(8,128)(2,1)S(1)}, bf16[128,512]{1,0:T(8,128)(2,1)S(1)}, u32[]{:S(2)}, u32[]{:S(2)}) collective-permute-start(bf16[128,512]{1,0:T(8,128)(2,1)S(1)} %dynamic-slice_bitcast_fusion.1), channel_id=1, source_target_pairs={{0,8},{1,9},{2,10},{3,11},{4,12},{5,13},{6,14},{7,15},{8,0},{9,1},... | collective-permute-start | bytes 393224 | tf_op jit(solution)/shard_map/ppermute | solution.py:48
  12.2 10.4 %collective-permute-start.8 = (bf16[128,512]{1,0:T(8,128)(2,1)S(1)}, bf16[128,512]{1,0:T(8,128)(2,1)S(1)}, u32[]{:S(2)}, u32[]{:S(2)}) collective-permute-start(bf16[128,512]{1,0:T(8,128)(2,1)S(1)} %dynamic-slice_bitcast_fusion.1), channel_id=1, source_target_pairs={{0,12},{1,13},{2,14},{3,15},{4,8},{5,9},{6,10},{7,11},{8,4},{9,5},... | collective-permute-start | bytes 393224 | tf_op jit(solution)/shard_map/ppermute | solution.py:48
  12.4 8.1 %collective-permute-start.2 = (bf16[2,128,512]{2,1,0:T(8,128)(2,1)S(1)}, bf16[2,128,512]{2,1,0:T(8,128)(2,1)S(1)}, u32[]{:S(2)}, u32[]{:S(2)}) collective-permute-start(bf16[2,128,512]{2,1,0:T(8,128)(2,1)S(1)} %pad_maximum_fusion.1), channel_id=1, source_target_pairs={{0,2},{1,3},{2,0},{3,1},{4,6},{5,7},{6,4},{7,5},{8,10},{9,11},{10,... | collective-permute-start | bytes 786440 | tf_op jit(solution)/shard_map/ppermute | solution.py:48
  15.3 11.2 %collective-permute-start.4 = (bf16[2,128,512]{2,1,0:T(8,128)(2,1)S(1)}, bf16[2,128,512]{2,1,0:T(8,128)(2,1)S(1)}, u32[]{:S(2)}, u32[]{:S(2)}) collective-permute-start(bf16[2,128,512]{2,1,0:T(8,128)(2,1)S(1)} %fusion.21), channel_id=1, source_target_pairs={{0,4},{1,5},{2,6},{3,7},{4,0},{5,1},{6,2},{7,3},{8,12},{9,13},{10,... | collective-permute-start | bytes 786440 | tf_op jit(solution)/shard_map/ppermute | solution.py:48
  22.6 12.3 %collective-permute-start.9 = (bf16[4,128,512]{2,1,0:T(8,128)(2,1)S(1)}, bf16[4,128,512]{2,1,0:T(8,128)(2,1)S(1)}, u32[]{:S(2)}, u32[]{:S(2)}) collective-permute-start(bf16[4,128,512]{2,1,0:T(8,128)(2,1)S(1)} %bitcast_dynamic-update-slice_fusion.18), channel_id=1, source_target_pairs={{0,1},{1,0},{2,3},{3,2},{4,5},{5,4},{6,7},{7,6},{8,9},{9,8},{10,11... | collective-permute-start | bytes 1572872 | tf_op jit(solution)/shard_map/ppermute | solution.py:48
  22.7 17.4 %collective-permute-start.13 = (bf16[4,128,512]{2,1,0:T(8,128)(2,1)S(1)}, bf16[4,128,512]{2,1,0:T(8,128)(2,1)S(1)}, u32[]{:S(2)}, u32[]{:S(2)}) collective-permute-start(bf16[4,128,512]{2,1,0:T(8,128)(2,1)S(1)} %bitcast_dynamic-update-slice_fusion.18), channel_id=1, source_target_pairs={{0,2},{1,3},{2,0},{3,1},{4,6},{5,7},{6,4},{7,5},{8,10},{9,11},{10,... | collective-permute-start | bytes 1572872 | tf_op jit(solution)/shard_map/ppermute | solution.py:48
  26.6 8.5 %copy-start.1 = (f32[1,128]{1,0:T(1,128)S(1)}, f32[1,128]{1,0:T(1,128)}, u32[]{:S(2)}) copy-start(f32[1,128]{1,0:T(1,128)} %param.7) | copy-start | bytes 1540
  26.6 8.4 %collective-permute-start.5 = (bf16[128,512]{1,0:T(8,128)(2,1)S(1)}, bf16[128,512]{1,0:T(8,128)(2,1)S(1)}, u32[]{:S(2)}, u32[]{:S(2)}) collective-permute-start(bf16[128,512]{1,0:T(8,128)(2,1)S(1)} %fusion.35), channel_id=1, source_target_pairs={{0,8},{1,9},{2,10},{3,11},{4,12},{5,13},{6,14},{7,15},{8,0},{9,1},... | collective-permute-start | bytes 393224 | tf_op jit(solution)/shard_map/ppermute | solution.py:48
  35.2 8.1 %collective-permute-start.10 = (bf16[128,512]{1,0:T(8,128)(2,1)S(1)}, bf16[128,512]{1,0:T(8,128)(2,1)S(1)}, u32[]{:S(2)}, u32[]{:S(2)}) collective-permute-start(bf16[128,512]{1,0:T(8,128)(2,1)S(1)} %get-tuple-element.96), channel_id=1, source_target_pairs={{0,8},{1,9},{2,10},{3,11},{4,12},{5,13},{6,14},{7,15},{8,0},{9,1},... | collective-permute-start | bytes 393224 | tf_op jit(solution)/shard_map/ppermute | solution.py:48
  35.3 8.0 %collective-permute-start.11 = (bf16[128,512]{1,0:T(8,128)(2,1)S(1)}, bf16[128,512]{1,0:T(8,128)(2,1)S(1)}, u32[]{:S(2)}, u32[]{:S(2)}) collective-permute-start(bf16[128,512]{1,0:T(8,128)(2,1)S(1)} %get-tuple-element.96), channel_id=1, source_target_pairs={{0,2},{1,3},{2,0},{3,1},{4,6},{5,7},{6,4},{7,5},{8,10},{9,11},{10,... | collective-permute-start | bytes 393224 | tf_op jit(solution)/shard_map/ppermute | solution.py:48
  36.5 8.1 %collective-permute-start.12 = (bf16[128,512]{1,0:T(8,128)(2,1)S(1)}, bf16[128,512]{1,0:T(8,128)(2,1)S(1)}, u32[]{:S(2)}, u32[]{:S(2)}) collective-permute-start(bf16[128,512]{1,0:T(8,128)(2,1)S(1)} %get-tuple-element.96), channel_id=1, source_target_pairs={{0,4},{1,5},{2,6},{3,7},{4,0},{5,1},{6,2},{7,3},{8,12},{9,13},{10,... | collective-permute-start | bytes 393224 | tf_op jit(solution)/shard_map/ppermute | solution.py:48
  39.3 10.6 %collective-permute-start.19 = (bf16[128,512]{1,0:T(8,128)(2,1)S(1)}, bf16[128,512]{1,0:T(8,128)(2,1)S(1)}, u32[]{:S(2)}, u32[]{:S(2)}) collective-permute-start(bf16[128,512]{1,0:T(8,128)(2,1)S(1)} %get-tuple-element.96), channel_id=1, source_target_pairs={{0,6},{1,7},{2,4},{3,5},{4,2},{5,3},{6,0},{7,1},{8,14},{9,15},{10,... | collective-permute-start | bytes 393224 | tf_op jit(solution)/shard_map/ppermute | solution.py:48
  40.2 9.8 %collective-permute-start.17 = (bf16[128,512]{1,0:T(8,128)(2,1)S(1)}, bf16[128,512]{1,0:T(8,128)(2,1)S(1)}, u32[]{:S(2)}, u32[]{:S(2)}) collective-permute-start(bf16[128,512]{1,0:T(8,128)(2,1)S(1)} %get-tuple-element.96), channel_id=1, source_target_pairs={{0,16},{16,0},{1,17},{17,1},{2,18},{18,2},{3,19},{19,3},{4,20},{20... | collective-permute-start | bytes 393224 | tf_op jit(solution)/shard_map/ppermute | solution.py:121
  44.7 10.1 %collective-permute-start.14 = (bf16[128,512]{1,0:T(8,128)(2,1)S(1)}, bf16[128,512]{1,0:T(8,128)(2,1)S(1)}, u32[]{:S(2)}, u32[]{:S(2)}) collective-permute-start(bf16[128,512]{1,0:T(8,128)(2,1)S(1)} %collective-permute-done.10), channel_id=1, source_target_pairs={{0,2},{1,3},{2,0},{3,1},{4,6},{5,7},{6,4},{7,5},{8,10},{9,11},{10,... | collective-permute-start | bytes 393224 | tf_op jit(solution)/shard_map/ppermute | solution.py:48
  47.6 7.1 %collective-permute-start.15 = (bf16[128,512]{1,0:T(8,128)(2,1)S(1)}, bf16[128,512]{1,0:T(8,128)(2,1)S(1)}, u32[]{:S(2)}, u32[]{:S(2)}) collective-permute-start(bf16[128,512]{1,0:T(8,128)(2,1)S(1)} %collective-permute-done.10), channel_id=1, source_target_pairs={{0,4},{1,5},{2,6},{3,7},{4,0},{5,1},{6,2},{7,3},{8,12},{9,13},{10,... | collective-permute-start | bytes 393224 | tf_op jit(solution)/shard_map/ppermute | solution.py:48
  47.6 7.1 %collective-permute-start.16 = (bf16[128,512]{1,0:T(8,128)(2,1)S(1)}, bf16[128,512]{1,0:T(8,128)(2,1)S(1)}, u32[]{:S(2)}, u32[]{:S(2)}) collective-permute-start(bf16[128,512]{1,0:T(8,128)(2,1)S(1)} %collective-permute-done.10), channel_id=1, source_target_pairs={{0,6},{1,7},{2,4},{3,5},{4,2},{5,3},{6,0},{7,1},{8,14},{9,15},{10,... | collective-permute-start | bytes 393224 | tf_op jit(solution)/shard_map/ppermute | solution.py:48
  49.9 2.0 %collective-permute-start.20 = (bf16[4,128,512]{2,1,0:T(8,128)(2,1)S(1)}, bf16[4,128,512]{2,1,0:T(8,128)(2,1)S(1)}, u32[]{:S(2)}, u32[]{:S(2)}) collective-permute-start(bf16[4,128,512]{2,1,0:T(8,128)(2,1)S(1)} %bitcast_dynamic-update-slice_fusion.12), channel_id=1, source_target_pairs={{0,1},{1,0},{2,3},{3,2},{4,5},{5,4},{6,7},{7,6},{8,9},{9,8},{10,11... | collective-permute-start | bytes 1572872 | tf_op jit(solution)/shard_map/ppermute | solution.py:48
  49.9 2.6 %collective-permute-start.18 = (bf16[4,128,512]{2,1,0:T(8,128)(2,1)S(1)}, bf16[4,128,512]{2,1,0:T(8,128)(2,1)S(1)}, u32[]{:S(2)}, u32[]{:S(2)}) collective-permute-start(bf16[4,128,512]{2,1,0:T(8,128)(2,1)S(1)} %collective-permute-done.13), channel_id=1, source_target_pairs={{0,1},{1,0},{2,3},{3,2},{4,5},{5,4},{6,7},{7,6},{8,9},{9,8},{10,11... | collective-permute-start | bytes 1572872 | tf_op jit(solution)/shard_map/ppermute | solution.py:48
  51.9 1.2 %copy-start.3 = (bf16[1,256,2048]{2,1,0:T(8,128)(2,1)S(1)}, bf16[1,256,2048]{2,1,0:T(8,128)(2,1)}, u32[]{:S(2)}) copy-start(bf16[1,256,2048]{2,1,0:T(8,128)(2,1)} %param.6) | copy-start | bytes 3145732
  54.9 2.0 %collective-permute-start.21 = (bf16[4,128,512]{2,1,0:T(8,128)(2,1)S(1)}, bf16[4,128,512]{2,1,0:T(8,128)(2,1)S(1)}, u32[]{:S(2)}, u32[]{:S(2)}) collective-permute-start(bf16[4,128,512]{2,1,0:T(8,128)(2,1)S(1)} %bitcast_dynamic-update-slice_fusion.8), channel_id=1, source_target_pairs={{0,1},{1,0},{2,3},{3,2},{4,5},{5,4},{6,7},{7,6},{8,9},{9,8},{10,11... | collective-permute-start | bytes 1572872 | tf_op jit(solution)/shard_map/ppermute | solution.py:48

commit v7 on v6

--- a/solution.py
+++ b/solution.py
@@ -35,11 +35,9 @@
         line=[line_idx ^ step for step in range(n_line)],
         quad=[item_idx // 2 % 4 ^ step for step in range(4)],
         high=[high_idx ^ step for step in range(n_high)],
-        is_high=[[high_idx ^ step == block for block in range(n_high)] for step in range(n_high)],
         source=[(resp_idx - step) % n_resp for step in range(n_resp)],
         own_start=resp_idx * sub_len,
         item_col=item_idx * sub_len,
-        low_col=item_idx % 8 * sub_len,
     )
     indices, where = lax.optimization_barrier((indices, where))
     own_start = where["own_start"]
@@ -135,52 +133,34 @@
         row_res = put_at(row_res, block[None], index)
     row_res = row_res.reshape(item_dev, batch)
 
-    row_ids = lax.broadcasted_iota(jnp.int32, (item_dev, width), 0) - own_start
-    col_ids = lax.broadcasted_iota(jnp.int32, (item_dev, width), 1) - where["low_col"]
+    row_ids = lax.broadcasted_iota(jnp.int32, couple.shape, 0) - own_start
+    col_ids = lax.broadcasted_iota(jnp.int32, couple.shape, 1) - where["item_col"]
     on_diag = (row_ids == col_ids) & (row_ids >= 0) & (row_ids < sub_len)
 
-    def product(left, right, step):
+    def product(left, right):
+        right = right.reshape(-1, batch)
         grad = lax.dot_general(left, right, NT, preferred_element_type=jnp.float32)
-        return jnp.where(on_diag, 0.0, grad) if step == 0 else grad
+        return jnp.where(on_diag, 0.0, grad)
 
-    def pick(blocks, step):
-        picked = blocks[0]
-        for index in range(1, n_high):
-            picked = jnp.where(where["is_high"][step][index], blocks[index], picked)
-        return picked
+    current = couple.astype(jnp.float32)
+    base = current + DRIFT * (DATA_RATIO * (product(row_res, all_spins) * inv_root) - current)
+    base = base + NOISE_SCALE * noise[0].astype(jnp.float32)
 
-    def pick_part(parts, block):
-        picked = parts[0]
-        for step in range(1, n_high):
-            picked = jnp.where(where["is_high"][step][block], parts[step], picked)
-        return picked
-
-    couple_blocks = jnp.split(couple, n_high, axis=1)
-    noise_blocks = jnp.split(noise[0], n_high, axis=1)
-    parts = []
+    all_res = jnp.zeros((n_high, 4, 2, sub_len, batch), jnp.bfloat16)
     for step in range(n_high):
-        current = pick(couple_blocks, step).astype(jnp.float32)
-        shake = pick(noise_blocks, step).astype(jnp.float32)
-        mirror = product(row_res, take(all_spins, where["high"][step], 0), step) * inv_root
-        base = current + DRIFT * (DATA_RATIO * mirror - current) + NOISE_SCALE * shake
-
         if step:
             blocks = [far[step - 1]] + [swap(far[step - 1], bits) for bits in (2, 4, 6)]
         else:
             blocks = [residual] + near
         if step == n_high - 1:
-            blocks, base, parts = lax.optimization_barrier((blocks, base, parts))
+            blocks, base, all_res = lax.optimization_barrier((blocks, base, all_res))
         quad = jnp.zeros((4, sub_len, batch), jnp.bfloat16)
         for index, block in zip(where["quad"], blocks):
             quad = put_at(quad, block[None], index)
-        peers = swap(quad, 1)
-        all_res = jnp.zeros((4, 2, sub_len, batch), jnp.bfloat16)
-        all_res = put_at(all_res, quad[:, None], 0, where["core"])
-        all_res = put_at(all_res, peers[:, None], 0, where["other_core"])
-        part = product(spins, all_res.reshape(width, batch), step)
-        part = base + (DRIFT * DATA_RATIO * inv_root) * part
-        parts.append(part.astype(jnp.bfloat16))
-    return jnp.concatenate([pick_part(parts, i) for i in range(n_high)], axis=1)[None]
+        for core, group in (("core", quad), ("other_core", swap(quad, 1))):
+            all_res = put_at(all_res, group[None, :, None], where["high"][step], 0, where[core])
+    change = (DRIFT * DATA_RATIO * inv_root) * product(spins, all_res)
+    return (base + change).astype(jnp.bfloat16)[None]
 
 
 def solution(mesh):

time: 59 us -> 58.7 us (level)
  waiting for transfers between devices: 24.8 us -> 25.4 us
    dot_general x4 -> x2, matrix products: 2.56 us -> 2.09 us  [product(): grad = lax.dot_general(left, right, NT, preferred_element_type=jnp.float32)]
  transfers between devices with their start and end apart: 22 -> 22, of which waited for: 12 -> 12; matrix products, arithmetic and copies ran while one was open for 8% -> 7% of each run, Pallas kernels for 0% -> 0%
where the time goes in v7:
time: 58.7 us; the launch traced here: 58.5 us
  waiting for transfers between devices  25.4 us (43%)
  starting transfers between devices  23.9 us (41%)
  matrix products  3.67 us (6%)
  local copies, waits for them, and re-layouts  3.07 us (5%)
  other arithmetic  2.1 us (4%)
    ppermute x21, waiting for transfers between devices, swap(): return lax.ppermute(array, 'item', [(i, i ^ bits) for i in range(n_item)])  25.4 us
    ppermute x21, starting transfers between devices, swap(): return lax.ppermute(array, 'item', [(i, i ^ bits) for i in range(n_item)])  22.4 us
    dot_general x2, matrix products, product(): grad = lax.dot_general(left, right, NT, preferred_element_type=jnp.float32)  2.09 us
    unnamed x11, local copies, waits for them, and re-layouts  1.59 us
    ppermute x1, starting transfers between devices, shards(): others.append(lax.ppermute(residual, 'resp', ring))  1.53 us
    broadcast_in_dim x1, other arithmetic, shards(): return (base + change).astype(jnp.bfloat16)[None]  1.23 us
  transfers between devices with their start and end apart: 22, of which 12 were waited for; matrix products, arithmetic and copies ran while one was open for 7% of the time, Pallas kernels for 0%

profile of v7, /device:TPU:0, one launch (start us, length us, event | category | flops | bytes accessed | tf_op | source)
XLA Modules:
  0.0 58.5 jit_solution(6881745165939071039)
XLA Ops:
  0.0 1.6 %copy.14 = bf16[1,256,2048]{1,2,0:T(8,128)(2,1)S(1)} copy(bf16[1,256,2048]{2,1,0:T(8,128)(2,1)} %param.5) | data formatting | bytes 2097152 | tf_op args[0]
  1.6 0.0 copy-start
  1.6 0.1 constant_dynamic-slice_fusion.9
  1.7 0.5 collective-permute-start
  2.2 0.7 %fusion.7 = bf16[256,512]{1,0:T(8,128)(2,1)S(1)} fusion(s32[512]{0:T(512)S(1)} %copy-done.4, s32[1024,256]{1,0:T(8,128)S(1)} %copy-done.2), kind=kOutput, calls=%fused_computation.16 | convolution fusion | flops 269877248 | bytes 1312768 | tf_op jit(solution)/shard_map/dot_general | solution.py:63
  2.9 0.1 collective-permute-start.1
  3.1 0.4 fusion.4
  3.5 0.4 fusion.33
  4.0 0.6 collective-permute-done.1
  4.5 0.0 collective-permute-done
  4.5 0.4 convolution_add_fusion
  5.0 0.1 fusion.10
  5.1 0.1 dynamic-slice_bitcast_fusion
  5.2 0.1 constant_dynamic-slice_fusion.4
  5.3 2.7 %collective-permute-start.3 = (bf16[2,128,512]{2,1,0:T(8,128)(2,1)S(1)}, bf16[2,128,512]{2,1,0:T(8,128)(2,1)S(1)}, u32[]{:S(2)}, u32[]{:S(2)}) collective-permute-start(bf16[2,128,512]{2,1,0:T(8,128)(2,1)S(1)} %pad_maximum_fusion), channel_id=1, source_target_pairs={{0,2},{1,3},{2,0},{3,1},{4,6},{5,7},{6,4},{7,5},{8,10},{9,11},{10,... | collective-permute-start | bytes 786440 | tf_op jit(solution)/shard_map/ppermute | solution.py:46
  8.0 1.6 %collective-permute-start.6 = (bf16[128,512]{1,0:T(8,128)(2,1)S(1)}, bf16[128,512]{1,0:T(8,128)(2,1)S(1)}, u32[]{:S(2)}, u32[]{:S(2)}) collective-permute-start(bf16[128,512]{1,0:T(8,128)(2,1)S(1)} %dynamic-slice_bitcast_fusion.1), channel_id=1, source_target_pairs={{0,4},{1,5},{2,6},{3,7},{4,0},{5,1},{6,2},{7,3},{8,12},{9,13},{10,... | collective-permute-start | bytes 393224 | tf_op jit(solution)/shard_map/ppermute | solution.py:46
  9.6 2.6 %collective-permute-start.7 = (bf16[128,512]{1,0:T(8,128)(2,1)S(1)}, bf16[128,512]{1,0:T(8,128)(2,1)S(1)}, u32[]{:S(2)}, u32[]{:S(2)}) collective-permute-start(bf16[128,512]{1,0:T(8,128)(2,1)S(1)} %dynamic-slice_bitcast_fusion.1), channel_id=1, source_target_pairs={{0,8},{1,9},{2,10},{3,11},{4,12},{5,13},{6,14},{7,15},{8,0},{9,1},... | collective-permute-start | bytes 393224 | tf_op jit(solution)/shard_map/ppermute | solution.py:46
  12.2 0.2 collective-permute-start.8
  12.4 0.3 collective-permute-start.2
  12.7 0.1 constant_dynamic-slice_fusion.2
  12.8 2.3 %collective-permute-done.3 = bf16[2,128,512]{2,1,0:T(8,128)(2,1)S(1)} collective-permute-done((bf16[2,128,512]{2,1,0:T(8,128)(2,1)S(1)}, bf16[2,128,512]{2,1,0:T(8,128)(2,1)S(1)}, u32[]{:S(2)}, u32[]{:S(2)}) %collective-permute-start.3) | collective-permute-done | bytes 262176 | tf_op jit(solution)/shard_map/ppermute | solution.py:46
  15.2 0.1 fusion.12
  15.3 2.1 %collective-permute-start.4 = (bf16[2,128,512]{2,1,0:T(8,128)(2,1)S(1)}, bf16[2,128,512]{2,1,0:T(8,128)(2,1)S(1)}, u32[]{:S(2)}, u32[]{:S(2)}) collective-permute-start(bf16[2,128,512]{2,1,0:T(8,128)(2,1)S(1)} %fusion.12), channel_id=1, source_target_pairs={{0,4},{1,5},{2,6},{3,7},{4,0},{5,1},{6,2},{7,3},{8,12},{9,13},{10,... | collective-permute-start | bytes 786440 | tf_op jit(solution)/shard_map/ppermute | solution.py:46
  17.4 3.1 %collective-permute-done.2 = bf16[2,128,512]{2,1,0:T(8,128)(2,1)S(1)} collective-permute-done((bf16[2,128,512]{2,1,0:T(8,128)(2,1)S(1)}, bf16[2,128,512]{2,1,0:T(8,128)(2,1)S(1)}, u32[]{:S(2)}, u32[]{:S(2)}) %collective-permute-start.2) | collective-permute-done | bytes 262176 | tf_op jit(solution)/shard_map/ppermute | solution.py:46
  20.5 0.0 collective-permute-done.6
  20.5 2.1 %collective-permute-done.7 = bf16[128,512]{1,0:T(8,128)(2,1)S(1)} collective-permute-done((bf16[128,512]{1,0:T(8,128)(2,1)S(1)}, bf16[128,512]{1,0:T(8,128)(2,1)S(1)}, u32[]{:S(2)}, u32[]{:S(2)}) %collective-permute-start.7) | collective-permute-done | bytes 131104 | tf_op jit(solution)/shard_map/ppermute | solution.py:46
  22.6 0.0 collective-permute-done.8
  22.6 0.1 collective-permute-start.9
  22.7 0.6 %collective-permute-start.13 = (bf16[4,128,512]{2,1,0:T(8,128)(2,1)S(1)}, bf16[4,128,512]{2,1,0:T(8,128)(2,1)S(1)}, u32[]{:S(2)}, u32[]{:S(2)}) collective-permute-start(bf16[4,128,512]{2,1,0:T(8,128)(2,1)S(1)} %bitcast_dynamic-update-slice_fusion.18), channel_id=1, source_target_pairs={{0,2},{1,3},{2,0},{3,1},{4,6},{5,7},{6,4},{7,5},{8,10},{9,11},{10,... | collective-permute-start | bytes 1572872 | tf_op jit(solution)/shard_map/ppermute | solution.py:46
  23.3 3.1 %collective-permute-done.4 = bf16[2,128,512]{2,1,0:T(8,128)(2,1)S(1)} collective-permute-done((bf16[2,128,512]{2,1,0:T(8,128)(2,1)S(1)}, bf16[2,128,512]{2,1,0:T(8,128)(2,1)S(1)}, u32[]{:S(2)}, u32[]{:S(2)}) %collective-permute-start.4) | collective-permute-done | bytes 262176 | tf_op jit(solution)/shard_map/ppermute | solution.py:46
  26.5 0.1 fusion.11
  26.6 0.0 copy-start.1
  26.6 1.2 %collective-permute-start.5 = (bf16[128,512]{1,0:T(8,128)(2,1)S(1)}, bf16[128,512]{1,0:T(8,128)(2,1)S(1)}, u32[]{:S(2)}, u32[]{:S(2)}) collective-permute-start(bf16[128,512]{1,0:T(8,128)(2,1)S(1)} %fusion.26), channel_id=1, source_target_pairs={{0,8},{1,9},{2,10},{3,11},{4,12},{5,13},{6,14},{7,15},{8,0},{9,1},... | collective-permute-start | bytes 393224 | tf_op jit(solution)/shard_map/ppermute | solution.py:46
  27.8 0.2 broadcast_in_dim.92
  28.0 7.0 %collective-permute-done.5 = bf16[128,512]{1,0:T(8,128)(2,1)S(1)} collective-permute-done((bf16[128,512]{1,0:T(8,128)(2,1)S(1)}, bf16[128,512]{1,0:T(8,128)(2,1)S(1)}, u32[]{:S(2)}, u32[]{:S(2)}) %collective-permute-start.5) | collective-permute-done | bytes 131104 | tf_op jit(solution)/shard_map/ppermute | solution.py:46
  35.0 0.0 collective-permute-done.9
  35.0 0.2 bitcast_dynamic-update-slice_fusion.16
  35.2 0.1 collective-permute-start.10
  35.3 1.2 %collective-permute-start.11 = (bf16[128,512]{1,0:T(8,128)(2,1)S(1)}, bf16[128,512]{1,0:T(8,128)(2,1)S(1)}, u32[]{:S(2)}, u32[]{:S(2)}) collective-permute-start(bf16[128,512]{1,0:T(8,128)(2,1)S(1)} %get-tuple-element.86), channel_id=1, source_target_pairs={{0,2},{1,3},{2,0},{3,1},{4,6},{5,7},{6,4},{7,5},{8,10},{9,11},{10,... | collective-permute-start | bytes 393224 | tf_op jit(solution)/shard_map/ppermute | solution.py:46
  36.6 2.7 %collective-permute-start.12 = (bf16[128,512]{1,0:T(8,128)(2,1)S(1)}, bf16[128,512]{1,0:T(8,128)(2,1)S(1)}, u32[]{:S(2)}, u32[]{:S(2)}) collective-permute-start(bf16[128,512]{1,0:T(8,128)(2,1)S(1)} %get-tuple-element.86), channel_id=1, source_target_pairs={{0,4},{1,5},{2,6},{3,7},{4,0},{5,1},{6,2},{7,3},{8,12},{9,13},{10,... | collective-permute-start | bytes 393224 | tf_op jit(solution)/shard_map/ppermute | solution.py:46
  39.3 1.5 %collective-permute-start.17 = (bf16[128,512]{1,0:T(8,128)(2,1)S(1)}, bf16[128,512]{1,0:T(8,128)(2,1)S(1)}, u32[]{:S(2)}, u32[]{:S(2)}) collective-permute-start(bf16[128,512]{1,0:T(8,128)(2,1)S(1)} %get-tuple-element.86), channel_id=1, source_target_pairs={{0,16},{16,0},{1,17},{17,1},{2,18},{18,2},{3,19},{19,3},{4,20},{20... | collective-permute-start | bytes 393224 | tf_op jit(solution)/shard_map/ppermute | solution.py:119
  40.9 0.0 collective-permute-done.13
  40.9 0.9 %collective-permute-start.19 = (bf16[128,512]{1,0:T(8,128)(2,1)S(1)}, bf16[128,512]{1,0:T(8,128)(2,1)S(1)}, u32[]{:S(2)}, u32[]{:S(2)}) collective-permute-start(bf16[128,512]{1,0:T(8,128)(2,1)S(1)} %get-tuple-element.86), channel_id=1, source_target_pairs={{0,6},{1,7},{2,4},{3,5},{4,2},{5,3},{6,0},{7,1},{8,14},{9,15},{10,... | collective-permute-start | bytes 393224 | tf_op jit(solution)/shard_map/ppermute | solution.py:46
  41.8 1.6 %collective-permute-done.10 = bf16[128,512]{1,0:T(8,128)(2,1)S(1)} collective-permute-done((bf16[128,512]{1,0:T(8,128)(2,1)S(1)}, bf16[128,512]{1,0:T(8,128)(2,1)S(1)}, u32[]{:S(2)}, u32[]{:S(2)}) %collective-permute-start.10) | collective-permute-done | bytes 131104 | tf_op jit(solution)/shard_map/ppermute | solution.py:46
  43.4 0.0 collective-permute-done.11
  43.4 0.9 %collective-permute-done.12 = bf16[128,512]{1,0:T(8,128)(2,1)S(1)} collective-permute-done((bf16[128,512]{1,0:T(8,128)(2,1)S(1)}, bf16[128,512]{1,0:T(8,128)(2,1)S(1)}, u32[]{:S(2)}, u32[]{:S(2)}) %collective-permute-start.12) | collective-permute-done | bytes 131104 | tf_op jit(solution)/shard_map/ppermute | solution.py:46
  44.2 3.4 %collective-permute-start.14 = (bf16[128,512]{1,0:T(8,128)(2,1)S(1)}, bf16[128,512]{1,0:T(8,128)(2,1)S(1)}, u32[]{:S(2)}, u32[]{:S(2)}) collective-permute-start(bf16[128,512]{1,0:T(8,128)(2,1)S(1)} %collective-permute-done.10), channel_id=1, source_target_pairs={{0,2},{1,3},{2,0},{3,1},{4,6},{5,7},{6,4},{7,5},{8,10},{9,11},{10,... | collective-permute-start | bytes 393224 | tf_op jit(solution)/shard_map/ppermute | solution.py:46
  47.6 0.0 collective-permute-start.15
  47.6 1.5 %collective-permute-start.16 = (bf16[128,512]{1,0:T(8,128)(2,1)S(1)}, bf16[128,512]{1,0:T(8,128)(2,1)S(1)}, u32[]{:S(2)}, u32[]{:S(2)}) collective-permute-start(bf16[128,512]{1,0:T(8,128)(2,1)S(1)} %collective-permute-done.10), channel_id=1, source_target_pairs={{0,6},{1,7},{2,4},{3,5},{4,2},{5,3},{6,0},{7,1},{8,14},{9,15},{10,... | collective-permute-start | bytes 393224 | tf_op jit(solution)/shard_map/ppermute | solution.py:46
  49.1 0.7 %collective-permute-done.19 = bf16[128,512]{1,0:T(8,128)(2,1)S(1)} collective-permute-done((bf16[128,512]{1,0:T(8,128)(2,1)S(1)}, bf16[128,512]{1,0:T(8,128)(2,1)S(1)}, u32[]{:S(2)}, u32[]{:S(2)}) %collective-permute-start.19) | collective-permute-done | bytes 131104 | tf_op jit(solution)/shard_map/ppermute | solution.py:46
  49.8 0.0 collective-permute-start.18
  49.9 0.0 collective-permute-done.17
  49.9 0.6 collective-permute-start.20
  50.5 0.0 copy-start.3
  50.5 0.2 broadcast_in_dim.97
  50.8 1.0 %collective-permute-done.18 = bf16[4,128,512]{2,1,0:T(8,128)(2,1)S(1)} collective-permute-done((bf16[4,128,512]{2,1,0:T(8,128)(2,1)S(1)}, bf16[4,128,512]{2,1,0:T(8,128)(2,1)S(1)}, u32[]{:S(2)}, u32[]{:S(2)}) %collective-permute-start.18) | collective-permute-done | bytes 524320 | tf_op jit(solution)/shard_map/ppermute | solution.py:46
  51.8 1.3 %fusion.3 = f32[256,2048]{1,0:T(8,128)S(1)} fusion(bf16[256,512]{1,0:T(8,128)(2,1)S(1)} %bitcast.112, bf16[2048,512]{1,0:T(8,128)(2,1)S(1)} %bitcast.107, bf16[1,256,2048]{2,1,0:T(8,128)(2,1)S(1)} %copy-done.3, bf16[1,256,2048]{2,1,0:T(8,128)(2,1)S(1)} %copy-done, s32[2048]{0:T(1024)S(1)} %iota_subtract_fusion, s32[256]{0:T(256)S(1)} %iota_subtract_fusion.1, ...), kind=kOutput, calls=%fused_computation.8 | convolution fusion | flops 543162368 | bytes 6563328 | tf_op jit(solution)/shard_map/dot_general | solution.py:142
  53.1 0.0 collective-permute-done.20
  53.2 0.0 collective-permute-done.14
  53.2 1.1 %collective-permute-done.16 = bf16[128,512]{1,0:T(8,128)(2,1)S(1)} collective-permute-done((bf16[128,512]{1,0:T(8,128)(2,1)S(1)}, bf16[128,512]{1,0:T(8,128)(2,1)S(1)}, u32[]{:S(2)}, u32[]{:S(2)}) %collective-permute-start.16) | collective-permute-done | bytes 131104 | tf_op jit(solution)/shard_map/ppermute | solution.py:46
  54.5 0.1 collective-permute-start.21
  54.6 1.8 %collective-permute-done.21 = bf16[4,128,512]{2,1,0:T(8,128)(2,1)S(1)} collective-permute-done((bf16[4,128,512]{2,1,0:T(8,128)(2,1)S(1)}, bf16[4,128,512]{2,1,0:T(8,128)(2,1)S(1)}, u32[]{:S(2)}, u32[]{:S(2)}) %collective-permute-start.21) | collective-permute-done | bytes 524320 | tf_op jit(solution)/shard_map/ppermute | solution.py:46
  56.5 0.8 %fusion.2 = f32[256,2048]{1,0:T(8,128)S(1)} fusion(bf16[256,512]{1,0:T(8,128)(2,1)S(1)} %fusion.7, bf16[2048,512]{1,0:T(8,128)(2,1)S(1)} %bitcast.108, s32[2048]{0:T(1024)S(1)} %iota_subtract_fusion, s32[256]{0:T(256)S(1)} %iota_subtract_fusion.1, pred[256]{0:T(512)(128)(4,1)S(1)} %get-tuple-element.98, pred[256]{0:T(512)(128)(4,1)S(1)} %get-tuple-element.99), kind=kOutput, calls=%fused_computation.7 | convolution fusion | flops 539492352 | bytes 4466176 | tf_op jit(solution)/shard_map/dot_general | solution.py:142
  57.3 1.2 %fusion.8 = bf16[1,256,2048]{2,1,0:T(8,128)(2,1)} fusion(f32[256,2048]{1,0:T(8,128)S(1)} %fusion.3, f32[256,2048]{1,0:T(8,128)S(1)} %fusion.2), kind=kLoop, calls=%fused_computation.17 | loop fusion | flops 1048576 | bytes 5242880 | tf_op jit(solution)/shard_map/broadcast_in_dim | solution.py:163
  (40 shorter events, 0.8 us)
Async XLA Ops:
  0.0 2.2 %copy-start.2 = (s32[1024,256]{1,0:T(8,128)S(1)}, s32[1024,256]{1,0:T(8,128)}, u32[]{:S(2)}) copy-start(s32[1024,256]{1,0:T(8,128)} %param.8) | copy-start | bytes 3145732
  0.0 2.2 %copy-start.4 = (s32[512]{0:T(512)S(1)}, s32[512]{0:T(512)}, u32[]{:S(2)}) copy-start(s32[512]{0:T(512)} %param.9) | copy-start | bytes 6148
  1.6 1.5 %copy-start = (bf16[1,256,2048]{2,1,0:T(8,128)(2,1)S(1)}, bf16[1,256,2048]{2,1,0:T(8,128)(2,1)}, u32[]{:S(2)}) copy-start(bf16[1,256,2048]{2,1,0:T(8,128)(2,1)} %param.5) | copy-start | bytes 3145732
  1.7 2.9 %collective-permute-start = (bf16[256,1024]{0,1:T(8,128)(2,1)S(1)}, bf16[256,1024]{0,1:T(8,128)(2,1)S(1)}, u32[]{:S(2)}, u32[]{:S(2)}) collective-permute-start(bf16[256,1024]{0,1:T(8,128)(2,1)S(1)} %bitcast.111), channel_id=1, source_target_pairs={{0,1},{1,0},{2,3},{3,2},{4,5},{5,4},{6,7},{7,6},{8,9},{9,8},{10,11... | collective-permute-start | bytes 1572872 | tf_op jit(solution)/shard_map/ppermute | solution.py:46
  2.9 1.6 %collective-permute-start.1 = (bf16[256,512]{1,0:T(8,128)(2,1)S(1)}, bf16[256,512]{1,0:T(8,128)(2,1)S(1)}, u32[]{:S(2)}, u32[]{:S(2)}) collective-permute-start(bf16[256,512]{1,0:T(8,128)(2,1)S(1)} %fusion.7), channel_id=1, source_target_pairs={{0,1},{1,0},{2,3},{3,2},{4,5},{5,4},{6,7},{7,6},{8,9},{9,8},{10,11... | collective-permute-start | bytes 786440 | tf_op jit(solution)/shard_map/ppermute | solution.py:46
  5.3 9.8 %collective-permute-start.3 = (bf16[2,128,512]{2,1,0:T(8,128)(2,1)S(1)}, bf16[2,128,512]{2,1,0:T(8,128)(2,1)S(1)}, u32[]{:S(2)}, u32[]{:S(2)}) collective-permute-start(bf16[2,128,512]{2,1,0:T(8,128)(2,1)S(1)} %pad_maximum_fusion), channel_id=1, source_target_pairs={{0,2},{1,3},{2,0},{3,1},{4,6},{5,7},{6,4},{7,5},{8,10},{9,11},{10,... | collective-permute-start | bytes 786440 | tf_op jit(solution)/shard_map/ppermute | solution.py:46
  8.0 12.4 %collective-permute-start.6 = (bf16[128,512]{1,0:T(8,128)(2,1)S(1)}, bf16[128,512]{1,0:T(8,128)(2,1)S(1)}, u32[]{:S(2)}, u32[]{:S(2)}) collective-permute-start(bf16[128,512]{1,0:T(8,128)(2,1)S(1)} %dynamic-slice_bitcast_fusion.1), channel_id=1, source_target_pairs={{0,4},{1,5},{2,6},{3,7},{4,0},{5,1},{6,2},{7,3},{8,12},{9,13},{10,... | collective-permute-start | bytes 393224 | tf_op jit(solution)/shard_map/ppermute | solution.py:46
  9.6 12.9 %collective-permute-start.7 = (bf16[128,512]{1,0:T(8,128)(2,1)S(1)}, bf16[128,512]{1,0:T(8,128)(2,1)S(1)}, u32[]{:S(2)}, u32[]{:S(2)}) collective-permute-start(bf16[128,512]{1,0:T(8,128)(2,1)S(1)} %dynamic-slice_bitcast_fusion.1), channel_id=1, source_target_pairs={{0,8},{1,9},{2,10},{3,11},{4,12},{5,13},{6,14},{7,15},{8,0},{9,1},... | collective-permute-start | bytes 393224 | tf_op jit(solution)/shard_map/ppermute | solution.py:46
  12.2 10.4 %collective-permute-start.8 = (bf16[128,512]{1,0:T(8,128)(2,1)S(1)}, bf16[128,512]{1,0:T(8,128)(2,1)S(1)}, u32[]{:S(2)}, u32[]{:S(2)}) collective-permute-start(bf16[128,512]{1,0:T(8,128)(2,1)S(1)} %dynamic-slice_bitcast_fusion.1), channel_id=1, source_target_pairs={{0,12},{1,13},{2,14},{3,15},{4,8},{5,9},{6,10},{7,11},{8,4},{9,5},... | collective-permute-start | bytes 393224 | tf_op jit(solution)/shard_map/ppermute | solution.py:46
  12.4 8.1 %collective-permute-start.2 = (bf16[2,128,512]{2,1,0:T(8,128)(2,1)S(1)}, bf16[2,128,512]{2,1,0:T(8,128)(2,1)S(1)}, u32[]{:S(2)}, u32[]{:S(2)}) collective-permute-start(bf16[2,128,512]{2,1,0:T(8,128)(2,1)S(1)} %pad_maximum_fusion.1), channel_id=1, source_target_pairs={{0,2},{1,3},{2,0},{3,1},{4,6},{5,7},{6,4},{7,5},{8,10},{9,11},{10,... | collective-permute-start | bytes 786440 | tf_op jit(solution)/shard_map/ppermute | solution.py:46
  15.3 11.2 %collective-permute-start.4 = (bf16[2,128,512]{2,1,0:T(8,128)(2,1)S(1)}, bf16[2,128,512]{2,1,0:T(8,128)(2,1)S(1)}, u32[]{:S(2)}, u32[]{:S(2)}) collective-permute-start(bf16[2,128,512]{2,1,0:T(8,128)(2,1)S(1)} %fusion.12), channel_id=1, source_target_pairs={{0,4},{1,5},{2,6},{3,7},{4,0},{5,1},{6,2},{7,3},{8,12},{9,13},{10,... | collective-permute-start | bytes 786440 | tf_op jit(solution)/shard_map/ppermute | solution.py:46
  22.6 12.3 %collective-permute-start.9 = (bf16[4,128,512]{2,1,0:T(8,128)(2,1)S(1)}, bf16[4,128,512]{2,1,0:T(8,128)(2,1)S(1)}, u32[]{:S(2)}, u32[]{:S(2)}) collective-permute-start(bf16[4,128,512]{2,1,0:T(8,128)(2,1)S(1)} %bitcast_dynamic-update-slice_fusion.18), channel_id=1, source_target_pairs={{0,1},{1,0},{2,3},{3,2},{4,5},{5,4},{6,7},{7,6},{8,9},{9,8},{10,11... | collective-permute-start | bytes 1572872 | tf_op jit(solution)/shard_map/ppermute | solution.py:46
  22.7 18.2 %collective-permute-start.13 = (bf16[4,128,512]{2,1,0:T(8,128)(2,1)S(1)}, bf16[4,128,512]{2,1,0:T(8,128)(2,1)S(1)}, u32[]{:S(2)}, u32[]{:S(2)}) collective-permute-start(bf16[4,128,512]{2,1,0:T(8,128)(2,1)S(1)} %bitcast_dynamic-update-slice_fusion.18), channel_id=1, source_target_pairs={{0,2},{1,3},{2,0},{3,1},{4,6},{5,7},{6,4},{7,5},{8,10},{9,11},{10,... | collective-permute-start | bytes 1572872 | tf_op jit(solution)/shard_map/ppermute | solution.py:46
  26.6 8.5 %copy-start.1 = (f32[1,128]{1,0:T(1,128)S(1)}, f32[1,128]{1,0:T(1,128)}, u32[]{:S(2)}) copy-start(f32[1,128]{1,0:T(1,128)} %param.7) | copy-start | bytes 1540
  26.6 8.4 %collective-permute-start.5 = (bf16[128,512]{1,0:T(8,128)(2,1)S(1)}, bf16[128,512]{1,0:T(8,128)(2,1)S(1)}, u32[]{:S(2)}, u32[]{:S(2)}) collective-permute-start(bf16[128,512]{1,0:T(8,128)(2,1)S(1)} %fusion.26), channel_id=1, source_target_pairs={{0,8},{1,9},{2,10},{3,11},{4,12},{5,13},{6,14},{7,15},{8,0},{9,1},... | collective-permute-start | bytes 393224 | tf_op jit(solution)/shard_map/ppermute | solution.py:46
  35.2 8.1 %collective-permute-start.10 = (bf16[128,512]{1,0:T(8,128)(2,1)S(1)}, bf16[128,512]{1,0:T(8,128)(2,1)S(1)}, u32[]{:S(2)}, u32[]{:S(2)}) collective-permute-start(bf16[128,512]{1,0:T(8,128)(2,1)S(1)} %get-tuple-element.86), channel_id=1, source_target_pairs={{0,8},{1,9},{2,10},{3,11},{4,12},{5,13},{6,14},{7,15},{8,0},{9,1},... | collective-permute-start | bytes 393224 | tf_op jit(solution)/shard_map/ppermute | solution.py:46
  35.3 8.0 %collective-permute-start.11 = (bf16[128,512]{1,0:T(8,128)(2,1)S(1)}, bf16[128,512]{1,0:T(8,128)(2,1)S(1)}, u32[]{:S(2)}, u32[]{:S(2)}) collective-permute-start(bf16[128,512]{1,0:T(8,128)(2,1)S(1)} %get-tuple-element.86), channel_id=1, source_target_pairs={{0,2},{1,3},{2,0},{3,1},{4,6},{5,7},{6,4},{7,5},{8,10},{9,11},{10,... | collective-permute-start | bytes 393224 | tf_op jit(solution)/shard_map/ppermute | solution.py:46
  36.6 7.7 %collective-permute-start.12 = (bf16[128,512]{1,0:T(8,128)(2,1)S(1)}, bf16[128,512]{1,0:T(8,128)(2,1)S(1)}, u32[]{:S(2)}, u32[]{:S(2)}) collective-permute-start(bf16[128,512]{1,0:T(8,128)(2,1)S(1)} %get-tuple-element.86), channel_id=1, source_target_pairs={{0,4},{1,5},{2,6},{3,7},{4,0},{5,1},{6,2},{7,3},{8,12},{9,13},{10,... | collective-permute-start | bytes 393224 | tf_op jit(solution)/shard_map/ppermute | solution.py:46
  39.3 10.6 %collective-permute-start.17 = (bf16[128,512]{1,0:T(8,128)(2,1)S(1)}, bf16[128,512]{1,0:T(8,128)(2,1)S(1)}, u32[]{:S(2)}, u32[]{:S(2)}) collective-permute-start(bf16[128,512]{1,0:T(8,128)(2,1)S(1)} %get-tuple-element.86), channel_id=1, source_target_pairs={{0,16},{16,0},{1,17},{17,1},{2,18},{18,2},{3,19},{19,3},{4,20},{20... | collective-permute-start | bytes 393224 | tf_op jit(solution)/shard_map/ppermute | solution.py:119
  40.9 8.9 %collective-permute-start.19 = (bf16[128,512]{1,0:T(8,128)(2,1)S(1)}, bf16[128,512]{1,0:T(8,128)(2,1)S(1)}, u32[]{:S(2)}, u32[]{:S(2)}) collective-permute-start(bf16[128,512]{1,0:T(8,128)(2,1)S(1)} %get-tuple-element.86), channel_id=1, source_target_pairs={{0,6},{1,7},{2,4},{3,5},{4,2},{5,3},{6,0},{7,1},{8,14},{9,15},{10,... | collective-permute-start | bytes 393224 | tf_op jit(solution)/shard_map/ppermute | solution.py:46
  44.2 8.9 %collective-permute-start.14 = (bf16[128,512]{1,0:T(8,128)(2,1)S(1)}, bf16[128,512]{1,0:T(8,128)(2,1)S(1)}, u32[]{:S(2)}, u32[]{:S(2)}) collective-permute-start(bf16[128,512]{1,0:T(8,128)(2,1)S(1)} %collective-permute-done.10), channel_id=1, source_target_pairs={{0,2},{1,3},{2,0},{3,1},{4,6},{5,7},{6,4},{7,5},{8,10},{9,11},{10,... | collective-permute-start | bytes 393224 | tf_op jit(solution)/shard_map/ppermute | solution.py:46
  47.6 5.6 %collective-permute-start.15 = (bf16[128,512]{1,0:T(8,128)(2,1)S(1)}, bf16[128,512]{1,0:T(8,128)(2,1)S(1)}, u32[]{:S(2)}, u32[]{:S(2)}) collective-permute-start(bf16[128,512]{1,0:T(8,128)(2,1)S(1)} %collective-permute-done.10), channel_id=1, source_target_pairs={{0,4},{1,5},{2,6},{3,7},{4,0},{5,1},{6,2},{7,3},{8,12},{9,13},{10,... | collective-permute-start | bytes 393224 | tf_op jit(solution)/shard_map/ppermute | solution.py:46
  47.6 6.7 %collective-permute-start.16 = (bf16[128,512]{1,0:T(8,128)(2,1)S(1)}, bf16[128,512]{1,0:T(8,128)(2,1)S(1)}, u32[]{:S(2)}, u32[]{:S(2)}) collective-permute-start(bf16[128,512]{1,0:T(8,128)(2,1)S(1)} %collective-permute-done.10), channel_id=1, source_target_pairs={{0,6},{1,7},{2,4},{3,5},{4,2},{5,3},{6,0},{7,1},{8,14},{9,15},{10,... | collective-permute-start | bytes 393224 | tf_op jit(solution)/shard_map/ppermute | solution.py:46
  49.8 1.9 %collective-permute-start.18 = (bf16[4,128,512]{2,1,0:T(8,128)(2,1)S(1)}, bf16[4,128,512]{2,1,0:T(8,128)(2,1)S(1)}, u32[]{:S(2)}, u32[]{:S(2)}) collective-permute-start(bf16[4,128,512]{2,1,0:T(8,128)(2,1)S(1)} %collective-permute-done.13), channel_id=1, source_target_pairs={{0,1},{1,0},{2,3},{3,2},{4,5},{5,4},{6,7},{7,6},{8,9},{9,8},{10,11... | collective-permute-start | bytes 1572872 | tf_op jit(solution)/shard_map/ppermute | solution.py:46
  49.9 3.2 %collective-permute-start.20 = (bf16[4,128,512]{2,1,0:T(8,128)(2,1)S(1)}, bf16[4,128,512]{2,1,0:T(8,128)(2,1)S(1)}, u32[]{:S(2)}, u32[]{:S(2)}) collective-permute-start(bf16[4,128,512]{2,1,0:T(8,128)(2,1)S(1)} %bitcast_dynamic-update-slice_fusion.12), channel_id=1, source_target_pairs={{0,1},{1,0},{2,3},{3,2},{4,5},{5,4},{6,7},{7,6},{8,9},{9,8},{10,11... | collective-permute-start | bytes 1572872 | tf_op jit(solution)/shard_map/ppermute | solution.py:46
  50.5 1.3 %copy-start.3 = (bf16[1,256,2048]{2,1,0:T(8,128)(2,1)S(1)}, bf16[1,256,2048]{2,1,0:T(8,128)(2,1)}, u32[]{:S(2)}) copy-start(bf16[1,256,2048]{2,1,0:T(8,128)(2,1)} %param.6) | copy-start | bytes 3145732
  54.5 2.0 %collective-permute-start.21 = (bf16[4,128,512]{2,1,0:T(8,128)(2,1)S(1)}, bf16[4,128,512]{2,1,0:T(8,128)(2,1)S(1)}, u32[]{:S(2)}, u32[]{:S(2)}) collective-permute-start(bf16[4,128,512]{2,1,0:T(8,128)(2,1)S(1)} %bitcast_dynamic-update-slice_fusion.8), channel_id=1, source_target_pairs={{0,1},{1,0},{2,3},{3,2},{4,5},{5,4},{6,7},{7,6},{8,9},{9,8},{10,11... | collective-permute-start | bytes 1572872 | tf_op jit(solution)/shard_map/ppermute | solution.py:46

commit v8 on v7

--- a/solution.py
+++ b/solution.py
@@ -118,7 +118,7 @@
         ring = [(i, (i + step) % n_resp) for i in range(n_resp)]
         others.append(lax.ppermute(residual, "resp", ring))
     near = [swap(residual, bits) for bits in (2, 4, 6)]
-    far, near[:2], near_spins = lax.optimization_barrier((far, near[:2], near_spins))
+    near_spins, near[1], near[0], far = lax.optimization_barrier((near_spins, near[1], near[0], far))
     all_spins = jnp.zeros((n_line, 2, 2, sub_len, batch), jnp.bfloat16)
     for side, core, group in (
         ("near", "core", line_spins),
@@ -149,13 +149,13 @@
     all_res = jnp.zeros((n_high, 4, 2, sub_len, batch), jnp.bfloat16)
     for step in range(n_high):
         if step:
-            blocks = [far[step - 1]] + [swap(far[step - 1], bits) for bits in (2, 4, 6)]
+            blocks = [swap(far[step - 1], bits) for bits in (6, 4, 2)] + [far[step - 1]]
         else:
-            blocks = [residual] + near
+            blocks = near[::-1] + [residual]
         if step == n_high - 1:
             blocks, base, all_res = lax.optimization_barrier((blocks, base, all_res))
         quad = jnp.zeros((4, sub_len, batch), jnp.bfloat16)
-        for index, block in zip(where["quad"], blocks):
+        for index, block in zip(where["quad"][::-1], blocks):
             quad = put_at(quad, block[None], index)
         for core, group in (("core", quad), ("other_core", swap(quad, 1))):
             all_res = put_at(all_res, group[None, :, None], where["high"][step], 0, where[core])

time: 58.7 us -> 57.5 us (0.980)
  starting transfers between devices: 23.9 us -> 22.6 us
    ppermute x21, starting transfers between devices: 22.4 us -> 21 us  [swap(): return lax.ppermute(array, 'item', [(i, i ^ bits) for i in range(n_item)])]
  transfers between devices with their start and end apart: 22 -> 22, of which waited for: 12 -> 10; matrix products, arithmetic and copies ran while one was open for 7% -> 7% of each run, Pallas kernels for 0% -> 0%
where the time goes in v8:
time: 57.5 us; the launch traced here: 57.4 us
  waiting for transfers between devices  25.4 us (44%)
  starting transfers between devices  22.6 us (39%)
  matrix products  3.66 us (6%)
  local copies, waits for them, and re-layouts  3.14 us (5%)
  other arithmetic  2.09 us (4%)
    ppermute x21, waiting for transfers between devices, swap(): return lax.ppermute(array, 'item', [(i, i ^ bits) for i in range(n_item)])  25.4 us
    ppermute x21, starting transfers between devices, swap(): return lax.ppermute(array, 'item', [(i, i ^ bits) for i in range(n_item)])  21 us
    dot_general x2, matrix products, product(): grad = lax.dot_general(left, right, NT, preferred_element_type=jnp.float32)  2.08 us
    unnamed x11, local copies, waits for them, and re-layouts  1.65 us
    ppermute x1, starting transfers between devices, shards(): others.append(lax.ppermute(residual, 'resp', ring))  1.61 us
    broadcast_in_dim x1, other arithmetic, shards(): return (base + change).astype(jnp.bfloat16)[None]  1.23 us
  transfers between devices with their start and end apart: 22, of which 10 were waited for; matrix products, arithmetic and copies ran while one was open for 7% of the time, Pallas kernels for 0%

profile of v8, /device:TPU:0, one launch (start us, length us, event | category | flops | bytes accessed | tf_op | source)
XLA Modules:
  0.0 57.4 jit_solution(14752201385714753317)
XLA Ops:
  0.0 1.6 %copy.14 = bf16[1,256,2048]{1,2,0:T(8,128)(2,1)S(1)} copy(bf16[1,256,2048]{2,1,0:T(8,128)(2,1)} %param.5) | data formatting | bytes 2097152 | tf_op args[0]
  1.6 0.0 copy-start
  1.6 0.1 constant_dynamic-slice_fusion.9
  1.7 0.5 collective-permute-start
  2.3 0.7 %fusion.7 = bf16[256,512]{1,0:T(8,128)(2,1)S(1)} fusion(s32[512]{0:T(512)S(1)} %copy-done.4, s32[1024,256]{1,0:T(8,128)S(1)} %copy-done.2), kind=kOutput, calls=%fused_computation.16 | convolution fusion | flops 269877248 | bytes 1312768 | tf_op jit(solution)/shard_map/dot_general | solution.py:63
  3.0 0.1 collective-permute-start.1
  3.2 0.4 fusion.4
  3.6 0.4 fusion.33
  4.0 0.6 %collective-permute-done.1 = bf16[256,512]{1,0:T(8,128)(2,1)S(1)} collective-permute-done((bf16[256,512]{1,0:T(8,128)(2,1)S(1)}, bf16[256,512]{1,0:T(8,128)(2,1)S(1)}, u32[]{:S(2)}, u32[]{:S(2)}) %collective-permute-start.1) | collective-permute-done | bytes 262176 | tf_op jit(solution)/shard_map/ppermute | solution.py:46
  4.6 0.0 collective-permute-done
  4.6 0.4 convolution_add_fusion
  5.0 0.1 fusion.10
  5.1 0.1 dynamic-slice_bitcast_fusion
  5.2 0.1 constant_dynamic-slice_fusion.6
  5.4 2.7 %collective-permute-start.6 = (bf16[2,128,512]{2,1,0:T(8,128)(2,1)S(1)}, bf16[2,128,512]{2,1,0:T(8,128)(2,1)S(1)}, u32[]{:S(2)}, u32[]{:S(2)}) collective-permute-start(bf16[2,128,512]{2,1,0:T(8,128)(2,1)S(1)} %pad_maximum_fusion), channel_id=1, source_target_pairs={{0,2},{1,3},{2,0},{3,1},{4,6},{5,7},{6,4},{7,5},{8,10},{9,11},{10,... | collective-permute-start | bytes 786440 | tf_op jit(solution)/shard_map/ppermute | solution.py:46
  8.1 1.6 %collective-permute-start.2 = (bf16[128,512]{1,0:T(8,128)(2,1)S(1)}, bf16[128,512]{1,0:T(8,128)(2,1)S(1)}, u32[]{:S(2)}, u32[]{:S(2)}) collective-permute-start(bf16[128,512]{1,0:T(8,128)(2,1)S(1)} %dynamic-slice_bitcast_fusion.1), channel_id=1, source_target_pairs={{0,4},{1,5},{2,6},{3,7},{4,0},{5,1},{6,2},{7,3},{8,12},{9,13},{10,... | collective-permute-start | bytes 393224 | tf_op jit(solution)/shard_map/ppermute | solution.py:46
  9.7 2.6 %collective-permute-start.3 = (bf16[128,512]{1,0:T(8,128)(2,1)S(1)}, bf16[128,512]{1,0:T(8,128)(2,1)S(1)}, u32[]{:S(2)}, u32[]{:S(2)}) collective-permute-start(bf16[128,512]{1,0:T(8,128)(2,1)S(1)} %dynamic-slice_bitcast_fusion.1), channel_id=1, source_target_pairs={{0,8},{1,9},{2,10},{3,11},{4,12},{5,13},{6,14},{7,15},{8,0},{9,1},... | collective-permute-start | bytes 393224 | tf_op jit(solution)/shard_map/ppermute | solution.py:46
  12.3 0.2 collective-permute-start.4
  12.5 0.3 collective-permute-start.5
  12.8 0.1 constant_dynamic-slice_fusion.2
  12.9 2.3 %collective-permute-done.6 = bf16[2,128,512]{2,1,0:T(8,128)(2,1)S(1)} collective-permute-done((bf16[2,128,512]{2,1,0:T(8,128)(2,1)S(1)}, bf16[2,128,512]{2,1,0:T(8,128)(2,1)S(1)}, u32[]{:S(2)}, u32[]{:S(2)}) %collective-permute-start.6) | collective-permute-done | bytes 262176 | tf_op jit(solution)/shard_map/ppermute | solution.py:46
  15.2 0.1 fusion.11
  15.3 2.1 %collective-permute-start.8 = (bf16[2,128,512]{2,1,0:T(8,128)(2,1)S(1)}, bf16[2,128,512]{2,1,0:T(8,128)(2,1)S(1)}, u32[]{:S(2)}, u32[]{:S(2)}) collective-permute-start(bf16[2,128,512]{2,1,0:T(8,128)(2,1)S(1)} %fusion.11), channel_id=1, source_target_pairs={{0,4},{1,5},{2,6},{3,7},{4,0},{5,1},{6,2},{7,3},{8,12},{9,13},{10,... | collective-permute-start | bytes 786440 | tf_op jit(solution)/shard_map/ppermute | solution.py:46
  17.4 3.1 %collective-permute-done.5 = bf16[2,128,512]{2,1,0:T(8,128)(2,1)S(1)} collective-permute-done((bf16[2,128,512]{2,1,0:T(8,128)(2,1)S(1)}, bf16[2,128,512]{2,1,0:T(8,128)(2,1)S(1)}, u32[]{:S(2)}, u32[]{:S(2)}) %collective-permute-start.5) | collective-permute-done | bytes 262176 | tf_op jit(solution)/shard_map/ppermute | solution.py:46
  20.5 0.0 collective-permute-done.2
  20.5 2.1 %collective-permute-done.3 = bf16[128,512]{1,0:T(8,128)(2,1)S(1)} collective-permute-done((bf16[128,512]{1,0:T(8,128)(2,1)S(1)}, bf16[128,512]{1,0:T(8,128)(2,1)S(1)}, u32[]{:S(2)}, u32[]{:S(2)}) %collective-permute-start.3) | collective-permute-done | bytes 131104 | tf_op jit(solution)/shard_map/ppermute | solution.py:46
  22.6 0.0 collective-permute-done.4
  22.7 0.6 %collective-permute-start.7 = (bf16[4,128,512]{2,1,0:T(8,128)(2,1)S(1)}, bf16[4,128,512]{2,1,0:T(8,128)(2,1)S(1)}, u32[]{:S(2)}, u32[]{:S(2)}) collective-permute-start(bf16[4,128,512]{2,1,0:T(8,128)(2,1)S(1)} %bitcast_dynamic-update-slice_fusion.18), channel_id=1, source_target_pairs={{0,2},{1,3},{2,0},{3,1},{4,6},{5,7},{6,4},{7,5},{8,10},{9,11},{10,... | collective-permute-start | bytes 1572872 | tf_op jit(solution)/shard_map/ppermute | solution.py:46
  23.3 0.0 collective-permute-start.10
  23.3 3.2 %collective-permute-done.8 = bf16[2,128,512]{2,1,0:T(8,128)(2,1)S(1)} collective-permute-done((bf16[2,128,512]{2,1,0:T(8,128)(2,1)S(1)}, bf16[2,128,512]{2,1,0:T(8,128)(2,1)S(1)}, u32[]{:S(2)}, u32[]{:S(2)}) %collective-permute-start.8) | collective-permute-done | bytes 262176 | tf_op jit(solution)/shard_map/ppermute | solution.py:46
  26.5 0.1 fusion.12
  26.6 0.0 copy-start.1
  26.7 1.2 %collective-permute-start.9 = (bf16[128,512]{1,0:T(8,128)(2,1)S(1)}, bf16[128,512]{1,0:T(8,128)(2,1)S(1)}, u32[]{:S(2)}, u32[]{:S(2)}) collective-permute-start(bf16[128,512]{1,0:T(8,128)(2,1)S(1)} %fusion.26), channel_id=1, source_target_pairs={{0,8},{1,9},{2,10},{3,11},{4,12},{5,13},{6,14},{7,15},{8,0},{9,1},... | collective-permute-start | bytes 393224 | tf_op jit(solution)/shard_map/ppermute | solution.py:46
  27.8 0.2 broadcast_in_dim.92
  28.1 7.0 %collective-permute-done.9 = bf16[128,512]{1,0:T(8,128)(2,1)S(1)} collective-permute-done((bf16[128,512]{1,0:T(8,128)(2,1)S(1)}, bf16[128,512]{1,0:T(8,128)(2,1)S(1)}, u32[]{:S(2)}, u32[]{:S(2)}) %collective-permute-start.9) | collective-permute-done | bytes 131104 | tf_op jit(solution)/shard_map/ppermute | solution.py:46
  35.0 0.0 collective-permute-done.10
  35.1 0.2 bitcast_dynamic-update-slice_fusion.17
  35.3 0.1 collective-permute-start.11
  35.3 1.3 %collective-permute-start.12 = (bf16[128,512]{1,0:T(8,128)(2,1)S(1)}, bf16[128,512]{1,0:T(8,128)(2,1)S(1)}, u32[]{:S(2)}, u32[]{:S(2)}) collective-permute-start(bf16[128,512]{1,0:T(8,128)(2,1)S(1)} %get-tuple-element.86), channel_id=1, source_target_pairs={{0,2},{1,3},{2,0},{3,1},{4,6},{5,7},{6,4},{7,5},{8,10},{9,11},{10,... | collective-permute-start | bytes 393224 | tf_op jit(solution)/shard_map/ppermute | solution.py:46
  36.7 2.9 %collective-permute-start.13 = (bf16[128,512]{1,0:T(8,128)(2,1)S(1)}, bf16[128,512]{1,0:T(8,128)(2,1)S(1)}, u32[]{:S(2)}, u32[]{:S(2)}) collective-permute-start(bf16[128,512]{1,0:T(8,128)(2,1)S(1)} %get-tuple-element.86), channel_id=1, source_target_pairs={{0,8},{1,9},{2,10},{3,11},{4,12},{5,13},{6,14},{7,15},{8,0},{9,1},... | collective-permute-start | bytes 393224 | tf_op jit(solution)/shard_map/ppermute | solution.py:46
  39.6 0.6 %collective-permute-start.19 = (bf16[128,512]{1,0:T(8,128)(2,1)S(1)}, bf16[128,512]{1,0:T(8,128)(2,1)S(1)}, u32[]{:S(2)}, u32[]{:S(2)}) collective-permute-start(bf16[128,512]{1,0:T(8,128)(2,1)S(1)} %get-tuple-element.86), channel_id=1, source_target_pairs={{0,6},{1,7},{2,4},{3,5},{4,2},{5,3},{6,0},{7,1},{8,14},{9,15},{10,... | collective-permute-start | bytes 393224 | tf_op jit(solution)/shard_map/ppermute | solution.py:46
  40.2 0.0 collective-permute-done.7
  40.2 1.6 %collective-permute-start.17 = (bf16[128,512]{1,0:T(8,128)(2,1)S(1)}, bf16[128,512]{1,0:T(8,128)(2,1)S(1)}, u32[]{:S(2)}, u32[]{:S(2)}) collective-permute-start(bf16[128,512]{1,0:T(8,128)(2,1)S(1)} %get-tuple-element.86), channel_id=1, source_target_pairs={{0,16},{16,0},{1,17},{17,1},{2,18},{18,2},{3,19},{19,3},{4,20},{20... | collective-permute-start | bytes 393224 | tf_op jit(solution)/shard_map/ppermute | solution.py:119
  41.8 0.0 collective-permute-done.11
  41.9 0.0 collective-permute-done.12
  41.9 3.8 %collective-permute-done.13 = bf16[128,512]{1,0:T(8,128)(2,1)S(1)} collective-permute-done((bf16[128,512]{1,0:T(8,128)(2,1)S(1)}, bf16[128,512]{1,0:T(8,128)(2,1)S(1)}, u32[]{:S(2)}, u32[]{:S(2)}) %collective-permute-start.13) | collective-permute-done | bytes 131104 | tf_op jit(solution)/shard_map/ppermute | solution.py:46
  45.7 0.5 collective-permute-start.14
  46.2 2.0 %collective-permute-start.15 = (bf16[128,512]{1,0:T(8,128)(2,1)S(1)}, bf16[128,512]{1,0:T(8,128)(2,1)S(1)}, u32[]{:S(2)}, u32[]{:S(2)}) collective-permute-start(bf16[128,512]{1,0:T(8,128)(2,1)S(1)} %collective-permute-done.13), channel_id=1, source_target_pairs={{0,4},{1,5},{2,6},{3,7},{4,0},{5,1},{6,2},{7,3},{8,12},{9,13},{10,... | collective-permute-start | bytes 393224 | tf_op jit(solution)/shard_map/ppermute | solution.py:46
  48.2 1.0 %collective-permute-start.16 = (bf16[128,512]{1,0:T(8,128)(2,1)S(1)}, bf16[128,512]{1,0:T(8,128)(2,1)S(1)}, u32[]{:S(2)}, u32[]{:S(2)}) collective-permute-start(bf16[128,512]{1,0:T(8,128)(2,1)S(1)} %collective-permute-done.13), channel_id=1, source_target_pairs={{0,2},{1,3},{2,0},{3,1},{4,6},{5,7},{6,4},{7,5},{8,10},{9,11},{10,... | collective-permute-start | bytes 393224 | tf_op jit(solution)/shard_map/ppermute | solution.py:46
  49.1 0.0 collective-permute-done.19
  49.1 0.0 collective-permute-start.18
  49.3 0.0 collective-permute-done.17
  49.3 0.6 collective-permute-start.20
  49.9 0.0 copy-start.3
  50.0 0.2 broadcast_in_dim.97
  50.2 0.8 %collective-permute-done.18 = bf16[4,128,512]{2,1,0:T(8,128)(2,1)S(1)} collective-permute-done((bf16[4,128,512]{2,1,0:T(8,128)(2,1)S(1)}, bf16[4,128,512]{2,1,0:T(8,128)(2,1)S(1)}, u32[]{:S(2)}, u32[]{:S(2)}) %collective-permute-start.18) | collective-permute-done | bytes 524320 | tf_op jit(solution)/shard_map/ppermute | solution.py:46
  51.1 0.1 copy-done.3
  51.2 1.3 %fusion.3 = f32[256,2048]{1,0:T(8,128)S(1)} fusion(bf16[256,512]{1,0:T(8,128)(2,1)S(1)} %bitcast.112, bf16[2048,512]{1,0:T(8,128)(2,1)S(1)} %bitcast.107, bf16[1,256,2048]{2,1,0:T(8,128)(2,1)S(1)} %copy-done.3, bf16[1,256,2048]{2,1,0:T(8,128)(2,1)S(1)} %copy-done, s32[2048]{0:T(1024)S(1)} %iota_subtract_fusion, s32[256]{0:T(256)S(1)} %iota_subtract_fusion.1, ...), kind=kOutput, calls=%fused_computation.8 | convolution fusion | flops 543162368 | bytes 6563328 | tf_op jit(solution)/shard_map/dot_general | solution.py:142
  52.5 0.0 collective-permute-done.15
  52.5 0.6 %collective-permute-done.16 = bf16[128,512]{1,0:T(8,128)(2,1)S(1)} collective-permute-done((bf16[128,512]{1,0:T(8,128)(2,1)S(1)}, bf16[128,512]{1,0:T(8,128)(2,1)S(1)}, u32[]{:S(2)}, u32[]{:S(2)}) %collective-permute-start.16) | collective-permute-done | bytes 131104 | tf_op jit(solution)/shard_map/ppermute | solution.py:46
  53.3 0.1 collective-permute-start.21
  53.4 1.8 %collective-permute-done.21 = bf16[4,128,512]{2,1,0:T(8,128)(2,1)S(1)} collective-permute-done((bf16[4,128,512]{2,1,0:T(8,128)(2,1)S(1)}, bf16[4,128,512]{2,1,0:T(8,128)(2,1)S(1)}, u32[]{:S(2)}, u32[]{:S(2)}) %collective-permute-start.21) | collective-permute-done | bytes 524320 | tf_op jit(solution)/shard_map/ppermute | solution.py:46
  55.3 0.8 %fusion.2 = f32[256,2048]{1,0:T(8,128)S(1)} fusion(bf16[256,512]{1,0:T(8,128)(2,1)S(1)} %fusion.7, bf16[2048,512]{1,0:T(8,128)(2,1)S(1)} %bitcast.108, s32[2048]{0:T(1024)S(1)} %iota_subtract_fusion, s32[256]{0:T(256)S(1)} %iota_subtract_fusion.1, pred[256]{0:T(512)(128)(4,1)S(1)} %get-tuple-element.98, pred[256]{0:T(512)(128)(4,1)S(1)} %get-tuple-element.99), kind=kOutput, calls=%fused_computation.7 | convolution fusion | flops 539492352 | bytes 4466176 | tf_op jit(solution)/shard_map/dot_general | solution.py:142
  56.1 1.2 %fusion.8 = bf16[1,256,2048]{2,1,0:T(8,128)(2,1)} fusion(f32[256,2048]{1,0:T(8,128)S(1)} %fusion.3, f32[256,2048]{1,0:T(8,128)S(1)} %fusion.2), kind=kLoop, calls=%fused_computation.17 | loop fusion | flops 1048576 | bytes 5242880 | tf_op jit(solution)/shard_map/broadcast_in_dim | solution.py:163
  (40 shorter events, 0.8 us)
Async XLA Ops:
  0.0 2.3 %copy-start.2 = (s32[1024,256]{1,0:T(8,128)S(1)}, s32[1024,256]{1,0:T(8,128)}, u32[]{:S(2)}) copy-start(s32[1024,256]{1,0:T(8,128)} %param.8) | copy-start | bytes 3145732
  0.0 2.3 %copy-start.4 = (s32[512]{0:T(512)S(1)}, s32[512]{0:T(512)}, u32[]{:S(2)}) copy-start(s32[512]{0:T(512)} %param.9) | copy-start | bytes 6148
  1.6 1.5 %copy-start = (bf16[1,256,2048]{2,1,0:T(8,128)(2,1)S(1)}, bf16[1,256,2048]{2,1,0:T(8,128)(2,1)}, u32[]{:S(2)}) copy-start(bf16[1,256,2048]{2,1,0:T(8,128)(2,1)} %param.5) | copy-start | bytes 3145732
  1.7 2.9 %collective-permute-start = (bf16[256,1024]{0,1:T(8,128)(2,1)S(1)}, bf16[256,1024]{0,1:T(8,128)(2,1)S(1)}, u32[]{:S(2)}, u32[]{:S(2)}) collective-permute-start(bf16[256,1024]{0,1:T(8,128)(2,1)S(1)} %bitcast.111), channel_id=1, source_target_pairs={{0,1},{1,0},{2,3},{3,2},{4,5},{5,4},{6,7},{7,6},{8,9},{9,8},{10,11... | collective-permute-start | bytes 1572872 | tf_op jit(solution)/shard_map/ppermute | solution.py:46
  3.0 1.6 %collective-permute-start.1 = (bf16[256,512]{1,0:T(8,128)(2,1)S(1)}, bf16[256,512]{1,0:T(8,128)(2,1)S(1)}, u32[]{:S(2)}, u32[]{:S(2)}) collective-permute-start(bf16[256,512]{1,0:T(8,128)(2,1)S(1)} %fusion.7), channel_id=1, source_target_pairs={{0,1},{1,0},{2,3},{3,2},{4,5},{5,4},{6,7},{7,6},{8,9},{9,8},{10,11... | collective-permute-start | bytes 786440 | tf_op jit(solution)/shard_map/ppermute | solution.py:46
  5.4 9.8 %collective-permute-start.6 = (bf16[2,128,512]{2,1,0:T(8,128)(2,1)S(1)}, bf16[2,128,512]{2,1,0:T(8,128)(2,1)S(1)}, u32[]{:S(2)}, u32[]{:S(2)}) collective-permute-start(bf16[2,128,512]{2,1,0:T(8,128)(2,1)S(1)} %pad_maximum_fusion), channel_id=1, source_target_pairs={{0,2},{1,3},{2,0},{3,1},{4,6},{5,7},{6,4},{7,5},{8,10},{9,11},{10,... | collective-permute-start | bytes 786440 | tf_op jit(solution)/shard_map/ppermute | solution.py:46
  8.1 12.4 %collective-permute-start.2 = (bf16[128,512]{1,0:T(8,128)(2,1)S(1)}, bf16[128,512]{1,0:T(8,128)(2,1)S(1)}, u32[]{:S(2)}, u32[]{:S(2)}) collective-permute-start(bf16[128,512]{1,0:T(8,128)(2,1)S(1)} %dynamic-slice_bitcast_fusion.1), channel_id=1, source_target_pairs={{0,4},{1,5},{2,6},{3,7},{4,0},{5,1},{6,2},{7,3},{8,12},{9,13},{10,... | collective-permute-start | bytes 393224 | tf_op jit(solution)/shard_map/ppermute | solution.py:46
  9.7 12.9 %collective-permute-start.3 = (bf16[128,512]{1,0:T(8,128)(2,1)S(1)}, bf16[128,512]{1,0:T(8,128)(2,1)S(1)}, u32[]{:S(2)}, u32[]{:S(2)}) collective-permute-start(bf16[128,512]{1,0:T(8,128)(2,1)S(1)} %dynamic-slice_bitcast_fusion.1), channel_id=1, source_target_pairs={{0,8},{1,9},{2,10},{3,11},{4,12},{5,13},{6,14},{7,15},{8,0},{9,1},... | collective-permute-start | bytes 393224 | tf_op jit(solution)/shard_map/ppermute | solution.py:46
  12.3 10.4 %collective-permute-start.4 = (bf16[128,512]{1,0:T(8,128)(2,1)S(1)}, bf16[128,512]{1,0:T(8,128)(2,1)S(1)}, u32[]{:S(2)}, u32[]{:S(2)}) collective-permute-start(bf16[128,512]{1,0:T(8,128)(2,1)S(1)} %dynamic-slice_bitcast_fusion.1), channel_id=1, source_target_pairs={{0,12},{1,13},{2,14},{3,15},{4,8},{5,9},{6,10},{7,11},{8,4},{9,5},... | collective-permute-start | bytes 393224 | tf_op jit(solution)/shard_map/ppermute | solution.py:46
  12.5 8.1 %collective-permute-start.5 = (bf16[2,128,512]{2,1,0:T(8,128)(2,1)S(1)}, bf16[2,128,512]{2,1,0:T(8,128)(2,1)S(1)}, u32[]{:S(2)}, u32[]{:S(2)}) collective-permute-start(bf16[2,128,512]{2,1,0:T(8,128)(2,1)S(1)} %pad_maximum_fusion.1), channel_id=1, source_target_pairs={{0,2},{1,3},{2,0},{3,1},{4,6},{5,7},{6,4},{7,5},{8,10},{9,11},{10,... | collective-permute-start | bytes 786440 | tf_op jit(solution)/shard_map/ppermute | solution.py:46
  15.3 11.2 %collective-permute-start.8 = (bf16[2,128,512]{2,1,0:T(8,128)(2,1)S(1)}, bf16[2,128,512]{2,1,0:T(8,128)(2,1)S(1)}, u32[]{:S(2)}, u32[]{:S(2)}) collective-permute-start(bf16[2,128,512]{2,1,0:T(8,128)(2,1)S(1)} %fusion.11), channel_id=1, source_target_pairs={{0,4},{1,5},{2,6},{3,7},{4,0},{5,1},{6,2},{7,3},{8,12},{9,13},{10,... | collective-permute-start | bytes 786440 | tf_op jit(solution)/shard_map/ppermute | solution.py:46
  22.7 17.5 %collective-permute-start.7 = (bf16[4,128,512]{2,1,0:T(8,128)(2,1)S(1)}, bf16[4,128,512]{2,1,0:T(8,128)(2,1)S(1)}, u32[]{:S(2)}, u32[]{:S(2)}) collective-permute-start(bf16[4,128,512]{2,1,0:T(8,128)(2,1)S(1)} %bitcast_dynamic-update-slice_fusion.18), channel_id=1, source_target_pairs={{0,2},{1,3},{2,0},{3,1},{4,6},{5,7},{6,4},{7,5},{8,10},{9,11},{10,... | collective-permute-start | bytes 1572872 | tf_op jit(solution)/shard_map/ppermute | solution.py:46
  23.3 11.7 %collective-permute-start.10 = (bf16[4,128,512]{2,1,0:T(8,128)(2,1)S(1)}, bf16[4,128,512]{2,1,0:T(8,128)(2,1)S(1)}, u32[]{:S(2)}, u32[]{:S(2)}) collective-permute-start(bf16[4,128,512]{2,1,0:T(8,128)(2,1)S(1)} %bitcast_dynamic-update-slice_fusion.18), channel_id=1, source_target_pairs={{0,1},{1,0},{2,3},{3,2},{4,5},{5,4},{6,7},{7,6},{8,9},{9,8},{10,11... | collective-permute-start | bytes 1572872 | tf_op jit(solution)/shard_map/ppermute | solution.py:46
  26.6 8.4 %copy-start.1 = (f32[1,128]{1,0:T(1,128)S(1)}, f32[1,128]{1,0:T(1,128)}, u32[]{:S(2)}) copy-start(f32[1,128]{1,0:T(1,128)} %param.7) | copy-start | bytes 1540
  26.7 8.4 %collective-permute-start.9 = (bf16[128,512]{1,0:T(8,128)(2,1)S(1)}, bf16[128,512]{1,0:T(8,128)(2,1)S(1)}, u32[]{:S(2)}, u32[]{:S(2)}) collective-permute-start(bf16[128,512]{1,0:T(8,128)(2,1)S(1)} %fusion.26), channel_id=1, source_target_pairs={{0,8},{1,9},{2,10},{3,11},{4,12},{5,13},{6,14},{7,15},{8,0},{9,1},... | collective-permute-start | bytes 393224 | tf_op jit(solution)/shard_map/ppermute | solution.py:46
  35.3 6.6 %collective-permute-start.11 = (bf16[128,512]{1,0:T(8,128)(2,1)S(1)}, bf16[128,512]{1,0:T(8,128)(2,1)S(1)}, u32[]{:S(2)}, u32[]{:S(2)}) collective-permute-start(bf16[128,512]{1,0:T(8,128)(2,1)S(1)} %get-tuple-element.86), channel_id=1, source_target_pairs={{0,4},{1,5},{2,6},{3,7},{4,0},{5,1},{6,2},{7,3},{8,12},{9,13},{10,... | collective-permute-start | bytes 393224 | tf_op jit(solution)/shard_map/ppermute | solution.py:46
  35.3 6.5 %collective-permute-start.12 = (bf16[128,512]{1,0:T(8,128)(2,1)S(1)}, bf16[128,512]{1,0:T(8,128)(2,1)S(1)}, u32[]{:S(2)}, u32[]{:S(2)}) collective-permute-start(bf16[128,512]{1,0:T(8,128)(2,1)S(1)} %get-tuple-element.86), channel_id=1, source_target_pairs={{0,2},{1,3},{2,0},{3,1},{4,6},{5,7},{6,4},{7,5},{8,10},{9,11},{10,... | collective-permute-start | bytes 393224 | tf_op jit(solution)/shard_map/ppermute | solution.py:46
  36.7 9.0 %collective-permute-start.13 = (bf16[128,512]{1,0:T(8,128)(2,1)S(1)}, bf16[128,512]{1,0:T(8,128)(2,1)S(1)}, u32[]{:S(2)}, u32[]{:S(2)}) collective-permute-start(bf16[128,512]{1,0:T(8,128)(2,1)S(1)} %get-tuple-element.86), channel_id=1, source_target_pairs={{0,8},{1,9},{2,10},{3,11},{4,12},{5,13},{6,14},{7,15},{8,0},{9,1},... | collective-permute-start | bytes 393224 | tf_op jit(solution)/shard_map/ppermute | solution.py:46
  39.6 9.6 %collective-permute-start.19 = (bf16[128,512]{1,0:T(8,128)(2,1)S(1)}, bf16[128,512]{1,0:T(8,128)(2,1)S(1)}, u32[]{:S(2)}, u32[]{:S(2)}) collective-permute-start(bf16[128,512]{1,0:T(8,128)(2,1)S(1)} %get-tuple-element.86), channel_id=1, source_target_pairs={{0,6},{1,7},{2,4},{3,5},{4,2},{5,3},{6,0},{7,1},{8,14},{9,15},{10,... | collective-permute-start | bytes 393224 | tf_op jit(solution)/shard_map/ppermute | solution.py:46
  40.2 9.1 %collective-permute-start.17 = (bf16[128,512]{1,0:T(8,128)(2,1)S(1)}, bf16[128,512]{1,0:T(8,128)(2,1)S(1)}, u32[]{:S(2)}, u32[]{:S(2)}) collective-permute-start(bf16[128,512]{1,0:T(8,128)(2,1)S(1)} %get-tuple-element.86), channel_id=1, source_target_pairs={{0,16},{16,0},{1,17},{17,1},{2,18},{18,2},{3,19},{19,3},{4,20},{20... | collective-permute-start | bytes 393224 | tf_op jit(solution)/shard_map/ppermute | solution.py:119
  45.7 6.9 %collective-permute-start.14 = (bf16[128,512]{1,0:T(8,128)(2,1)S(1)}, bf16[128,512]{1,0:T(8,128)(2,1)S(1)}, u32[]{:S(2)}, u32[]{:S(2)}) collective-permute-start(bf16[128,512]{1,0:T(8,128)(2,1)S(1)} %collective-permute-done.13), channel_id=1, source_target_pairs={{0,6},{1,7},{2,4},{3,5},{4,2},{5,3},{6,0},{7,1},{8,14},{9,15},{10,... | collective-permute-start | bytes 393224 | tf_op jit(solution)/shard_map/ppermute | solution.py:46
  46.2 6.4 %collective-permute-start.15 = (bf16[128,512]{1,0:T(8,128)(2,1)S(1)}, bf16[128,512]{1,0:T(8,128)(2,1)S(1)}, u32[]{:S(2)}, u32[]{:S(2)}) collective-permute-start(bf16[128,512]{1,0:T(8,128)(2,1)S(1)} %collective-permute-done.13), channel_id=1, source_target_pairs={{0,4},{1,5},{2,6},{3,7},{4,0},{5,1},{6,2},{7,3},{8,12},{9,13},{10,... | collective-permute-start | bytes 393224 | tf_op jit(solution)/shard_map/ppermute | solution.py:46
  48.2 5.0 %collective-permute-start.16 = (bf16[128,512]{1,0:T(8,128)(2,1)S(1)}, bf16[128,512]{1,0:T(8,128)(2,1)S(1)}, u32[]{:S(2)}, u32[]{:S(2)}) collective-permute-start(bf16[128,512]{1,0:T(8,128)(2,1)S(1)} %collective-permute-done.13), channel_id=1, source_target_pairs={{0,2},{1,3},{2,0},{3,1},{4,6},{5,7},{6,4},{7,5},{8,10},{9,11},{10,... | collective-permute-start | bytes 393224 | tf_op jit(solution)/shard_map/ppermute | solution.py:46
  49.1 1.9 %collective-permute-start.18 = (bf16[4,128,512]{2,1,0:T(8,128)(2,1)S(1)}, bf16[4,128,512]{2,1,0:T(8,128)(2,1)S(1)}, u32[]{:S(2)}, u32[]{:S(2)}) collective-permute-start(bf16[4,128,512]{2,1,0:T(8,128)(2,1)S(1)} %collective-permute-done.7), channel_id=1, source_target_pairs={{0,1},{1,0},{2,3},{3,2},{4,5},{5,4},{6,7},{7,6},{8,9},{9,8},{10,11... | collective-permute-start | bytes 1572872 | tf_op jit(solution)/shard_map/ppermute | solution.py:46
  49.3 3.2 %collective-permute-start.20 = (bf16[4,128,512]{2,1,0:T(8,128)(2,1)S(1)}, bf16[4,128,512]{2,1,0:T(8,128)(2,1)S(1)}, u32[]{:S(2)}, u32[]{:S(2)}) collective-permute-start(bf16[4,128,512]{2,1,0:T(8,128)(2,1)S(1)} %bitcast_dynamic-update-slice_fusion.16), channel_id=1, source_target_pairs={{0,1},{1,0},{2,3},{3,2},{4,5},{5,4},{6,7},{7,6},{8,9},{9,8},{10,11... | collective-permute-start | bytes 1572872 | tf_op jit(solution)/shard_map/ppermute | solution.py:46
  49.9 1.2 %copy-start.3 = (bf16[1,256,2048]{2,1,0:T(8,128)(2,1)S(1)}, bf16[1,256,2048]{2,1,0:T(8,128)(2,1)}, u32[]{:S(2)}) copy-start(bf16[1,256,2048]{2,1,0:T(8,128)(2,1)} %param.6) | copy-start | bytes 3145732
  53.3 2.0 %collective-permute-start.21 = (bf16[4,128,512]{2,1,0:T(8,128)(2,1)S(1)}, bf16[4,128,512]{2,1,0:T(8,128)(2,1)S(1)}, u32[]{:S(2)}, u32[]{:S(2)}) collective-permute-start(bf16[4,128,512]{2,1,0:T(8,128)(2,1)S(1)} %bitcast_dynamic-update-slice_fusion.8), channel_id=1, source_target_pairs={{0,1},{1,0},{2,3},{3,2},{4,5},{5,4},{6,7},{7,6},{8,9},{9,8},{10,11... | collective-permute-start | bytes 1572872 | tf_op jit(solution)/shard_map/ppermute | solution.py:46

commit v9 on v8

--- a/solution.py
+++ b/solution.py
@@ -118,7 +118,7 @@
         ring = [(i, (i + step) % n_resp) for i in range(n_resp)]
         others.append(lax.ppermute(residual, "resp", ring))
     near = [swap(residual, bits) for bits in (2, 4, 6)]
-    near_spins, near[1], near[0], far = lax.optimization_barrier((near_spins, near[1], near[0], far))
+    near_spins, near[0], near[1], far = lax.optimization_barrier((near_spins, near[0], near[1], far))
     all_spins = jnp.zeros((n_line, 2, 2, sub_len, batch), jnp.bfloat16)
     for side, core, group in (
         ("near", "core", line_spins),

time: 57.5 us -> 57.4 us (level)
  no operation moved by 1% of the time
where the time goes in v9:
time: 57.4 us; the launch traced here: 57.2 us
  waiting for transfers between devices  25.3 us (44%)
  starting transfers between devices  22.5 us (39%)
  matrix products  3.67 us (6%)
  local copies, waits for them, and re-layouts  3.14 us (5%)
  other arithmetic  2.09 us (4%)
    ppermute x21, waiting for transfers between devices, swap(): return lax.ppermute(array, 'item', [(i, i ^ bits) for i in range(n_item)])  25.3 us
    ppermute x21, starting transfers between devices, swap(): return lax.ppermute(array, 'item', [(i, i ^ bits) for i in range(n_item)])  20.9 us
    dot_general x2, matrix products, product(): grad = lax.dot_general(left, right, NT, preferred_element_type=jnp.float32)  2.09 us
    unnamed x11, local copies, waits for them, and re-layouts  1.65 us
    ppermute x1, starting transfers between devices, shards(): others.append(lax.ppermute(residual, 'resp', ring))  1.61 us
    broadcast_in_dim x1, other arithmetic, shards(): return (base + change).astype(jnp.bfloat16)[None]  1.23 us
  transfers between devices with their start and end apart: 22, of which 10 were waited for; matrix products, arithmetic and copies ran while one was open for 7% of the time, Pallas kernels for 0%

profile of v9, /device:TPU:0, one launch (start us, length us, event | category | flops | bytes accessed | tf_op | source)
XLA Modules:
  0.0 57.2 jit_solution(10446073263828494458)
XLA Ops:
  0.0 1.6 %copy.14 = bf16[1,256,2048]{1,2,0:T(8,128)(2,1)S(1)} copy(bf16[1,256,2048]{2,1,0:T(8,128)(2,1)} %param.5) | data formatting | bytes 2097152 | tf_op args[0]
  1.6 0.0 copy-start
  1.6 0.1 constant_dynamic-slice_fusion.9
  1.7 0.5 collective-permute-start
  2.3 0.7 %fusion.7 = bf16[256,512]{1,0:T(8,128)(2,1)S(1)} fusion(s32[512]{0:T(512)S(1)} %copy-done.4, s32[1024,256]{1,0:T(8,128)S(1)} %copy-done.2), kind=kOutput, calls=%fused_computation.16 | convolution fusion | flops 269877248 | bytes 1312768 | tf_op jit(solution)/shard_map/dot_general | solution.py:63
  3.0 0.1 collective-permute-start.1
  3.2 0.4 fusion.4
  3.6 0.4 fusion.33
  4.0 0.6 %collective-permute-done.1 = bf16[256,512]{1,0:T(8,128)(2,1)S(1)} collective-permute-done((bf16[256,512]{1,0:T(8,128)(2,1)S(1)}, bf16[256,512]{1,0:T(8,128)(2,1)S(1)}, u32[]{:S(2)}, u32[]{:S(2)}) %collective-permute-start.1) | collective-permute-done | bytes 262176 | tf_op jit(solution)/shard_map/ppermute | solution.py:46
  4.6 0.0 collective-permute-done
  4.6 0.4 convolution_add_fusion
  5.0 0.1 fusion.10
  5.1 0.1 dynamic-slice_bitcast_fusion
  5.2 0.1 constant_dynamic-slice_fusion.6
  5.4 2.7 %collective-permute-start.6 = (bf16[2,128,512]{2,1,0:T(8,128)(2,1)S(1)}, bf16[2,128,512]{2,1,0:T(8,128)(2,1)S(1)}, u32[]{:S(2)}, u32[]{:S(2)}) collective-permute-start(bf16[2,128,512]{2,1,0:T(8,128)(2,1)S(1)} %pad_maximum_fusion), channel_id=1, source_target_pairs={{0,2},{1,3},{2,0},{3,1},{4,6},{5,7},{6,4},{7,5},{8,10},{9,11},{10,... | collective-permute-start | bytes 786440 | tf_op jit(solution)/shard_map/ppermute | solution.py:46
  8.1 1.6 %collective-permute-start.2 = (bf16[128,512]{1,0:T(8,128)(2,1)S(1)}, bf16[128,512]{1,0:T(8,128)(2,1)S(1)}, u32[]{:S(2)}, u32[]{:S(2)}) collective-permute-start(bf16[128,512]{1,0:T(8,128)(2,1)S(1)} %dynamic-slice_bitcast_fusion.1), channel_id=1, source_target_pairs={{0,4},{1,5},{2,6},{3,7},{4,0},{5,1},{6,2},{7,3},{8,12},{9,13},{10,... | collective-permute-start | bytes 393224 | tf_op jit(solution)/shard_map/ppermute | solution.py:46
  9.7 2.6 %collective-permute-start.3 = (bf16[128,512]{1,0:T(8,128)(2,1)S(1)}, bf16[128,512]{1,0:T(8,128)(2,1)S(1)}, u32[]{:S(2)}, u32[]{:S(2)}) collective-permute-start(bf16[128,512]{1,0:T(8,128)(2,1)S(1)} %dynamic-slice_bitcast_fusion.1), channel_id=1, source_target_pairs={{0,8},{1,9},{2,10},{3,11},{4,12},{5,13},{6,14},{7,15},{8,0},{9,1},... | collective-permute-start | bytes 393224 | tf_op jit(solution)/shard_map/ppermute | solution.py:46
  12.3 0.2 collective-permute-start.4
  12.5 0.3 collective-permute-start.5
  12.8 0.1 constant_dynamic-slice_fusion.2
  12.9 2.3 %collective-permute-done.6 = bf16[2,128,512]{2,1,0:T(8,128)(2,1)S(1)} collective-permute-done((bf16[2,128,512]{2,1,0:T(8,128)(2,1)S(1)}, bf16[2,128,512]{2,1,0:T(8,128)(2,1)S(1)}, u32[]{:S(2)}, u32[]{:S(2)}) %collective-permute-start.6) | collective-permute-done | bytes 262176 | tf_op jit(solution)/shard_map/ppermute | solution.py:46
  15.2 0.1 fusion.11
  15.3 2.1 %collective-permute-start.8 = (bf16[2,128,512]{2,1,0:T(8,128)(2,1)S(1)}, bf16[2,128,512]{2,1,0:T(8,128)(2,1)S(1)}, u32[]{:S(2)}, u32[]{:S(2)}) collective-permute-start(bf16[2,128,512]{2,1,0:T(8,128)(2,1)S(1)} %fusion.11), channel_id=1, source_target_pairs={{0,4},{1,5},{2,6},{3,7},{4,0},{5,1},{6,2},{7,3},{8,12},{9,13},{10,... | collective-permute-start | bytes 786440 | tf_op jit(solution)/shard_map/ppermute | solution.py:46
  17.4 3.1 %collective-permute-done.5 = bf16[2,128,512]{2,1,0:T(8,128)(2,1)S(1)} collective-permute-done((bf16[2,128,512]{2,1,0:T(8,128)(2,1)S(1)}, bf16[2,128,512]{2,1,0:T(8,128)(2,1)S(1)}, u32[]{:S(2)}, u32[]{:S(2)}) %collective-permute-start.5) | collective-permute-done | bytes 262176 | tf_op jit(solution)/shard_map/ppermute | solution.py:46
  20.5 0.0 collective-permute-done.2
  20.5 2.1 %collective-permute-done.3 = bf16[128,512]{1,0:T(8,128)(2,1)S(1)} collective-permute-done((bf16[128,512]{1,0:T(8,128)(2,1)S(1)}, bf16[128,512]{1,0:T(8,128)(2,1)S(1)}, u32[]{:S(2)}, u32[]{:S(2)}) %collective-permute-start.3) | collective-permute-done | bytes 131104 | tf_op jit(solution)/shard_map/ppermute | solution.py:46
  22.6 0.0 collective-permute-done.4
  22.7 0.6 %collective-permute-start.7 = (bf16[4,128,512]{2,1,0:T(8,128)(2,1)S(1)}, bf16[4,128,512]{2,1,0:T(8,128)(2,1)S(1)}, u32[]{:S(2)}, u32[]{:S(2)}) collective-permute-start(bf16[4,128,512]{2,1,0:T(8,128)(2,1)S(1)} %bitcast_dynamic-update-slice_fusion.18), channel_id=1, source_target_pairs={{0,2},{1,3},{2,0},{3,1},{4,6},{5,7},{6,4},{7,5},{8,10},{9,11},{10,... | collective-permute-start | bytes 1572872 | tf_op jit(solution)/shard_map/ppermute | solution.py:46
  23.3 0.0 collective-permute-start.10
  23.3 3.2 %collective-permute-done.8 = bf16[2,128,512]{2,1,0:T(8,128)(2,1)S(1)} collective-permute-done((bf16[2,128,512]{2,1,0:T(8,128)(2,1)S(1)}, bf16[2,128,512]{2,1,0:T(8,128)(2,1)S(1)}, u32[]{:S(2)}, u32[]{:S(2)}) %collective-permute-start.8) | collective-permute-done | bytes 262176 | tf_op jit(solution)/shard_map/ppermute | solution.py:46
  26.5 0.1 fusion.12
  26.6 0.0 copy-start.1
  26.7 1.2 %collective-permute-start.9 = (bf16[128,512]{1,0:T(8,128)(2,1)S(1)}, bf16[128,512]{1,0:T(8,128)(2,1)S(1)}, u32[]{:S(2)}, u32[]{:S(2)}) collective-permute-start(bf16[128,512]{1,0:T(8,128)(2,1)S(1)} %fusion.26), channel_id=1, source_target_pairs={{0,8},{1,9},{2,10},{3,11},{4,12},{5,13},{6,14},{7,15},{8,0},{9,1},... | collective-permute-start | bytes 393224 | tf_op jit(solution)/shard_map/ppermute | solution.py:46
  27.8 0.2 broadcast_in_dim.92
  28.1 7.0 %collective-permute-done.9 = bf16[128,512]{1,0:T(8,128)(2,1)S(1)} collective-permute-done((bf16[128,512]{1,0:T(8,128)(2,1)S(1)}, bf16[128,512]{1,0:T(8,128)(2,1)S(1)}, u32[]{:S(2)}, u32[]{:S(2)}) %collective-permute-start.9) | collective-permute-done | bytes 131104 | tf_op jit(solution)/shard_map/ppermute | solution.py:46
  35.0 0.0 collective-permute-done.10
  35.1 0.2 bitcast_dynamic-update-slice_fusion.17
  35.3 1.3 %collective-permute-start.11 = (bf16[128,512]{1,0:T(8,128)(2,1)S(1)}, bf16[128,512]{1,0:T(8,128)(2,1)S(1)}, u32[]{:S(2)}, u32[]{:S(2)}) collective-permute-start(bf16[128,512]{1,0:T(8,128)(2,1)S(1)} %get-tuple-element.86), channel_id=1, source_target_pairs={{0,2},{1,3},{2,0},{3,1},{4,6},{5,7},{6,4},{7,5},{8,10},{9,11},{10,... | collective-permute-start | bytes 393224 | tf_op jit(solution)/shard_map/ppermute | solution.py:46
  36.6 0.0 collective-permute-start.12
  36.6 3.0 %collective-permute-start.13 = (bf16[128,512]{1,0:T(8,128)(2,1)S(1)}, bf16[128,512]{1,0:T(8,128)(2,1)S(1)}, u32[]{:S(2)}, u32[]{:S(2)}) collective-permute-start(bf16[128,512]{1,0:T(8,128)(2,1)S(1)} %get-tuple-element.86), channel_id=1, source_target_pairs={{0,8},{1,9},{2,10},{3,11},{4,12},{5,13},{6,14},{7,15},{8,0},{9,1},... | collective-permute-start | bytes 393224 | tf_op jit(solution)/shard_map/ppermute | solution.py:46
  39.6 0.5 collective-permute-start.19
  40.1 0.0 collective-permute-done.7
  40.2 1.6 %collective-permute-start.17 = (bf16[128,512]{1,0:T(8,128)(2,1)S(1)}, bf16[128,512]{1,0:T(8,128)(2,1)S(1)}, u32[]{:S(2)}, u32[]{:S(2)}) collective-permute-start(bf16[128,512]{1,0:T(8,128)(2,1)S(1)} %get-tuple-element.86), channel_id=1, source_target_pairs={{0,16},{16,0},{1,17},{17,1},{2,18},{18,2},{3,19},{19,3},{4,20},{20... | collective-permute-start | bytes 393224 | tf_op jit(solution)/shard_map/ppermute | solution.py:119
  41.8 0.0 collective-permute-done.11
  41.8 3.9 %collective-permute-done.12 = bf16[128,512]{1,0:T(8,128)(2,1)S(1)} collective-permute-done((bf16[128,512]{1,0:T(8,128)(2,1)S(1)}, bf16[128,512]{1,0:T(8,128)(2,1)S(1)}, u32[]{:S(2)}, u32[]{:S(2)}) %collective-permute-start.12) | collective-permute-done | bytes 131104 | tf_op jit(solution)/shard_map/ppermute | solution.py:46
  45.6 0.0 collective-permute-done.13
  45.6 1.6 %collective-permute-start.14 = (bf16[128,512]{1,0:T(8,128)(2,1)S(1)}, bf16[128,512]{1,0:T(8,128)(2,1)S(1)}, u32[]{:S(2)}, u32[]{:S(2)}) collective-permute-start(bf16[128,512]{1,0:T(8,128)(2,1)S(1)} %collective-permute-done.13), channel_id=1, source_target_pairs={{0,6},{1,7},{2,4},{3,5},{4,2},{5,3},{6,0},{7,1},{8,14},{9,15},{10,... | collective-permute-start | bytes 393224 | tf_op jit(solution)/shard_map/ppermute | solution.py:46
  47.2 0.5 collective-permute-start.15
  47.8 1.3 %collective-permute-start.16 = (bf16[128,512]{1,0:T(8,128)(2,1)S(1)}, bf16[128,512]{1,0:T(8,128)(2,1)S(1)}, u32[]{:S(2)}, u32[]{:S(2)}) collective-permute-start(bf16[128,512]{1,0:T(8,128)(2,1)S(1)} %collective-permute-done.13), channel_id=1, source_target_pairs={{0,2},{1,3},{2,0},{3,1},{4,6},{5,7},{6,4},{7,5},{8,10},{9,11},{10,... | collective-permute-start | bytes 393224 | tf_op jit(solution)/shard_map/ppermute | solution.py:46
  49.1 0.0 collective-permute-done.19
  49.1 0.0 collective-permute-start.18
  49.3 0.6 collective-permute-start.20
  49.9 0.0 copy-start.3
  49.9 0.2 broadcast_in_dim.97
  50.2 0.8 %collective-permute-done.18 = bf16[4,128,512]{2,1,0:T(8,128)(2,1)S(1)} collective-permute-done((bf16[4,128,512]{2,1,0:T(8,128)(2,1)S(1)}, bf16[4,128,512]{2,1,0:T(8,128)(2,1)S(1)}, u32[]{:S(2)}, u32[]{:S(2)}) %collective-permute-start.18) | collective-permute-done | bytes 524320 | tf_op jit(solution)/shard_map/ppermute | solution.py:46
  51.1 0.1 copy-done.3
  51.1 1.3 %fusion.3 = f32[256,2048]{1,0:T(8,128)S(1)} fusion(bf16[256,512]{1,0:T(8,128)(2,1)S(1)} %bitcast.112, bf16[2048,512]{1,0:T(8,128)(2,1)S(1)} %bitcast.107, bf16[1,256,2048]{2,1,0:T(8,128)(2,1)S(1)} %copy-done.3, bf16[1,256,2048]{2,1,0:T(8,128)(2,1)S(1)} %copy-done, s32[2048]{0:T(1024)S(1)} %iota_subtract_fusion, s32[256]{0:T(256)S(1)} %iota_subtract_fusion.1, ...), kind=kOutput, calls=%fused_computation.8 | convolution fusion | flops 543162368 | bytes 6563328 | tf_op jit(solution)/shard_map/dot_general | solution.py:142
  52.5 0.0 collective-permute-done.14
  52.5 0.4 collective-permute-done.15
  53.0 0.0 collective-permute-done.16
  53.1 0.1 collective-permute-start.21
  53.3 1.8 %collective-permute-done.21 = bf16[4,128,512]{2,1,0:T(8,128)(2,1)S(1)} collective-permute-done((bf16[4,128,512]{2,1,0:T(8,128)(2,1)S(1)}, bf16[4,128,512]{2,1,0:T(8,128)(2,1)S(1)}, u32[]{:S(2)}, u32[]{:S(2)}) %collective-permute-start.21) | collective-permute-done | bytes 524320 | tf_op jit(solution)/shard_map/ppermute | solution.py:46
  55.2 0.8 %fusion.2 = f32[256,2048]{1,0:T(8,128)S(1)} fusion(bf16[256,512]{1,0:T(8,128)(2,1)S(1)} %fusion.7, bf16[2048,512]{1,0:T(8,128)(2,1)S(1)} %bitcast.108, s32[2048]{0:T(1024)S(1)} %iota_subtract_fusion, s32[256]{0:T(256)S(1)} %iota_subtract_fusion.1, pred[256]{0:T(512)(128)(4,1)S(1)} %get-tuple-element.98, pred[256]{0:T(512)(128)(4,1)S(1)} %get-tuple-element.99), kind=kOutput, calls=%fused_computation.7 | convolution fusion | flops 539492352 | bytes 4466176 | tf_op jit(solution)/shard_map/dot_general | solution.py:142
  56.0 1.2 %fusion.8 = bf16[1,256,2048]{2,1,0:T(8,128)(2,1)} fusion(f32[256,2048]{1,0:T(8,128)S(1)} %fusion.3, f32[256,2048]{1,0:T(8,128)S(1)} %fusion.2), kind=kLoop, calls=%fused_computation.17 | loop fusion | flops 1048576 | bytes 5242880 | tf_op jit(solution)/shard_map/broadcast_in_dim | solution.py:163
  (40 shorter events, 0.8 us)
Async XLA Ops:
  0.0 2.3 %copy-start.2 = (s32[1024,256]{1,0:T(8,128)S(1)}, s32[1024,256]{1,0:T(8,128)}, u32[]{:S(2)}) copy-start(s32[1024,256]{1,0:T(8,128)} %param.8) | copy-start | bytes 3145732
  0.0 2.3 %copy-start.4 = (s32[512]{0:T(512)S(1)}, s32[512]{0:T(512)}, u32[]{:S(2)}) copy-start(s32[512]{0:T(512)} %param.9) | copy-start | bytes 6148
  1.6 1.5 %copy-start = (bf16[1,256,2048]{2,1,0:T(8,128)(2,1)S(1)}, bf16[1,256,2048]{2,1,0:T(8,128)(2,1)}, u32[]{:S(2)}) copy-start(bf16[1,256,2048]{2,1,0:T(8,128)(2,1)} %param.5) | copy-start | bytes 3145732
  1.7 2.9 %collective-permute-start = (bf16[256,1024]{0,1:T(8,128)(2,1)S(1)}, bf16[256,1024]{0,1:T(8,128)(2,1)S(1)}, u32[]{:S(2)}, u32[]{:S(2)}) collective-permute-start(bf16[256,1024]{0,1:T(8,128)(2,1)S(1)} %bitcast.111), channel_id=1, source_target_pairs={{0,1},{1,0},{2,3},{3,2},{4,5},{5,4},{6,7},{7,6},{8,9},{9,8},{10,11... | collective-permute-start | bytes 1572872 | tf_op jit(solution)/shard_map/ppermute | solution.py:46
  3.0 1.6 %collective-permute-start.1 = (bf16[256,512]{1,0:T(8,128)(2,1)S(1)}, bf16[256,512]{1,0:T(8,128)(2,1)S(1)}, u32[]{:S(2)}, u32[]{:S(2)}) collective-permute-start(bf16[256,512]{1,0:T(8,128)(2,1)S(1)} %fusion.7), channel_id=1, source_target_pairs={{0,1},{1,0},{2,3},{3,2},{4,5},{5,4},{6,7},{7,6},{8,9},{9,8},{10,11... | collective-permute-start | bytes 786440 | tf_op jit(solution)/shard_map/ppermute | solution.py:46
  5.4 9.8 %collective-permute-start.6 = (bf16[2,128,512]{2,1,0:T(8,128)(2,1)S(1)}, bf16[2,128,512]{2,1,0:T(8,128)(2,1)S(1)}, u32[]{:S(2)}, u32[]{:S(2)}) collective-permute-start(bf16[2,128,512]{2,1,0:T(8,128)(2,1)S(1)} %pad_maximum_fusion), channel_id=1, source_target_pairs={{0,2},{1,3},{2,0},{3,1},{4,6},{5,7},{6,4},{7,5},{8,10},{9,11},{10,... | collective-permute-start | bytes 786440 | tf_op jit(solution)/shard_map/ppermute | solution.py:46
  8.1 12.4 %collective-permute-start.2 = (bf16[128,512]{1,0:T(8,128)(2,1)S(1)}, bf16[128,512]{1,0:T(8,128)(2,1)S(1)}, u32[]{:S(2)}, u32[]{:S(2)}) collective-permute-start(bf16[128,512]{1,0:T(8,128)(2,1)S(1)} %dynamic-slice_bitcast_fusion.1), channel_id=1, source_target_pairs={{0,4},{1,5},{2,6},{3,7},{4,0},{5,1},{6,2},{7,3},{8,12},{9,13},{10,... | collective-permute-start | bytes 393224 | tf_op jit(solution)/shard_map/ppermute | solution.py:46
  9.7 12.9 %collective-permute-start.3 = (bf16[128,512]{1,0:T(8,128)(2,1)S(1)}, bf16[128,512]{1,0:T(8,128)(2,1)S(1)}, u32[]{:S(2)}, u32[]{:S(2)}) collective-permute-start(bf16[128,512]{1,0:T(8,128)(2,1)S(1)} %dynamic-slice_bitcast_fusion.1), channel_id=1, source_target_pairs={{0,8},{1,9},{2,10},{3,11},{4,12},{5,13},{6,14},{7,15},{8,0},{9,1},... | collective-permute-start | bytes 393224 | tf_op jit(solution)/shard_map/ppermute | solution.py:46
  12.3 10.4 %collective-permute-start.4 = (bf16[128,512]{1,0:T(8,128)(2,1)S(1)}, bf16[128,512]{1,0:T(8,128)(2,1)S(1)}, u32[]{:S(2)}, u32[]{:S(2)}) collective-permute-start(bf16[128,512]{1,0:T(8,128)(2,1)S(1)} %dynamic-slice_bitcast_fusion.1), channel_id=1, source_target_pairs={{0,12},{1,13},{2,14},{3,15},{4,8},{5,9},{6,10},{7,11},{8,4},{9,5},... | collective-permute-start | bytes 393224 | tf_op jit(solution)/shard_map/ppermute | solution.py:46
  12.5 8.1 %collective-permute-start.5 = (bf16[2,128,512]{2,1,0:T(8,128)(2,1)S(1)}, bf16[2,128,512]{2,1,0:T(8,128)(2,1)S(1)}, u32[]{:S(2)}, u32[]{:S(2)}) collective-permute-start(bf16[2,128,512]{2,1,0:T(8,128)(2,1)S(1)} %pad_maximum_fusion.1), channel_id=1, source_target_pairs={{0,2},{1,3},{2,0},{3,1},{4,6},{5,7},{6,4},{7,5},{8,10},{9,11},{10,... | collective-permute-start | bytes 786440 | tf_op jit(solution)/shard_map/ppermute | solution.py:46
  15.3 11.2 %collective-permute-start.8 = (bf16[2,128,512]{2,1,0:T(8,128)(2,1)S(1)}, bf16[2,128,512]{2,1,0:T(8,128)(2,1)S(1)}, u32[]{:S(2)}, u32[]{:S(2)}) collective-permute-start(bf16[2,128,512]{2,1,0:T(8,128)(2,1)S(1)} %fusion.11), channel_id=1, source_target_pairs={{0,4},{1,5},{2,6},{3,7},{4,0},{5,1},{6,2},{7,3},{8,12},{9,13},{10,... | collective-permute-start | bytes 786440 | tf_op jit(solution)/shard_map/ppermute | solution.py:46
  22.7 17.5 %collective-permute-start.7 = (bf16[4,128,512]{2,1,0:T(8,128)(2,1)S(1)}, bf16[4,128,512]{2,1,0:T(8,128)(2,1)S(1)}, u32[]{:S(2)}, u32[]{:S(2)}) collective-permute-start(bf16[4,128,512]{2,1,0:T(8,128)(2,1)S(1)} %bitcast_dynamic-update-slice_fusion.18), channel_id=1, source_target_pairs={{0,2},{1,3},{2,0},{3,1},{4,6},{5,7},{6,4},{7,5},{8,10},{9,11},{10,... | collective-permute-start | bytes 1572872 | tf_op jit(solution)/shard_map/ppermute | solution.py:46
  23.3 11.7 %collective-permute-start.10 = (bf16[4,128,512]{2,1,0:T(8,128)(2,1)S(1)}, bf16[4,128,512]{2,1,0:T(8,128)(2,1)S(1)}, u32[]{:S(2)}, u32[]{:S(2)}) collective-permute-start(bf16[4,128,512]{2,1,0:T(8,128)(2,1)S(1)} %bitcast_dynamic-update-slice_fusion.18), channel_id=1, source_target_pairs={{0,1},{1,0},{2,3},{3,2},{4,5},{5,4},{6,7},{7,6},{8,9},{9,8},{10,11... | collective-permute-start | bytes 1572872 | tf_op jit(solution)/shard_map/ppermute | solution.py:46
  26.6 8.4 %copy-start.1 = (f32[1,128]{1,0:T(1,128)S(1)}, f32[1,128]{1,0:T(1,128)}, u32[]{:S(2)}) copy-start(f32[1,128]{1,0:T(1,128)} %param.7) | copy-start | bytes 1540
  26.7 8.4 %collective-permute-start.9 = (bf16[128,512]{1,0:T(8,128)(2,1)S(1)}, bf16[128,512]{1,0:T(8,128)(2,1)S(1)}, u32[]{:S(2)}, u32[]{:S(2)}) collective-permute-start(bf16[128,512]{1,0:T(8,128)(2,1)S(1)} %fusion.26), channel_id=1, source_target_pairs={{0,8},{1,9},{2,10},{3,11},{4,12},{5,13},{6,14},{7,15},{8,0},{9,1},... | collective-permute-start | bytes 393224 | tf_op jit(solution)/shard_map/ppermute | solution.py:46
  35.3 6.5 %collective-permute-start.11 = (bf16[128,512]{1,0:T(8,128)(2,1)S(1)}, bf16[128,512]{1,0:T(8,128)(2,1)S(1)}, u32[]{:S(2)}, u32[]{:S(2)}) collective-permute-start(bf16[128,512]{1,0:T(8,128)(2,1)S(1)} %get-tuple-element.86), channel_id=1, source_target_pairs={{0,2},{1,3},{2,0},{3,1},{4,6},{5,7},{6,4},{7,5},{8,10},{9,11},{10,... | collective-permute-start | bytes 393224 | tf_op jit(solution)/shard_map/ppermute | solution.py:46
  36.6 9.0 %collective-permute-start.12 = (bf16[128,512]{1,0:T(8,128)(2,1)S(1)}, bf16[128,512]{1,0:T(8,128)(2,1)S(1)}, u32[]{:S(2)}, u32[]{:S(2)}) collective-permute-start(bf16[128,512]{1,0:T(8,128)(2,1)S(1)} %get-tuple-element.86), channel_id=1, source_target_pairs={{0,4},{1,5},{2,6},{3,7},{4,0},{5,1},{6,2},{7,3},{8,12},{9,13},{10,... | collective-permute-start | bytes 393224 | tf_op jit(solution)/shard_map/ppermute | solution.py:46
  36.6 9.0 %collective-permute-start.13 = (bf16[128,512]{1,0:T(8,128)(2,1)S(1)}, bf16[128,512]{1,0:T(8,128)(2,1)S(1)}, u32[]{:S(2)}, u32[]{:S(2)}) collective-permute-start(bf16[128,512]{1,0:T(8,128)(2,1)S(1)} %get-tuple-element.86), channel_id=1, source_target_pairs={{0,8},{1,9},{2,10},{3,11},{4,12},{5,13},{6,14},{7,15},{8,0},{9,1},... | collective-permute-start | bytes 393224 | tf_op jit(solution)/shard_map/ppermute | solution.py:46
  39.6 9.5 %collective-permute-start.19 = (bf16[128,512]{1,0:T(8,128)(2,1)S(1)}, bf16[128,512]{1,0:T(8,128)(2,1)S(1)}, u32[]{:S(2)}, u32[]{:S(2)}) collective-permute-start(bf16[128,512]{1,0:T(8,128)(2,1)S(1)} %get-tuple-element.86), channel_id=1, source_target_pairs={{0,6},{1,7},{2,4},{3,5},{4,2},{5,3},{6,0},{7,1},{8,14},{9,15},{10,... | collective-permute-start | bytes 393224 | tf_op jit(solution)/shard_map/ppermute | solution.py:46
  40.2 9.1 %collective-permute-start.17 = (bf16[128,512]{1,0:T(8,128)(2,1)S(1)}, bf16[128,512]{1,0:T(8,128)(2,1)S(1)}, u32[]{:S(2)}, u32[]{:S(2)}) collective-permute-start(bf16[128,512]{1,0:T(8,128)(2,1)S(1)} %get-tuple-element.86), channel_id=1, source_target_pairs={{0,16},{16,0},{1,17},{17,1},{2,18},{18,2},{3,19},{19,3},{4,20},{20... | collective-permute-start | bytes 393224 | tf_op jit(solution)/shard_map/ppermute | solution.py:119
  45.6 6.9 %collective-permute-start.14 = (bf16[128,512]{1,0:T(8,128)(2,1)S(1)}, bf16[128,512]{1,0:T(8,128)(2,1)S(1)}, u32[]{:S(2)}, u32[]{:S(2)}) collective-permute-start(bf16[128,512]{1,0:T(8,128)(2,1)S(1)} %collective-permute-done.13), channel_id=1, source_target_pairs={{0,6},{1,7},{2,4},{3,5},{4,2},{5,3},{6,0},{7,1},{8,14},{9,15},{10,... | collective-permute-start | bytes 393224 | tf_op jit(solution)/shard_map/ppermute | solution.py:46
  47.2 5.7 %collective-permute-start.15 = (bf16[128,512]{1,0:T(8,128)(2,1)S(1)}, bf16[128,512]{1,0:T(8,128)(2,1)S(1)}, u32[]{:S(2)}, u32[]{:S(2)}) collective-permute-start(bf16[128,512]{1,0:T(8,128)(2,1)S(1)} %collective-permute-done.13), channel_id=1, source_target_pairs={{0,4},{1,5},{2,6},{3,7},{4,0},{5,1},{6,2},{7,3},{8,12},{9,13},{10,... | collective-permute-start | bytes 393224 | tf_op jit(solution)/shard_map/ppermute | solution.py:46
  47.8 5.2 %collective-permute-start.16 = (bf16[128,512]{1,0:T(8,128)(2,1)S(1)}, bf16[128,512]{1,0:T(8,128)(2,1)S(1)}, u32[]{:S(2)}, u32[]{:S(2)}) collective-permute-start(bf16[128,512]{1,0:T(8,128)(2,1)S(1)} %collective-permute-done.13), channel_id=1, source_target_pairs={{0,2},{1,3},{2,0},{3,1},{4,6},{5,7},{6,4},{7,5},{8,10},{9,11},{10,... | collective-permute-start | bytes 393224 | tf_op jit(solution)/shard_map/ppermute | solution.py:46
  49.1 1.9 %collective-permute-start.18 = (bf16[4,128,512]{2,1,0:T(8,128)(2,1)S(1)}, bf16[4,128,512]{2,1,0:T(8,128)(2,1)S(1)}, u32[]{:S(2)}, u32[]{:S(2)}) collective-permute-start(bf16[4,128,512]{2,1,0:T(8,128)(2,1)S(1)} %collective-permute-done.7), channel_id=1, source_target_pairs={{0,1},{1,0},{2,3},{3,2},{4,5},{5,4},{6,7},{7,6},{8,9},{9,8},{10,11... | collective-permute-start | bytes 1572872 | tf_op jit(solution)/shard_map/ppermute | solution.py:46
  49.3 3.2 %collective-permute-start.20 = (bf16[4,128,512]{2,1,0:T(8,128)(2,1)S(1)}, bf16[4,128,512]{2,1,0:T(8,128)(2,1)S(1)}, u32[]{:S(2)}, u32[]{:S(2)}) collective-permute-start(bf16[4,128,512]{2,1,0:T(8,128)(2,1)S(1)} %bitcast_dynamic-update-slice_fusion.16), channel_id=1, source_target_pairs={{0,1},{1,0},{2,3},{3,2},{4,5},{5,4},{6,7},{7,6},{8,9},{9,8},{10,11... | collective-permute-start | bytes 1572872 | tf_op jit(solution)/shard_map/ppermute | solution.py:46
  49.9 1.2 %copy-start.3 = (bf16[1,256,2048]{2,1,0:T(8,128)(2,1)S(1)}, bf16[1,256,2048]{2,1,0:T(8,128)(2,1)}, u32[]{:S(2)}) copy-start(bf16[1,256,2048]{2,1,0:T(8,128)(2,1)} %param.6) | copy-start | bytes 3145732
  53.1 2.0 %collective-permute-start.21 = (bf16[4,128,512]{2,1,0:T(8,128)(2,1)S(1)}, bf16[4,128,512]{2,1,0:T(8,128)(2,1)S(1)}, u32[]{:S(2)}, u32[]{:S(2)}) collective-permute-start(bf16[4,128,512]{2,1,0:T(8,128)(2,1)S(1)} %bitcast_dynamic-update-slice_fusion.8), channel_id=1, source_target_pairs={{0,1},{1,0},{2,3},{3,2},{4,5},{5,4},{6,7},{7,6},{8,9},{9,8},{10,11... | collective-permute-start | bytes 1572872 | tf_op jit(solution)/shard_map/ppermute | solution.py:46

commit v10 on v9

--- a/solution.py
+++ b/solution.py
@@ -88,7 +88,7 @@
     given_sums = added(given_steps, came[0]).astype(jnp.bfloat16)
     passed = swap(given_sums, 4)
     came_kept, _ = lax.optimization_barrier((came[1], given_sums))
-    line, _ = lax.optimization_barrier((line, came_kept))
+    line, _ = lax.optimization_barrier((line, given_sums))
     kept_sums = added(kept_steps, came_kept)
     line_spins = jnp.zeros((n_line, sub_len, batch), jnp.bfloat16)
     for index, block in zip(where["line"], [own_spins] + line):

time: 57.4 us -> 57.4 us (level)
  transfers between devices with their start and end apart: 22 -> 22, of which waited for: 10 -> 9; matrix products, arithmetic and copies ran while one was open for 7% -> 7% of each run, Pallas kernels for 0% -> 0%
where the time goes in v10:
time: 57.4 us; the launch traced here: 57.2 us
  waiting for transfers between devices  25.3 us (44%)
  starting transfers between devices  22.5 us (39%)
  matrix products  3.66 us (6%)
  local copies, waits for them, and re-layouts  3.14 us (5%)
  other arithmetic  2.09 us (4%)
    ppermute x21, waiting for transfers between devices, swap(): return lax.ppermute(array, 'item', [(i, i ^ bits) for i in range(n_item)])  25.3 us
    ppermute x21, starting transfers between devices, swap(): return lax.ppermute(array, 'item', [(i, i ^ bits) for i in range(n_item)])  20.9 us
    dot_general x2, matrix products, product(): grad = lax.dot_general(left, right, NT, preferred_element_type=jnp.float32)  2.08 us
    unnamed x11, local copies, waits for them, and re-layouts  1.65 us
    ppermute x1, starting transfers between devices, shards(): others.append(lax.ppermute(residual, 'resp', ring))  1.61 us
    broadcast_in_dim x1, other arithmetic, shards(): return (base + change).astype(jnp.bfloat16)[None]  1.23 us
  transfers between devices with their start and end apart: 22, of which 9 were waited for; matrix products, arithmetic and copies ran while one was open for 7% of the time, Pallas kernels for 0%

profile of v10, /device:TPU:0, one launch (start us, length us, event | category | flops | bytes accessed | tf_op | source)
XLA Modules:
  0.0 57.2 jit_solution(10561332663150150512)
XLA Ops:
  0.0 1.6 %copy.14 = bf16[1,256,2048]{1,2,0:T(8,128)(2,1)S(1)} copy(bf16[1,256,2048]{2,1,0:T(8,128)(2,1)} %param.5) | data formatting | bytes 2097152 | tf_op args[0]
  1.6 0.0 copy-start
  1.6 0.1 constant_dynamic-slice_fusion.9
  1.7 0.5 collective-permute-start
  2.3 0.7 %fusion.7 = bf16[256,512]{1,0:T(8,128)(2,1)S(1)} fusion(s32[512]{0:T(512)S(1)} %copy-done.4, s32[1024,256]{1,0:T(8,128)S(1)} %copy-done.2), kind=kOutput, calls=%fused_computation.16 | convolution fusion | flops 269877248 | bytes 1312768 | tf_op jit(solution)/shard_map/dot_general | solution.py:63
  3.0 0.1 collective-permute-start.1
  3.2 0.4 fusion.4
  3.6 0.4 fusion.33
  4.0 0.6 %collective-permute-done.1 = bf16[256,512]{1,0:T(8,128)(2,1)S(1)} collective-permute-done((bf16[256,512]{1,0:T(8,128)(2,1)S(1)}, bf16[256,512]{1,0:T(8,128)(2,1)S(1)}, u32[]{:S(2)}, u32[]{:S(2)}) %collective-permute-start.1) | collective-permute-done | bytes 262176 | tf_op jit(solution)/shard_map/ppermute | solution.py:46
  4.6 0.0 collective-permute-done
  4.6 0.4 convolution_add_fusion
  5.0 0.1 fusion.10
  5.1 0.1 dynamic-slice_bitcast_fusion
  5.2 0.1 constant_dynamic-slice_fusion.4
  5.4 2.7 %collective-permute-start.5 = (bf16[2,128,512]{2,1,0:T(8,128)(2,1)S(1)}, bf16[2,128,512]{2,1,0:T(8,128)(2,1)S(1)}, u32[]{:S(2)}, u32[]{:S(2)}) collective-permute-start(bf16[2,128,512]{2,1,0:T(8,128)(2,1)S(1)} %pad_maximum_fusion), channel_id=1, source_target_pairs={{0,2},{1,3},{2,0},{3,1},{4,6},{5,7},{6,4},{7,5},{8,10},{9,11},{10,... | collective-permute-start | bytes 786440 | tf_op jit(solution)/shard_map/ppermute | solution.py:46
  8.1 1.6 %collective-permute-start.2 = (bf16[128,512]{1,0:T(8,128)(2,1)S(1)}, bf16[128,512]{1,0:T(8,128)(2,1)S(1)}, u32[]{:S(2)}, u32[]{:S(2)}) collective-permute-start(bf16[128,512]{1,0:T(8,128)(2,1)S(1)} %dynamic-slice_bitcast_fusion.1), channel_id=1, source_target_pairs={{0,4},{1,5},{2,6},{3,7},{4,0},{5,1},{6,2},{7,3},{8,12},{9,13},{10,... | collective-permute-start | bytes 393224 | tf_op jit(solution)/shard_map/ppermute | solution.py:46
  9.7 2.6 %collective-permute-start.3 = (bf16[128,512]{1,0:T(8,128)(2,1)S(1)}, bf16[128,512]{1,0:T(8,128)(2,1)S(1)}, u32[]{:S(2)}, u32[]{:S(2)}) collective-permute-start(bf16[128,512]{1,0:T(8,128)(2,1)S(1)} %dynamic-slice_bitcast_fusion.1), channel_id=1, source_target_pairs={{0,8},{1,9},{2,10},{3,11},{4,12},{5,13},{6,14},{7,15},{8,0},{9,1},... | collective-permute-start | bytes 393224 | tf_op jit(solution)/shard_map/ppermute | solution.py:46
  12.3 0.2 collective-permute-start.4
  12.5 0.3 collective-permute-start.7
  12.8 0.1 constant_dynamic-slice_fusion.2
  12.9 2.3 %collective-permute-done.5 = bf16[2,128,512]{2,1,0:T(8,128)(2,1)S(1)} collective-permute-done((bf16[2,128,512]{2,1,0:T(8,128)(2,1)S(1)}, bf16[2,128,512]{2,1,0:T(8,128)(2,1)S(1)}, u32[]{:S(2)}, u32[]{:S(2)}) %collective-permute-start.5) | collective-permute-done | bytes 262176 | tf_op jit(solution)/shard_map/ppermute | solution.py:46
  15.2 0.1 fusion.11
  15.3 2.1 %collective-permute-start.8 = (bf16[2,128,512]{2,1,0:T(8,128)(2,1)S(1)}, bf16[2,128,512]{2,1,0:T(8,128)(2,1)S(1)}, u32[]{:S(2)}, u32[]{:S(2)}) collective-permute-start(bf16[2,128,512]{2,1,0:T(8,128)(2,1)S(1)} %fusion.11), channel_id=1, source_target_pairs={{0,4},{1,5},{2,6},{3,7},{4,0},{5,1},{6,2},{7,3},{8,12},{9,13},{10,... | collective-permute-start | bytes 786440 | tf_op jit(solution)/shard_map/ppermute | solution.py:46
  17.4 0.0 collective-permute-done.2
  17.5 5.2 %collective-permute-done.3 = bf16[128,512]{1,0:T(8,128)(2,1)S(1)} collective-permute-done((bf16[128,512]{1,0:T(8,128)(2,1)S(1)}, bf16[128,512]{1,0:T(8,128)(2,1)S(1)}, u32[]{:S(2)}, u32[]{:S(2)}) %collective-permute-start.3) | collective-permute-done | bytes 131104 | tf_op jit(solution)/shard_map/ppermute | solution.py:46
  22.6 0.0 collective-permute-done.4
  22.7 0.6 %collective-permute-start.6 = (bf16[4,128,512]{2,1,0:T(8,128)(2,1)S(1)}, bf16[4,128,512]{2,1,0:T(8,128)(2,1)S(1)}, u32[]{:S(2)}, u32[]{:S(2)}) collective-permute-start(bf16[4,128,512]{2,1,0:T(8,128)(2,1)S(1)} %bitcast_dynamic-update-slice_fusion.18), channel_id=1, source_target_pairs={{0,2},{1,3},{2,0},{3,1},{4,6},{5,7},{6,4},{7,5},{8,10},{9,11},{10,... | collective-permute-start | bytes 1572872 | tf_op jit(solution)/shard_map/ppermute | solution.py:46
  23.3 0.0 collective-permute-start.10
  23.3 0.0 collective-permute-done.7
  23.3 3.2 %collective-permute-done.8 = bf16[2,128,512]{2,1,0:T(8,128)(2,1)S(1)} collective-permute-done((bf16[2,128,512]{2,1,0:T(8,128)(2,1)S(1)}, bf16[2,128,512]{2,1,0:T(8,128)(2,1)S(1)}, u32[]{:S(2)}, u32[]{:S(2)}) %collective-permute-start.8) | collective-permute-done | bytes 262176 | tf_op jit(solution)/shard_map/ppermute | solution.py:46
  26.5 0.1 fusion.12
  26.6 0.0 copy-start.1
  26.7 1.2 %collective-permute-start.9 = (bf16[128,512]{1,0:T(8,128)(2,1)S(1)}, bf16[128,512]{1,0:T(8,128)(2,1)S(1)}, u32[]{:S(2)}, u32[]{:S(2)}) collective-permute-start(bf16[128,512]{1,0:T(8,128)(2,1)S(1)} %fusion.26), channel_id=1, source_target_pairs={{0,8},{1,9},{2,10},{3,11},{4,12},{5,13},{6,14},{7,15},{8,0},{9,1},... | collective-permute-start | bytes 393224 | tf_op jit(solution)/shard_map/ppermute | solution.py:46
  27.8 0.2 broadcast_in_dim.92
  28.1 7.0 %collective-permute-done.9 = bf16[128,512]{1,0:T(8,128)(2,1)S(1)} collective-permute-done((bf16[128,512]{1,0:T(8,128)(2,1)S(1)}, bf16[128,512]{1,0:T(8,128)(2,1)S(1)}, u32[]{:S(2)}, u32[]{:S(2)}) %collective-permute-start.9) | collective-permute-done | bytes 131104 | tf_op jit(solution)/shard_map/ppermute | solution.py:46
  35.0 0.0 collective-permute-done.10
  35.1 0.2 bitcast_dynamic-update-slice_fusion.17
  35.3 1.3 %collective-permute-start.11 = (bf16[128,512]{1,0:T(8,128)(2,1)S(1)}, bf16[128,512]{1,0:T(8,128)(2,1)S(1)}, u32[]{:S(2)}, u32[]{:S(2)}) collective-permute-start(bf16[128,512]{1,0:T(8,128)(2,1)S(1)} %get-tuple-element.86), channel_id=1, source_target_pairs={{0,2},{1,3},{2,0},{3,1},{4,6},{5,7},{6,4},{7,5},{8,10},{9,11},{10,... | collective-permute-start | bytes 393224 | tf_op jit(solution)/shard_map/ppermute | solution.py:46
  36.6 0.0 collective-permute-start.12
  36.6 3.0 %collective-permute-start.13 = (bf16[128,512]{1,0:T(8,128)(2,1)S(1)}, bf16[128,512]{1,0:T(8,128)(2,1)S(1)}, u32[]{:S(2)}, u32[]{:S(2)}) collective-permute-start(bf16[128,512]{1,0:T(8,128)(2,1)S(1)} %get-tuple-element.86), channel_id=1, source_target_pairs={{0,8},{1,9},{2,10},{3,11},{4,12},{5,13},{6,14},{7,15},{8,0},{9,1},... | collective-permute-start | bytes 393224 | tf_op jit(solution)/shard_map/ppermute | solution.py:46
  39.6 0.5 collective-permute-start.19
  40.1 0.0 collective-permute-done.6
  40.2 1.6 %collective-permute-start.17 = (bf16[128,512]{1,0:T(8,128)(2,1)S(1)}, bf16[128,512]{1,0:T(8,128)(2,1)S(1)}, u32[]{:S(2)}, u32[]{:S(2)}) collective-permute-start(bf16[128,512]{1,0:T(8,128)(2,1)S(1)} %get-tuple-element.86), channel_id=1, source_target_pairs={{0,16},{16,0},{1,17},{17,1},{2,18},{18,2},{3,19},{19,3},{4,20},{20... | collective-permute-start | bytes 393224 | tf_op jit(solution)/shard_map/ppermute | solution.py:119
  41.8 0.0 collective-permute-done.11
  41.8 3.9 %collective-permute-done.12 = bf16[128,512]{1,0:T(8,128)(2,1)S(1)} collective-permute-done((bf16[128,512]{1,0:T(8,128)(2,1)S(1)}, bf16[128,512]{1,0:T(8,128)(2,1)S(1)}, u32[]{:S(2)}, u32[]{:S(2)}) %collective-permute-start.12) | collective-permute-done | bytes 131104 | tf_op jit(solution)/shard_map/ppermute | solution.py:46
  45.6 1.6 %collective-permute-start.14 = (bf16[128,512]{1,0:T(8,128)(2,1)S(1)}, bf16[128,512]{1,0:T(8,128)(2,1)S(1)}, u32[]{:S(2)}, u32[]{:S(2)}) collective-permute-start(bf16[128,512]{1,0:T(8,128)(2,1)S(1)} %collective-permute-done.13), channel_id=1, source_target_pairs={{0,6},{1,7},{2,4},{3,5},{4,2},{5,3},{6,0},{7,1},{8,14},{9,15},{10,... | collective-permute-start | bytes 393224 | tf_op jit(solution)/shard_map/ppermute | solution.py:46
  47.2 0.5 collective-permute-start.15
  47.8 1.3 %collective-permute-start.16 = (bf16[128,512]{1,0:T(8,128)(2,1)S(1)}, bf16[128,512]{1,0:T(8,128)(2,1)S(1)}, u32[]{:S(2)}, u32[]{:S(2)}) collective-permute-start(bf16[128,512]{1,0:T(8,128)(2,1)S(1)} %collective-permute-done.13), channel_id=1, source_target_pairs={{0,2},{1,3},{2,0},{3,1},{4,6},{5,7},{6,4},{7,5},{8,10},{9,11},{10,... | collective-permute-start | bytes 393224 | tf_op jit(solution)/shard_map/ppermute | solution.py:46
  49.1 0.0 collective-permute-done.19
  49.1 0.0 collective-permute-start.18
  49.3 0.0 collective-permute-done.17
  49.3 0.6 collective-permute-start.20
  49.9 0.0 copy-start.3
  49.9 0.2 broadcast_in_dim.97
  50.2 0.8 %collective-permute-done.18 = bf16[4,128,512]{2,1,0:T(8,128)(2,1)S(1)} collective-permute-done((bf16[4,128,512]{2,1,0:T(8,128)(2,1)S(1)}, bf16[4,128,512]{2,1,0:T(8,128)(2,1)S(1)}, u32[]{:S(2)}, u32[]{:S(2)}) %collective-permute-start.18) | collective-permute-done | bytes 524320 | tf_op jit(solution)/shard_map/ppermute | solution.py:46
  51.1 0.1 copy-done.3
  51.2 1.3 %fusion.3 = f32[256,2048]{1,0:T(8,128)S(1)} fusion(bf16[256,512]{1,0:T(8,128)(2,1)S(1)} %bitcast.112, bf16[2048,512]{1,0:T(8,128)(2,1)S(1)} %bitcast.107, bf16[1,256,2048]{2,1,0:T(8,128)(2,1)S(1)} %copy-done.3, bf16[1,256,2048]{2,1,0:T(8,128)(2,1)S(1)} %copy-done, s32[2048]{0:T(1024)S(1)} %iota_subtract_fusion, s32[256]{0:T(256)S(1)} %iota_subtract_fusion.1, ...), kind=kOutput, calls=%fused_computation.8 | convolution fusion | flops 543162368 | bytes 6563328 | tf_op jit(solution)/shard_map/dot_general | solution.py:142
  52.5 0.0 collective-permute-done.14
  52.5 0.5 collective-permute-done.15
  53.0 0.0 collective-permute-done.16
  53.1 0.1 collective-permute-start.21
  53.3 1.8 %collective-permute-done.21 = bf16[4,128,512]{2,1,0:T(8,128)(2,1)S(1)} collective-permute-done((bf16[4,128,512]{2,1,0:T(8,128)(2,1)S(1)}, bf16[4,128,512]{2,1,0:T(8,128)(2,1)S(1)}, u32[]{:S(2)}, u32[]{:S(2)}) %collective-permute-start.21) | collective-permute-done | bytes 524320 | tf_op jit(solution)/shard_map/ppermute | solution.py:46
  55.2 0.8 %fusion.2 = f32[256,2048]{1,0:T(8,128)S(1)} fusion(bf16[256,512]{1,0:T(8,128)(2,1)S(1)} %fusion.7, bf16[2048,512]{1,0:T(8,128)(2,1)S(1)} %bitcast.108, s32[2048]{0:T(1024)S(1)} %iota_subtract_fusion, s32[256]{0:T(256)S(1)} %iota_subtract_fusion.1, pred[256]{0:T(512)(128)(4,1)S(1)} %get-tuple-element.98, pred[256]{0:T(512)(128)(4,1)S(1)} %get-tuple-element.99), kind=kOutput, calls=%fused_computation.7 | convolution fusion | flops 539492352 | bytes 4466176 | tf_op jit(solution)/shard_map/dot_general | solution.py:142
  56.0 1.2 %fusion.8 = bf16[1,256,2048]{2,1,0:T(8,128)(2,1)} fusion(f32[256,2048]{1,0:T(8,128)S(1)} %fusion.3, f32[256,2048]{1,0:T(8,128)S(1)} %fusion.2), kind=kLoop, calls=%fused_computation.17 | loop fusion | flops 1048576 | bytes 5242880 | tf_op jit(solution)/shard_map/broadcast_in_dim | solution.py:163
  (40 shorter events, 0.8 us)
Async XLA Ops:
  0.0 2.3 %copy-start.2 = (s32[1024,256]{1,0:T(8,128)S(1)}, s32[1024,256]{1,0:T(8,128)}, u32[]{:S(2)}) copy-start(s32[1024,256]{1,0:T(8,128)} %param.8) | copy-start | bytes 3145732
  0.0 2.3 %copy-start.4 = (s32[512]{0:T(512)S(1)}, s32[512]{0:T(512)}, u32[]{:S(2)}) copy-start(s32[512]{0:T(512)} %param.9) | copy-start | bytes 6148
  1.6 1.5 %copy-start = (bf16[1,256,2048]{2,1,0:T(8,128)(2,1)S(1)}, bf16[1,256,2048]{2,1,0:T(8,128)(2,1)}, u32[]{:S(2)}) copy-start(bf16[1,256,2048]{2,1,0:T(8,128)(2,1)} %param.5) | copy-start | bytes 3145732
  1.7 2.9 %collective-permute-start = (bf16[256,1024]{0,1:T(8,128)(2,1)S(1)}, bf16[256,1024]{0,1:T(8,128)(2,1)S(1)}, u32[]{:S(2)}, u32[]{:S(2)}) collective-permute-start(bf16[256,1024]{0,1:T(8,128)(2,1)S(1)} %bitcast.111), channel_id=1, source_target_pairs={{0,1},{1,0},{2,3},{3,2},{4,5},{5,4},{6,7},{7,6},{8,9},{9,8},{10,11... | collective-permute-start | bytes 1572872 | tf_op jit(solution)/shard_map/ppermute | solution.py:46
  3.0 1.6 %collective-permute-start.1 = (bf16[256,512]{1,0:T(8,128)(2,1)S(1)}, bf16[256,512]{1,0:T(8,128)(2,1)S(1)}, u32[]{:S(2)}, u32[]{:S(2)}) collective-permute-start(bf16[256,512]{1,0:T(8,128)(2,1)S(1)} %fusion.7), channel_id=1, source_target_pairs={{0,1},{1,0},{2,3},{3,2},{4,5},{5,4},{6,7},{7,6},{8,9},{9,8},{10,11... | collective-permute-start | bytes 786440 | tf_op jit(solution)/shard_map/ppermute | solution.py:46
  5.4 9.8 %collective-permute-start.5 = (bf16[2,128,512]{2,1,0:T(8,128)(2,1)S(1)}, bf16[2,128,512]{2,1,0:T(8,128)(2,1)S(1)}, u32[]{:S(2)}, u32[]{:S(2)}) collective-permute-start(bf16[2,128,512]{2,1,0:T(8,128)(2,1)S(1)} %pad_maximum_fusion), channel_id=1, source_target_pairs={{0,2},{1,3},{2,0},{3,1},{4,6},{5,7},{6,4},{7,5},{8,10},{9,11},{10,... | collective-permute-start | bytes 786440 | tf_op jit(solution)/shard_map/ppermute | solution.py:46
  8.1 9.4 %collective-permute-start.2 = (bf16[128,512]{1,0:T(8,128)(2,1)S(1)}, bf16[128,512]{1,0:T(8,128)(2,1)S(1)}, u32[]{:S(2)}, u32[]{:S(2)}) collective-permute-start(bf16[128,512]{1,0:T(8,128)(2,1)S(1)} %dynamic-slice_bitcast_fusion.1), channel_id=1, source_target_pairs={{0,4},{1,5},{2,6},{3,7},{4,0},{5,1},{6,2},{7,3},{8,12},{9,13},{10,... | collective-permute-start | bytes 393224 | tf_op jit(solution)/shard_map/ppermute | solution.py:46
  9.7 12.9 %collective-permute-start.3 = (bf16[128,512]{1,0:T(8,128)(2,1)S(1)}, bf16[128,512]{1,0:T(8,128)(2,1)S(1)}, u32[]{:S(2)}, u32[]{:S(2)}) collective-permute-start(bf16[128,512]{1,0:T(8,128)(2,1)S(1)} %dynamic-slice_bitcast_fusion.1), channel_id=1, source_target_pairs={{0,8},{1,9},{2,10},{3,11},{4,12},{5,13},{6,14},{7,15},{8,0},{9,1},... | collective-permute-start | bytes 393224 | tf_op jit(solution)/shard_map/ppermute | solution.py:46
  12.3 10.4 %collective-permute-start.4 = (bf16[128,512]{1,0:T(8,128)(2,1)S(1)}, bf16[128,512]{1,0:T(8,128)(2,1)S(1)}, u32[]{:S(2)}, u32[]{:S(2)}) collective-permute-start(bf16[128,512]{1,0:T(8,128)(2,1)S(1)} %dynamic-slice_bitcast_fusion.1), channel_id=1, source_target_pairs={{0,12},{1,13},{2,14},{3,15},{4,8},{5,9},{6,10},{7,11},{8,4},{9,5},... | collective-permute-start | bytes 393224 | tf_op jit(solution)/shard_map/ppermute | solution.py:46
  12.5 10.8 %collective-permute-start.7 = (bf16[2,128,512]{2,1,0:T(8,128)(2,1)S(1)}, bf16[2,128,512]{2,1,0:T(8,128)(2,1)S(1)}, u32[]{:S(2)}, u32[]{:S(2)}) collective-permute-start(bf16[2,128,512]{2,1,0:T(8,128)(2,1)S(1)} %pad_maximum_fusion.1), channel_id=1, source_target_pairs={{0,2},{1,3},{2,0},{3,1},{4,6},{5,7},{6,4},{7,5},{8,10},{9,11},{10,... | collective-permute-start | bytes 786440 | tf_op jit(solution)/shard_map/ppermute | solution.py:46
  15.3 11.2 %collective-permute-start.8 = (bf16[2,128,512]{2,1,0:T(8,128)(2,1)S(1)}, bf16[2,128,512]{2,1,0:T(8,128)(2,1)S(1)}, u32[]{:S(2)}, u32[]{:S(2)}) collective-permute-start(bf16[2,128,512]{2,1,0:T(8,128)(2,1)S(1)} %fusion.11), channel_id=1, source_target_pairs={{0,4},{1,5},{2,6},{3,7},{4,0},{5,1},{6,2},{7,3},{8,12},{9,13},{10,... | collective-permute-start | bytes 786440 | tf_op jit(solution)/shard_map/ppermute | solution.py:46
  22.7 17.5 %collective-permute-start.6 = (bf16[4,128,512]{2,1,0:T(8,128)(2,1)S(1)}, bf16[4,128,512]{2,1,0:T(8,128)(2,1)S(1)}, u32[]{:S(2)}, u32[]{:S(2)}) collective-permute-start(bf16[4,128,512]{2,1,0:T(8,128)(2,1)S(1)} %bitcast_dynamic-update-slice_fusion.18), channel_id=1, source_target_pairs={{0,2},{1,3},{2,0},{3,1},{4,6},{5,7},{6,4},{7,5},{8,10},{9,11},{10,... | collective-permute-start | bytes 1572872 | tf_op jit(solution)/shard_map/ppermute | solution.py:46
  23.3 11.7 %collective-permute-start.10 = (bf16[4,128,512]{2,1,0:T(8,128)(2,1)S(1)}, bf16[4,128,512]{2,1,0:T(8,128)(2,1)S(1)}, u32[]{:S(2)}, u32[]{:S(2)}) collective-permute-start(bf16[4,128,512]{2,1,0:T(8,128)(2,1)S(1)} %bitcast_dynamic-update-slice_fusion.18), channel_id=1, source_target_pairs={{0,1},{1,0},{2,3},{3,2},{4,5},{5,4},{6,7},{7,6},{8,9},{9,8},{10,11... | collective-permute-start | bytes 1572872 | tf_op jit(solution)/shard_map/ppermute | solution.py:46
  26.6 8.4 %copy-start.1 = (f32[1,128]{1,0:T(1,128)S(1)}, f32[1,128]{1,0:T(1,128)}, u32[]{:S(2)}) copy-start(f32[1,128]{1,0:T(1,128)} %param.7) | copy-start | bytes 1540
  26.7 8.4 %collective-permute-start.9 = (bf16[128,512]{1,0:T(8,128)(2,1)S(1)}, bf16[128,512]{1,0:T(8,128)(2,1)S(1)}, u32[]{:S(2)}, u32[]{:S(2)}) collective-permute-start(bf16[128,512]{1,0:T(8,128)(2,1)S(1)} %fusion.26), channel_id=1, source_target_pairs={{0,8},{1,9},{2,10},{3,11},{4,12},{5,13},{6,14},{7,15},{8,0},{9,1},... | collective-permute-start | bytes 393224 | tf_op jit(solution)/shard_map/ppermute | solution.py:46
  35.3 6.5 %collective-permute-start.11 = (bf16[128,512]{1,0:T(8,128)(2,1)S(1)}, bf16[128,512]{1,0:T(8,128)(2,1)S(1)}, u32[]{:S(2)}, u32[]{:S(2)}) collective-permute-start(bf16[128,512]{1,0:T(8,128)(2,1)S(1)} %get-tuple-element.86), channel_id=1, source_target_pairs={{0,2},{1,3},{2,0},{3,1},{4,6},{5,7},{6,4},{7,5},{8,10},{9,11},{10,... | collective-permute-start | bytes 393224 | tf_op jit(solution)/shard_map/ppermute | solution.py:46
  36.6 9.0 %collective-permute-start.12 = (bf16[128,512]{1,0:T(8,128)(2,1)S(1)}, bf16[128,512]{1,0:T(8,128)(2,1)S(1)}, u32[]{:S(2)}, u32[]{:S(2)}) collective-permute-start(bf16[128,512]{1,0:T(8,128)(2,1)S(1)} %get-tuple-element.86), channel_id=1, source_target_pairs={{0,4},{1,5},{2,6},{3,7},{4,0},{5,1},{6,2},{7,3},{8,12},{9,13},{10,... | collective-permute-start | bytes 393224 | tf_op jit(solution)/shard_map/ppermute | solution.py:46
  36.6 9.0 %collective-permute-start.13 = (bf16[128,512]{1,0:T(8,128)(2,1)S(1)}, bf16[128,512]{1,0:T(8,128)(2,1)S(1)}, u32[]{:S(2)}, u32[]{:S(2)}) collective-permute-start(bf16[128,512]{1,0:T(8,128)(2,1)S(1)} %get-tuple-element.86), channel_id=1, source_target_pairs={{0,8},{1,9},{2,10},{3,11},{4,12},{5,13},{6,14},{7,15},{8,0},{9,1},... | collective-permute-start | bytes 393224 | tf_op jit(solution)/shard_map/ppermute | solution.py:46
  39.6 9.5 %collective-permute-start.19 = (bf16[128,512]{1,0:T(8,128)(2,1)S(1)}, bf16[128,512]{1,0:T(8,128)(2,1)S(1)}, u32[]{:S(2)}, u32[]{:S(2)}) collective-permute-start(bf16[128,512]{1,0:T(8,128)(2,1)S(1)} %get-tuple-element.86), channel_id=1, source_target_pairs={{0,6},{1,7},{2,4},{3,5},{4,2},{5,3},{6,0},{7,1},{8,14},{9,15},{10,... | collective-permute-start | bytes 393224 | tf_op jit(solution)/shard_map/ppermute | solution.py:46
  40.2 9.1 %collective-permute-start.17 = (bf16[128,512]{1,0:T(8,128)(2,1)S(1)}, bf16[128,512]{1,0:T(8,128)(2,1)S(1)}, u32[]{:S(2)}, u32[]{:S(2)}) collective-permute-start(bf16[128,512]{1,0:T(8,128)(2,1)S(1)} %get-tuple-element.86), channel_id=1, source_target_pairs={{0,16},{16,0},{1,17},{17,1},{2,18},{18,2},{3,19},{19,3},{4,20},{20... | collective-permute-start | bytes 393224 | tf_op jit(solution)/shard_map/ppermute | solution.py:119
  45.6 6.9 %collective-permute-start.14 = (bf16[128,512]{1,0:T(8,128)(2,1)S(1)}, bf16[128,512]{1,0:T(8,128)(2,1)S(1)}, u32[]{:S(2)}, u32[]{:S(2)}) collective-permute-start(bf16[128,512]{1,0:T(8,128)(2,1)S(1)} %collective-permute-done.13), channel_id=1, source_target_pairs={{0,6},{1,7},{2,4},{3,5},{4,2},{5,3},{6,0},{7,1},{8,14},{9,15},{10,... | collective-permute-start | bytes 393224 | tf_op jit(solution)/shard_map/ppermute | solution.py:46
  47.2 5.7 %collective-permute-start.15 = (bf16[128,512]{1,0:T(8,128)(2,1)S(1)}, bf16[128,512]{1,0:T(8,128)(2,1)S(1)}, u32[]{:S(2)}, u32[]{:S(2)}) collective-permute-start(bf16[128,512]{1,0:T(8,128)(2,1)S(1)} %collective-permute-done.13), channel_id=1, source_target_pairs={{0,4},{1,5},{2,6},{3,7},{4,0},{5,1},{6,2},{7,3},{8,12},{9,13},{10,... | collective-permute-start | bytes 393224 | tf_op jit(solution)/shard_map/ppermute | solution.py:46
  47.8 5.2 %collective-permute-start.16 = (bf16[128,512]{1,0:T(8,128)(2,1)S(1)}, bf16[128,512]{1,0:T(8,128)(2,1)S(1)}, u32[]{:S(2)}, u32[]{:S(2)}) collective-permute-start(bf16[128,512]{1,0:T(8,128)(2,1)S(1)} %collective-permute-done.13), channel_id=1, source_target_pairs={{0,2},{1,3},{2,0},{3,1},{4,6},{5,7},{6,4},{7,5},{8,10},{9,11},{10,... | collective-permute-start | bytes 393224 | tf_op jit(solution)/shard_map/ppermute | solution.py:46
  49.1 1.9 %collective-permute-start.18 = (bf16[4,128,512]{2,1,0:T(8,128)(2,1)S(1)}, bf16[4,128,512]{2,1,0:T(8,128)(2,1)S(1)}, u32[]{:S(2)}, u32[]{:S(2)}) collective-permute-start(bf16[4,128,512]{2,1,0:T(8,128)(2,1)S(1)} %collective-permute-done.6), channel_id=1, source_target_pairs={{0,1},{1,0},{2,3},{3,2},{4,5},{5,4},{6,7},{7,6},{8,9},{9,8},{10,11... | collective-permute-start | bytes 1572872 | tf_op jit(solution)/shard_map/ppermute | solution.py:46
  49.3 3.1 %collective-permute-start.20 = (bf16[4,128,512]{2,1,0:T(8,128)(2,1)S(1)}, bf16[4,128,512]{2,1,0:T(8,128)(2,1)S(1)}, u32[]{:S(2)}, u32[]{:S(2)}) collective-permute-start(bf16[4,128,512]{2,1,0:T(8,128)(2,1)S(1)} %bitcast_dynamic-update-slice_fusion.16), channel_id=1, source_target_pairs={{0,1},{1,0},{2,3},{3,2},{4,5},{5,4},{6,7},{7,6},{8,9},{9,8},{10,11... | collective-permute-start | bytes 1572872 | tf_op jit(solution)/shard_map/ppermute | solution.py:46
  49.9 1.2 %copy-start.3 = (bf16[1,256,2048]{2,1,0:T(8,128)(2,1)S(1)}, bf16[1,256,2048]{2,1,0:T(8,128)(2,1)}, u32[]{:S(2)}) copy-start(bf16[1,256,2048]{2,1,0:T(8,128)(2,1)} %param.6) | copy-start | bytes 3145732
  53.1 2.0 %collective-permute-start.21 = (bf16[4,128,512]{2,1,0:T(8,128)(2,1)S(1)}, bf16[4,128,512]{2,1,0:T(8,128)(2,1)S(1)}, u32[]{:S(2)}, u32[]{:S(2)}) collective-permute-start(bf16[4,128,512]{2,1,0:T(8,128)(2,1)S(1)} %bitcast_dynamic-update-slice_fusion.8), channel_id=1, source_target_pairs={{0,1},{1,0},{2,3},{3,2},{4,5},{5,4},{6,7},{7,6},{8,9},{9,8},{10,11... | collective-permute-start | bytes 1572872 | tf_op jit(solution)/shard_map/ppermute | solution.py:46
